TPU v7x, 32 devices: a whole 2x2x4 slice. The times are simulated.
32 devices in a mesh: grp: 2 (over x), col: 16 (over z, y, core).
Axes of the slice: x: 2, y: 2, z: 4, core: 2. Of those that a mesh axis runs over, the one named last changes fastest.
Arguments:
- state_emb: bfloat16 [8192, 512], P('col'), may hold values from -6 to 6
- from_weight: bfloat16 [512, 512], replicated, may hold values from -0.25 to 0.25
- to_weight: bfloat16 [512, 512], replicated, may hold values from -0.25 to 0.25
- emit_weight: bfloat16 [512, 512], replicated, may hold values from -0.25 to 0.25
- code_emb: bfloat16 [4096, 512], replicated, may hold values from -0.25 to 0.25
- init_vec: bfloat16 [512], replicated, may hold values from -0.25 to 0.25
- restart_logit: float32 [8192], P('col'), may hold values from -3 to 0
- block_mask: int32 [16, 8], replicated, may hold values from 0 to 1, as said below
- codes: int32 [64, 4], P('grp'), parts along dimension 0, may hold values from 0 to 4095
- lengths: int32 [64], P('grp'), parts along dimension 0, may hold values from 1 to 4, as said below
Outputs:
- scaled: float32 [64, 8192], P('grp', 'col'), parts along dimension 0
- log_like: float32 [64], P('grp'), parts along dimension 0
There are 2 independent parts, one for each index of `grp`. A program takes and returns all parts, laid end to end along the dimension named above; an argument that names none is the same for every part. Nothing has to cross between parts.
Inputs may be any that keep to these rules, and one draw needn't show every extreme that they name: `block_mask`: entries are 0 or 1, and entry [c, c % 8] is 1 for every block c. `lengths`: some sequence has length 4 and another has length 1.
All inputs are finite; a program needn't handle non-finite values.
Results may differ from a plain program's by a relative error of at most 0.0057.
Values may be sent and summed in bfloat16 or wider, within the bound.
No kernel may reach another device: no remote copies, remote signals or barrier semaphores. Data moves between devices by JAX's collectives and lax.ppermute only.
A program may use at most 128 MiB of HBM per device.

v0:
```python
import math

import jax
import jax.numpy as jnp
from jax import lax
from jax.sharding import PartitionSpec as P

SOFT_CAP = 10.0


def swapped(shard, axis, apart):
    return lax.ppermute(shard, axis, [(i, i ^ 1 << apart) for i in range(lax.axis_size(axis))])


def soft_cap(values):
    return SOFT_CAP * jnp.tanh(values / SOFT_CAP)


def collect(own_piece, dev_index, levels, transfer):
    stacked = own_piece[None]
    for bit_pos in range(levels):
        received = transfer(stacked, bit_pos)
        is_upper = dev_index // 2**bit_pos % 2 == 1
        stacked = jnp.where(
            is_upper,
            jnp.concatenate([received, stacked], axis=0),
            jnp.concatenate([stacked, received], axis=0),
        )
    return stacked


def per_device(
    state_emb,
    from_weight,
    to_weight,
    emit_weight,
    code_emb,
    init_vec,
    restart_logit,
    block_mask,
    codes,
    lengths,
):
    states_dev = state_emb.shape[0]
    embed_width = state_emb.shape[1]
    cluster_size = block_mask.shape[1]
    levels = cluster_size.bit_length() - 1
    batch_rows = codes.shape[0]
    step_count = codes.shape[1]
    dev_index = lax.axis_index("col")
    cluster_pos = dev_index % cluster_size
    logit_scale = 2.0 / math.sqrt(embed_width)
    from_part = jnp.dot(state_emb, from_weight, preferred_element_type=jnp.float32).astype(
        jnp.bfloat16
    )
    to_part = jnp.dot(state_emb, to_weight, preferred_element_type=jnp.float32).astype(jnp.bfloat16)
    query_part = jnp.dot(state_emb, emit_weight, preferred_element_type=jnp.float32).astype(
        jnp.bfloat16
    )
    prior_raw = jnp.exp(
        soft_cap(2.0 * jnp.dot(state_emb, init_vec, preferred_element_type=jnp.float32))
    )
    restart_prob = jax.nn.sigmoid(restart_logit)
    prior_total = lax.psum(jnp.sum(prior_raw), "col")
    emit_full = jnp.exp(
        soft_cap(
            3.0 * jnp.einsum("se,ve->sv", query_part, code_emb, preferred_element_type=jnp.float32)
        )
    )
    emit_total = jnp.sum(emit_full, axis=1)
    picked = jnp.take(emit_full, codes.reshape(-1), axis=1) / emit_total[:, None]
    emission = picked.reshape(states_dev, batch_rows, step_count).transpose(2, 1, 0)
    rows_from = collect(
        from_part, dev_index, levels, lambda payload, bit_pos: swapped(payload, "col", bit_pos)
    )
    rows_from = rows_from.reshape(cluster_size * states_dev, embed_width)
    logits = (
        jnp.einsum("ie,je->ij", rows_from, to_part, preferred_element_type=jnp.float32)
        * logit_scale
    )
    allow_row = lax.dynamic_slice_in_dim(block_mask, dev_index, 1, 0)[0]
    allowed = jnp.repeat(allow_row, states_dev) == 1
    weights_exp = jnp.where(allowed[:, None], jnp.exp(soft_cap(logits)), jnp.zeros_like(logits))
    sums_left = jnp.sum(weights_exp, axis=1).reshape(cluster_size, states_dev)
    for bit_pos in reversed(range(levels)):
        half_count = sums_left.shape[0] // 2
        halves = sums_left.reshape(2, half_count, states_dev)
        is_upper = cluster_pos // 2**bit_pos % 2 == 1
        keep_half = jnp.where(is_upper, halves[1], halves[0])
        send_half = jnp.where(is_upper, halves[0], halves[1])
        sums_left = keep_half + swapped(send_half, "col", bit_pos)
    own_sums = sums_left.reshape(states_dev)
    row_sum = collect(
        own_sums, dev_index, levels, lambda payload, bit_pos: swapped(payload, "col", bit_pos)
    )
    row_sum = row_sum.reshape(cluster_size * states_dev)
    trans = (weights_exp / row_sum[:, None]).astype(jnp.bfloat16)
    prior = prior_raw / prior_total

    def both_of(forward):
        return lax.psum(
            (jnp.sum(forward, axis=1), jnp.sum(forward * restart_prob[None, :], axis=1)), "col"
        )

    forward = prior[None, :] * emission[0]
    totals, carried = both_of(forward)
    restart = carried / totals
    scaled = forward / totals[:, None]
    log_like = jnp.log(totals)
    for step_num in range(1, step_count):
        weighted = (scaled * (1.0 - restart_prob)[None, :]).astype(jnp.bfloat16)
        gathered = collect(
            weighted, dev_index, levels, lambda payload, bit_pos: swapped(payload, "col", bit_pos)
        )
        gathered = gathered.transpose(1, 0, 2).reshape(batch_rows, cluster_size * states_dev)
        predicted = (
            jnp.dot(gathered, trans, preferred_element_type=jnp.float32)
            + prior[None, :] * restart[:, None]
        )
        forward = predicted * emission[step_num]
        is_live = step_num < lengths
        totals, carried = both_of(forward)
        restart = jnp.where(is_live, carried / totals, restart)
        scaled = jnp.where(is_live[:, None], forward / totals[:, None], scaled)
        log_like = log_like + jnp.where(is_live, jnp.log(totals), jnp.zeros_like(totals))
    return (scaled, log_like)


def solution(mesh):
    in_specs = (P("col", None), P(), P(), P(), P(), P(), P("col"), P(), P("grp", None), P("grp"))
    out_specs = (P("grp", "col"), P("grp"))
    return jax.shard_map(
        per_device, mesh=mesh, in_specs=in_specs, out_specs=out_specs, check_vma=False
    )
```

profile of v0, /device:TPU:0, one launch (start us, length us, event | category | flops | bytes accessed | tf_op | source)
XLA Modules:
  0.0 288.2 jit_solution(10402148499705621093)
XLA Ops:
  5.4 3.0 %collective-permute-start.4 = (bf16[2,512,512]{2,1,0:T(8,128)(2,1)S(1)}, bf16[2,512,512]{2,1,0:T(8,128)(2,1)}, u32[]{:S(2)}, u32[]{:S(2)}) collective-permute-start(bf16[2,512,512]{2,1,0:T(8,128)(2,1)S(1)} %maximum_select_fusion.2), channel_id=1, source_target_pairs={{0,2},{1,3},{2,0},{3,1},{4,6},{5,7},{6,4},{7,5},{8,10},{9,11},{10,... | collective-permute-start | bytes 3145736 | tf_op jit(solution)/shard_map/ppermute | solution.py:12
  9.9 45.1 %psum.56 = f32[]{:T(128)} all-reduce(f32[]{:T(128)} %fusion.16), channel_id=1, replica_groups=mesh['grp'=2,'col'=16] {'col'}, use_global_device_ids=true, to_apply=%region_1.2 | all-reduce | flops 1 | bytes 8 | tf_op jit(solution)/shard_map/psum | solution.py:64
  55.0 2.6 maximum_select_fusion.1
  57.7 7.6 %fusion.18 = (f32[512]{0:T(512)S(1)}, f32[512,4096]{1,0:T(8,128)}) fusion(bf16[4096,512]{1,0:T(8,128)(2,1)} %param.14, bf16[512,512]{1,0:T(8,128)(2,1)S(1)} %copy-done, bf16[512,512]{1,0:T(8,128)(2,1)S(1)} %copy-done.7), kind=kOutput, calls=%fused_computation.78 | convolution fusion | flops 2422472192 | bytes 13633536 | tf_op jit(solution)/shard_map/se,ve->sv/dot_general | solution.py:67
  65.4 9.0 %copy.15 = f32[512,4096]{0,1:T(8,128)} copy(f32[512,4096]{1,0:T(8,128)} %get-tuple-element.24) | data formatting | bytes 16777216 | tf_op jit(solution)/shard_map/exp | solution.py:65
  74.6 4.3 %gather_fusion = f32[128,512]{1,0:T(8,128)S(1)} fusion(f32[512,4096]{0,1:T(8,128)} %copy.15, s32[1024]{0:T(1024)S(1)} %pad_clamp_fusion), kind=kCustom, calls=%fused_computation | custom fusion | bytes 524800 | tf_op jit(solution)/shard_map/jit(_take)/gather | solution.py:71
  80.1 24.1 %collective-permute-done.5 = bf16[4,512,512]{2,1,0:T(8,128)(2,1)} collective-permute-done((bf16[4,512,512]{2,1,0:T(8,128)(2,1)S(1)}, bf16[4,512,512]{2,1,0:T(8,128)(2,1)}, u32[]{:S(2)}, u32[]{:S(2)}) %collective-permute-start.5) | collective-permute-done | bytes 2097184 | tf_op jit(solution)/shard_map/ppermute | solution.py:12
  104.1 3.9 %maximum_select_fusion = bf16[8,512,512]{2,1,0:T(8,128)(2,1)} fusion(bf16[4,512,512]{2,1,0:T(8,128)(2,1)S(1)} %maximum_select_fusion.1, bf16[4,512,512]{2,1,0:T(8,128)(2,1)} %collective-permute-done.5, pred[]{:T(512)S(6)} %eq.67), kind=kLoop, calls=%fused_computation.4 | loop fusion | flops 6291456 | bytes 8388609 | tf_op jit(solution)/shard_map/jit(_where)/select_n | solution.py:24
  108.1 7.7 %fusion.19 = (f32[4096]{0:T(1024)S(1)}, f32[4096,512]{0,1:T(8,128)}) fusion(bf16[4096,512]{1,0:T(8,128)(2,1)} %bitcast.70, bf16[512,512]{1,0:T(8,128)(2,1)S(1)} %copy-done, bf16[512,512]{1,0:T(8,128)(2,1)} %param.12, pred[4096]{0:T(1024)(128)(4,1)S(1)} %bitcast.78), kind=kOutput, calls=%fused_computation.79 | convolution fusion | flops 2424565760 | bytes 13651968 | tf_op jit(solution)/shard_map/ie,je->ij/dot_general | solution.py:78
  116.3 29.5 %all-reduce.2 = (f32[32]{0:T(128)S(1)}, f32[32]{0:T(128)S(1)}) all-reduce(f32[32]{0:T(128)S(1)} %get-tuple-element.3, f32[32]{0:T(128)S(1)} %get-tuple-element.2), channel_id=1, replica_groups=mesh['grp'=2,'col'=16] {'col'}, use_global_device_ids=true, to_apply=%region_4.5 | all-reduce | flops 64 | bytes 512 | tf_op jit(solution)/shard_map/psum | solution.py:101
  146.1 3.4 %collective-permute-done.7 = f32[2,512]{1,0:T(2,128)S(1)} collective-permute-done((f32[2,512]{1,0:T(2,128)S(1)}, f32[2,512]{1,0:T(2,128)S(1)}, u32[]{:S(2)}, u32[]{:S(2)}) %collective-permute-start.7) | collective-permute-done | bytes 4128 | tf_op jit(solution)/shard_map/ppermute | solution.py:12
  150.9 3.3 %collective-permute-done.1 = bf16[2,32,512]{2,1,0:T(8,128)(2,1)S(1)} collective-permute-done((bf16[2,32,512]{2,1,0:T(8,128)(2,1)S(1)}, bf16[2,32,512]{2,1,0:T(8,128)(2,1)S(1)}, u32[]{:S(2)}, u32[]{:S(2)}) %collective-permute-start.1) | collective-permute-done | bytes 65568 | tf_op jit(solution)/shard_map/ppermute | solution.py:12
  154.7 3.3 %collective-permute-done.10 = f32[2,512]{1,0:T(2,128)S(1)} collective-permute-done((f32[2,512]{1,0:T(2,128)S(1)}, f32[2,512]{1,0:T(2,128)S(1)}, u32[]{:S(2)}, u32[]{:S(2)}) %collective-permute-start.10) | collective-permute-done | bytes 4128 | tf_op jit(solution)/shard_map/ppermute | solution.py:12
  158.0 2.1 collective-permute-start.11
  161.7 4.4 %divide_convert_fusion = bf16[4096,512]{0,1:T(8,128)(2,1)S(1)} fusion(f32[4096,512]{0,1:T(8,128)} %get-tuple-element.26, f32[4096]{0:T(1024)S(1)} %bitcast.75), kind=kLoop, calls=%fused_computation.1 | loop fusion | flops 4194304 | bytes 12599296 | tf_op jit(solution)/shard_map/convert_element_type | solution.py:97
  169.5 29.5 %all-reduce.1 = (f32[32]{0:T(128)S(1)}, f32[32]{0:T(128)S(1)}) all-reduce(f32[32]{0:T(128)S(1)} %get-tuple-element.7, f32[32]{0:T(128)S(1)} %get-tuple-element.6), channel_id=1, replica_groups=mesh['grp'=2,'col'=16] {'col'}, use_global_device_ids=true, to_apply=%region_9.10 | all-reduce | flops 64 | bytes 512 | tf_op jit(solution)/shard_map/psum | solution.py:101
  200.5 4.3 %collective-permute-done.13 = bf16[2,32,512]{2,1,0:T(8,128)(2,1)S(1)} collective-permute-done((bf16[2,32,512]{2,1,0:T(8,128)(2,1)S(1)}, bf16[2,32,512]{2,1,0:T(8,128)(2,1)S(1)}, u32[]{:S(2)}, u32[]{:S(2)}) %collective-permute-start.13) | collective-permute-done | bytes 65568 | tf_op jit(solution)/shard_map/ppermute | solution.py:12
  204.8 4.9 %collective-permute-done.14 = bf16[4,32,512]{2,1,0:T(8,128)(2,1)S(1)} collective-permute-done((bf16[4,32,512]{2,1,0:T(8,128)(2,1)S(1)}, bf16[4,32,512]{2,1,0:T(8,128)(2,1)S(1)}, u32[]{:S(2)}, u32[]{:S(2)}) %collective-permute-start.14) | collective-permute-done | bytes 131104 | tf_op jit(solution)/shard_map/ppermute | solution.py:12
  209.8 3.7 %multiply_reduce_fusion = (f32[32]{0:T(128)S(1)}, f32[32]{0:T(128)S(1)}, f32[32,512]{1,0:T(8,128)S(1)}) fusion(f32[512]{0:T(512)S(1)} %get-tuple-element.17, f32[4,32,512]{2,1,0:T(8,128)S(1)} %fusion.8, f32[32]{0:T(128)S(1)} %divide_select_fusion.4, f32[512]{0:T(512)S(1)} %fusion.15, bf16[32,4096]{1,0:T(8,128)(2,1)S(1)} %bitcast.73, ...), kind=kOutput, calls=%fused_computation.37 | convolution fusion | flops 134315968 | bytes 4592000 | tf_op jit(solution)/shard_map/dot_general | solution.py:117
  213.5 29.5 %all-reduce = (f32[32]{0:T(128)S(1)}, f32[32]{0:T(128)S(1)}) all-reduce(f32[32]{0:T(128)S(1)} %get-tuple-element.5, f32[32]{0:T(128)S(1)} %get-tuple-element.4), channel_id=1, replica_groups=mesh['grp'=2,'col'=16] {'col'}, use_global_device_ids=true, to_apply=%region_13.14 | all-reduce | flops 64 | bytes 512 | tf_op jit(solution)/shard_map/psum | solution.py:101
  244.4 4.3 %collective-permute-done.16 = bf16[2,32,512]{2,1,0:T(8,128)(2,1)S(1)} collective-permute-done((bf16[2,32,512]{2,1,0:T(8,128)(2,1)S(1)}, bf16[2,32,512]{2,1,0:T(8,128)(2,1)S(1)}, u32[]{:S(2)}, u32[]{:S(2)}) %collective-permute-start.16) | collective-permute-done | bytes 65568 | tf_op jit(solution)/shard_map/ppermute | solution.py:12
  248.8 4.9 %collective-permute-done.17 = bf16[4,32,512]{2,1,0:T(8,128)(2,1)S(1)} collective-permute-done((bf16[4,32,512]{2,1,0:T(8,128)(2,1)S(1)}, bf16[4,32,512]{2,1,0:T(8,128)(2,1)S(1)}, u32[]{:S(2)}, u32[]{:S(2)}) %collective-permute-start.17) | collective-permute-done | bytes 131104 | tf_op jit(solution)/shard_map/ppermute | solution.py:12
  253.8 3.7 %fusion.20 = (f32[32]{0:T(128)S(1)}, f32[32,512]{1,0:T(8,128)S(1)}) fusion(f32[4,32,512]{2,1,0:T(8,128)S(1)} %fusion.8, f32[32]{0:T(128)S(1)} %divide_select_fusion.3, f32[512]{0:T(512)S(1)} %fusion.15, bf16[32,4096]{1,0:T(8,128)(2,1)S(1)} %bitcast.72, bf16[4096,512]{0,1:T(8,128)(2,1)} %copy-done.1), kind=kOutput, calls=%fused_computation.80 | convolution fusion | flops 134283232 | bytes 4589824 | tf_op jit(solution)/shard_map/dot_general | solution.py:117
  257.5 29.5 %psum.63 = f32[32]{0:T(128)S(1)} all-reduce(f32[32]{0:T(128)S(1)} %get-tuple-element.29), channel_id=1, replica_groups=mesh['grp'=2,'col'=16] {'col'}, use_global_device_ids=true, to_apply=%region_17.18 | all-reduce | flops 32 | bytes 256 | tf_op jit(solution)/shard_map/psum | solution.py:101
  (94 shorter events, 19.7 us)
Async XLA Ops:
  0.6 57.0 %copy-start.7 = (bf16[512,512]{1,0:T(8,128)(2,1)S(1)}, bf16[512,512]{1,0:T(8,128)(2,1)}, u32[]{:S(2)}) copy-start(bf16[512,512]{1,0:T(8,128)(2,1)} %param.13) | copy-start | bytes 1572868
  3.2 2.1 collective-permute-start.3
  5.4 49.6 %copy-start.2 = (bf16[2,512,512]{2,1,0:T(8,128)(2,1)}, bf16[2,512,512]{2,1,0:T(8,128)(2,1)S(1)}, u32[]{:S(2)}) copy-start(bf16[2,512,512]{2,1,0:T(8,128)(2,1)S(1)} %maximum_select_fusion.2) | copy-start | bytes 3145732
  5.4 49.6 %collective-permute-start.4 = (bf16[2,512,512]{2,1,0:T(8,128)(2,1)S(1)}, bf16[2,512,512]{2,1,0:T(8,128)(2,1)}, u32[]{:S(2)}, u32[]{:S(2)}) collective-permute-start(bf16[2,512,512]{2,1,0:T(8,128)(2,1)S(1)} %maximum_select_fusion.2), channel_id=1, source_target_pairs={{0,2},{1,3},{2,0},{3,1},{4,6},{5,7},{6,4},{7,5},{8,10},{9,11},{10,... | collective-permute-start | bytes 3145736 | tf_op jit(solution)/shard_map/ppermute | solution.py:12
  57.6 46.5 %collective-permute-start.5 = (bf16[4,512,512]{2,1,0:T(8,128)(2,1)S(1)}, bf16[4,512,512]{2,1,0:T(8,128)(2,1)}, u32[]{:S(2)}, u32[]{:S(2)}) collective-permute-start(bf16[4,512,512]{2,1,0:T(8,128)(2,1)S(1)} %maximum_select_fusion.1), channel_id=1, source_target_pairs={{0,4},{1,5},{2,6},{3,7},{4,0},{5,1},{6,2},{7,3},{8,12},{9,13},{10,... | collective-permute-start | bytes 6291464 | tf_op jit(solution)/shard_map/ppermute | solution.py:12
  65.3 9.0 %copy-start.3 = (s32[32,4]{0,1:T(4,128)S(1)}, s32[32,4]{0,1:T(4,128)}, u32[]{:S(2)}) copy-start(s32[32,4]{0,1:T(4,128)} %param.18) | copy-start | bytes 1540
  65.4 13.6 %copy-start.5 = (s32[16,8]{0,1:T(8,128)S(1)}, s32[16,8]{0,1:T(8,128)}, u32[]{:S(2)}) copy-start(s32[16,8]{0,1:T(8,128)} %param.17) | copy-start | bytes 1540
  65.4 14.6 %copy-start.6 = (f32[512]{0:T(512)S(1)}, f32[512]{0:T(512)}, u32[]{:S(2)}) copy-start(f32[512]{0:T(512)} %param.16) | copy-start | bytes 6148
  108.1 46.6 %copy-start.4 = (s32[32]{0:T(128)S(1)}, s32[32]{0:T(128)}, u32[]{:S(2)}) copy-start(s32[32]{0:T(128)} %param.19) | copy-start | bytes 388
  115.8 30.0 %collective-permute-start.6 = (f32[4,512]{1,0:T(4,128)S(1)}, f32[4,512]{1,0:T(4,128)S(1)}, u32[]{:S(2)}, u32[]{:S(2)}) collective-permute-start(f32[4,512]{1,0:T(4,128)S(1)} %select_n.320), channel_id=1, source_target_pairs={{0,4},{1,5},{2,6},{3,7},{4,0},{5,1},{6,2},{7,3},{8,12},{9,13},{10,... | collective-permute-start | bytes 24584 | tf_op jit(solution)/shard_map/ppermute | solution.py:12
  145.8 3.7 %collective-permute-start.7 = (f32[2,512]{1,0:T(2,128)S(1)}, f32[2,512]{1,0:T(2,128)S(1)}, u32[]{:S(2)}, u32[]{:S(2)}) collective-permute-start(f32[2,512]{1,0:T(2,128)S(1)} %broadcast_select_fusion), channel_id=1, source_target_pairs={{0,2},{1,3},{2,0},{3,1},{4,6},{5,7},{6,4},{7,5},{8,10},{9,11},{10,... | collective-permute-start | bytes 12296 | tf_op jit(solution)/shard_map/ppermute | solution.py:12
  146.0 3.6 %collective-permute-start = (bf16[1,32,512]{2,1,0:T(8,128)(2,1)S(1)}, bf16[1,32,512]{2,1,0:T(8,128)(2,1)S(1)}, u32[]{:S(2)}, u32[]{:S(2)}) collective-permute-start(bf16[1,32,512]{2,1,0:T(8,128)(2,1)S(1)} %multiply_convert_fusion.2), channel_id=1, source_target_pairs={{0,1},{1,0},{2,3},{3,2},{4,5},{5,4},{6,7},{7,6},{8,9},{9,8},{10,11... | collective-permute-start | bytes 98312 | tf_op jit(solution)/shard_map/ppermute | solution.py:12
  149.5 1.2 collective-permute-start.8
  149.6 4.5 %collective-permute-start.1 = (bf16[2,32,512]{2,1,0:T(8,128)(2,1)S(1)}, bf16[2,32,512]{2,1,0:T(8,128)(2,1)S(1)}, u32[]{:S(2)}, u32[]{:S(2)}) collective-permute-start(bf16[2,32,512]{2,1,0:T(8,128)(2,1)S(1)} %maximum_select_fusion.9), channel_id=1, source_target_pairs={{0,2},{1,3},{2,0},{3,1},{4,6},{5,7},{6,4},{7,5},{8,10},{9,11},{10,... | collective-permute-start | bytes 196616 | tf_op jit(solution)/shard_map/ppermute | solution.py:12
  150.8 3.5 %collective-permute-start.9 = (f32[1,512]{1,0:T(1,128)S(1)}, f32[1,512]{1,0:T(1,128)S(1)}, u32[]{:S(2)}, u32[]{:S(2)}) collective-permute-start(f32[1,512]{1,0:T(1,128)S(1)} %fusion.14), channel_id=1, source_target_pairs={{0,1},{1,0},{2,3},{3,2},{4,5},{5,4},{6,7},{7,6},{8,9},{9,8},{10,11... | collective-permute-start | bytes 6152 | tf_op jit(solution)/shard_map/ppermute | solution.py:12
  154.2 5.9 %collective-permute-start.2 = (bf16[4,32,512]{2,1,0:T(8,128)(2,1)S(1)}, bf16[4,32,512]{2,1,0:T(8,128)(2,1)S(1)}, u32[]{:S(2)}, u32[]{:S(2)}) collective-permute-start(bf16[4,32,512]{2,1,0:T(8,128)(2,1)S(1)} %maximum_select_fusion.6), channel_id=1, source_target_pairs={{0,4},{1,5},{2,6},{3,7},{4,0},{5,1},{6,2},{7,3},{8,12},{9,13},{10,... | collective-permute-start | bytes 393224 | tf_op jit(solution)/shard_map/ppermute | solution.py:12
  154.3 3.7 %collective-permute-start.10 = (f32[2,512]{1,0:T(2,128)S(1)}, f32[2,512]{1,0:T(2,128)S(1)}, u32[]{:S(2)}, u32[]{:S(2)}) collective-permute-start(f32[2,512]{1,0:T(2,128)S(1)} %maximum_select_fusion.14), channel_id=1, source_target_pairs={{0,2},{1,3},{2,0},{3,1},{4,6},{5,7},{6,4},{7,5},{8,10},{9,11},{10,... | collective-permute-start | bytes 12296 | tf_op jit(solution)/shard_map/ppermute | solution.py:12
  158.0 3.7 %collective-permute-start.11 = (f32[4,512]{1,0:T(4,128)S(1)}, f32[4,512]{1,0:T(4,128)S(1)}, u32[]{:S(2)}, u32[]{:S(2)}) collective-permute-start(f32[4,512]{1,0:T(4,128)S(1)} %maximum_select_fusion.13), channel_id=1, source_target_pairs={{0,4},{1,5},{2,6},{3,7},{4,0},{5,1},{6,2},{7,3},{8,12},{9,13},{10,... | collective-permute-start | bytes 24584 | tf_op jit(solution)/shard_map/ppermute | solution.py:12
  199.1 1.3 collective-permute-start.12
  200.4 4.3 %collective-permute-start.13 = (bf16[2,32,512]{2,1,0:T(8,128)(2,1)S(1)}, bf16[2,32,512]{2,1,0:T(8,128)(2,1)S(1)}, u32[]{:S(2)}, u32[]{:S(2)}) collective-permute-start(bf16[2,32,512]{2,1,0:T(8,128)(2,1)S(1)} %maximum_select_fusion.10), channel_id=1, source_target_pairs={{0,2},{1,3},{2,0},{3,1},{4,6},{5,7},{6,4},{7,5},{8,10},{9,11},{10,... | collective-permute-start | bytes 196616 | tf_op jit(solution)/shard_map/ppermute | solution.py:12
  204.7 5.0 %collective-permute-start.14 = (bf16[4,32,512]{2,1,0:T(8,128)(2,1)S(1)}, bf16[4,32,512]{2,1,0:T(8,128)(2,1)S(1)}, u32[]{:S(2)}, u32[]{:S(2)}) collective-permute-start(bf16[4,32,512]{2,1,0:T(8,128)(2,1)S(1)} %maximum_select_fusion.7), channel_id=1, source_target_pairs={{0,4},{1,5},{2,6},{3,7},{4,0},{5,1},{6,2},{7,3},{8,12},{9,13},{10,... | collective-permute-start | bytes 393224 | tf_op jit(solution)/shard_map/ppermute | solution.py:12
  243.1 1.3 collective-permute-start.15
  244.4 4.3 %collective-permute-start.16 = (bf16[2,32,512]{2,1,0:T(8,128)(2,1)S(1)}, bf16[2,32,512]{2,1,0:T(8,128)(2,1)S(1)}, u32[]{:S(2)}, u32[]{:S(2)}) collective-permute-start(bf16[2,32,512]{2,1,0:T(8,128)(2,1)S(1)} %maximum_select_fusion.11), channel_id=1, source_target_pairs={{0,2},{1,3},{2,0},{3,1},{4,6},{5,7},{6,4},{7,5},{8,10},{9,11},{10,... | collective-permute-start | bytes 196616 | tf_op jit(solution)/shard_map/ppermute | solution.py:12
  248.7 5.0 %collective-permute-start.17 = (bf16[4,32,512]{2,1,0:T(8,128)(2,1)S(1)}, bf16[4,32,512]{2,1,0:T(8,128)(2,1)S(1)}, u32[]{:S(2)}, u32[]{:S(2)}) collective-permute-start(bf16[4,32,512]{2,1,0:T(8,128)(2,1)S(1)} %maximum_select_fusion.8), channel_id=1, source_target_pairs={{0,4},{1,5},{2,6},{3,7},{4,0},{5,1},{6,2},{7,3},{8,12},{9,13},{10,... | collective-permute-start | bytes 393224 | tf_op jit(solution)/shard_map/ppermute | solution.py:12
  (2 other events, 3.0 us)
where the time goes:
time: 289 us; the launch traced here: 288 us
  blocking collectives  163 us (56%)
  waiting for transfers between devices  59 us (20%)
  matrix products  25.8 us (9%)
  local copies, waits for them, and re-layouts  17.4 us (6%)
  other arithmetic  14.6 us (5%)
  starting transfers between devices  7.26 us (3%)
    psum x4, blocking collectives, both_of(): lax.psum((jnp.sum(forward, axis=1), jnp.sum(forward * restart_prob[None,...  118 us
    ppermute x18, waiting for transfers between devices, swapped(): lax.ppermute(shard, axis, [(i, i ^ 1 << apart) for i in range(lax.axis_si...  59 us
    psum x1, blocking collectives, per_device(): prior_total = lax.psum(jnp.sum(prior_raw), 'col')  45.1 us
    exp x1, local copies, waits for them, and re-layouts, per_device(): jnp.exp(soft_cap(3.0 * jnp.einsum('se,ve->sv', query_part, code_emb, pref...  9.02 us
    dot_general x3, matrix products, per_device(): jnp.dot(gathered, trans, preferred_element_type=jnp.float32)  8.79 us
    dot_general x1, matrix products, per_device(): jnp.einsum('ie,je->ij', rows_from, to_part, preferred_element_type=jnp.fl...  7.7 us
    dot_general x1, matrix products, per_device(): jnp.einsum('se,ve->sv', query_part, code_emb, preferred_element_type=jnp....  7.65 us
    ppermute x18, starting transfers between devices, swapped(): lax.ppermute(shard, axis, [(i, i ^ 1 << apart) for i in range(lax.axis_si...  7.26 us
  transfers between devices with their start and end apart: 18, of which 13 were waited for; matrix products, arithmetic and copies ran while one was open for 8% of the time, Pallas kernels for 0%

commit v1 on v0

v1 whole, which is shorter than its diff:
```python
import math

import jax
import jax.numpy as jnp
from jax import lax
from jax.experimental import pallas as pl
from jax.experimental.pallas import tpu as pltpu
from jax.sharding import PartitionSpec as P

SOFT_CAP = 10.0
EMIT_SCALE = 2.0**20
F32 = jnp.float32
BF16 = jnp.bfloat16
NT = (((1,), (1,)), ((), ()))
NN = (((1,), (0,)), ((), ()))


def soft_cap(values):
    return SOFT_CAP * jnp.tanh(values * (1.0 / SOFT_CAP))


def dot(lhs, rhs, dims):
    return lax.dot_general(lhs, rhs, dims, preferred_element_type=F32)


def across(shard, apart, axis="col"):
    return lax.ppermute(shard, axis, [(i, i ^ apart) for i in range(lax.axis_size(axis))])


def vmem_call(body, out_shape, name, flops=0, nbytes=0, n_in=None, smem=()):
    def run(*args):
        in_specs = [
            pl.BlockSpec(memory_space=pltpu.SMEM if k in smem else pltpu.VMEM)
            for k in range(len(args))
        ]
        outs = jax.tree.map(lambda s: pl.BlockSpec(memory_space=pltpu.VMEM), out_shape)
        return pl.pallas_call(
            body,
            out_shape=out_shape,
            in_specs=in_specs,
            out_specs=outs,
            name=name,
            cost_estimate=pl.CostEstimate(flops=flops, bytes_accessed=nbytes, transcendentals=0),
            compiler_params=pltpu.CompilerParams(vmem_limit_bytes=40 << 20),
        )(*args)

    return run


def shape(dims, dtype):
    return jax.ShapeDtypeStruct(dims, dtype)


def project_kernel(emb, weight, out):
    out[...] = dot(emb[...], weight[...], NN).astype(BF16)


def sources_kernel(emb, from_w, emit_w, init_vec, from_out, query_out, prior_out):
    from_out[...] = dot(emb[...], from_w[...], NN).astype(BF16)
    query_out[...] = dot(emb[...], emit_w[...], NN).astype(BF16)
    prior = dot(jnp.broadcast_to(init_vec[...], (8, emb.shape[1])), emb[...], NT)
    prior_out[...] = jnp.exp(soft_cap(2.0 * prior))[:1]


def emission_kernel(half_tiles, place, code, query, codes, pick_out, total_out, rows_acc, total_acc):
    tile = pl.program_id(0)
    tile_rows = code.shape[0]

    @pl.when(tile == 0)
    def _():
        rows_acc[...] = jnp.zeros_like(rows_acc)
        total_acc[...] = jnp.zeros_like(total_acc)

    ids = codes[...]
    lanes = lax.broadcasted_iota(jnp.int32, (ids.shape[0], tile_rows), 1) + tile * tile_rows
    one_hot = jnp.where(lanes == ids, 1.0, 0.0).astype(BF16)
    rows_acc[...] += dot(one_hot, code[...], NN)

    @pl.when(tile // half_tiles == place[0])
    def _():
        def chunk(k, carry):
            rows = code[pl.ds(pl.multiple_of(k * 128, 128), 128), :]
            logits = dot(rows, query[...], NT)
            weights = jnp.exp(soft_cap(3.0 * logits))
            return carry + jnp.sum(weights.reshape(16, 8, -1), axis=0)

        total_acc[...] += lax.fori_loop(
            0, tile_rows // 128, chunk, jnp.zeros(total_acc.shape, F32), unroll=True
        )

    @pl.when(tile == pl.num_programs(0) - 1)
    def _():
        pick_out[...] = jnp.exp(soft_cap(3.0 * dot(rows_acc[...].astype(BF16), query[...], NT)))
        total_out[...] = jnp.sum(total_acc[...], axis=0, keepdims=True)


def lane_pack(columns, rows):
    lane = lax.broadcasted_iota(jnp.int32, (rows, 128), 1)
    packed = jnp.zeros((rows, 128), F32)
    for k, column in enumerate(columns):
        packed = jnp.where(lane == k, column, packed)
    return packed


def lane_pick(packed, k):
    lane = lax.broadcasted_iota(jnp.int32, packed.shape, 1)
    return jnp.sum(jnp.where(lane == k, packed, 0.0), axis=1, keepdims=True)


def hidden_kernel(pick, total_a, total_b, prior, logit, emit_out, msg_out):
    batch = pick.shape[0] // 4
    factor = EMIT_SCALE / (total_a[...] + total_b[...])
    emit = pick[...] * factor
    emit_out[...] = emit
    p = prior[...]
    restart = jax.nn.sigmoid(logit[...])
    first = p * emit[:batch]
    third = p * emit[2 * batch : 3 * batch]
    states = p.shape[1]
    msg_out[:batch, :states] = first * (1.0 - restart)
    msg_out[batch:, :states] = third * (1.0 - restart)
    mass = jnp.sum(first * restart, axis=1, keepdims=True)
    norm = jnp.broadcast_to(jnp.sum(p, axis=1, keepdims=True), mass.shape)
    msg_out[:batch, states:] = lane_pack([mass, norm], batch)
    msg_out[batch:, states:] = jnp.zeros((batch, 128), F32)


def weights_kernel(scale, to_blk, from_a, from_b, allow, wt_out, sum_out):
    states = from_a.shape[0]
    for side, source in ((0, from_a), (1, from_b)):
        keep = allow[side]

        def chunk(k, carry):
            rows = pl.ds(pl.multiple_of(k * 128, 128), 128)
            logits = dot(to_blk[rows, :], source[...], NT) * scale
            weights = jnp.exp(soft_cap(logits)) * keep
            wt_out[rows, side * states : (side + 1) * states] = weights.astype(BF16)
            return carry + jnp.sum(weights.reshape(16, 8, -1), axis=0)

        sums = lax.fori_loop(
            0, to_blk.shape[0] // 128, chunk, jnp.zeros((8, states), F32), unroll=True
        )
        sum_out[:, side * states : (side + 1) * states] = jnp.sum(sums, axis=0, keepdims=True)


def first_kernel(msg_a, msg_b, sums_own, sums_sib, mass, w0, w1, w2, w3, own, s1, s2, s3, inv_out):
    states = w0.shape[0]
    batch = mass.shape[0]
    rho_a = sums_own[:, :states] + sums_sib[:, states:]
    rho_b = sums_own[:, states:] + sums_sib[:, :states]
    inv_a = 1.0 / rho_a
    inv_out[...] = inv_a
    u_a = (msg_a[:, :states] * inv_a).astype(BF16)
    u_b = (msg_b[:, :states] * (1.0 / rho_b)).astype(BF16)
    u = jnp.concatenate([u_a, u_b], axis=1)
    own[...] = dot(u, w0[...], NT)
    total = mass[...]
    high = total.astype(BF16)
    low = (total - high.astype(F32)).astype(BF16)
    for w, s in ((w1, s1), (w2, s2), (w3, s3)):
        s[:, :states] = dot(u, w[...], NT).astype(BF16)
        s[:batch, states:] = high
        s[batch:, states:] = low


def combine_first_kernel(
    own, r1, r2, r3, mass, emit, prior, logit, inv, f_out, chain_out, u_out, part_out
):
    states = own.shape[1]
    batch = mass.shape[0]
    summed = own[...]
    total = mass[...]
    for r in (r1, r2, r3):
        summed = summed + r[:, :states].astype(F32)
        total = total + r[:batch, states:].astype(F32) + r[batch:, states:].astype(F32)
    ratio = lane_pick(total, 0) / lane_pick(total, 1)
    p = prior[...]
    restart = jax.nn.sigmoid(logit[...])
    f = emit[batch : 2 * batch] * (summed[:batch] + p * ratio)
    f_out[...] = f
    chain_out[...] = emit[3 * batch :] * summed[batch:]
    u_out[...] = (f * (1.0 - restart) * inv[...]).astype(BF16)
    part_out[...] = lane_pack(
        [lane_pick(total, 1), jnp.sum(f * restart, axis=1, keepdims=True)], batch
    )


def step_kernel(u_a, u_b, w0, w1, w2, w3, own, s1, s2, s3):
    u = jnp.concatenate([u_a[...], u_b[...]], axis=1)
    own[...] = dot(u, w0[...], NT)
    for w, s in ((w1, s1), (w2, s2), (w3, s3)):
        s[...] = dot(u, w[...], NT).astype(BF16)


def combine_kernel(own, r1, r2, r3, emit, logit, inv, g_out, u_out):
    batch = own.shape[0]
    summed = own[...]
    for r in (r1, r2, r3):
        summed = summed + r[...].astype(F32)
    restart = jax.nn.sigmoid(logit[...])
    g = emit[2 * batch : 3 * batch] * summed
    g_out[...] = g
    u_out[...] = (g * (1.0 - restart) * inv[...]).astype(BF16)


def last_kernel(
    own, r1, r2, r3, emit, prior, logit, f1, g2, chain, part, lengths, main_out, part_out
):
    batch = own.shape[0]
    summed = own[...]
    for r in (r1, r2, r3):
        summed = summed + r[...].astype(F32)
    restart = jax.nn.sigmoid(logit[...])
    p = prior[...]
    e = emit[...]
    length = lengths[...]
    h2 = p * e[2 * batch : 3 * batch]
    h3 = p * e[3 * batch :]
    main = jnp.where(
        length == 1,
        p * e[:batch],
        jnp.where(
            length == 2, f1[...], jnp.where(length == 3, g2[...], e[3 * batch :] * summed)
        ),
    )
    side = jnp.where(length == 3, h2, jnp.where(length == 4, chain[...], 0.0))
    tail = jnp.where(length == 4, h3, 0.0)
    main_out[0] = main
    main_out[1] = side
    main_out[2] = tail

    def row(values):
        return jnp.sum(values, axis=1, keepdims=True)

    part_out[...] = lane_pack(
        [
            lane_pick(part[...], 1),
            row(g2[...] * restart),
            row(h2 * restart),
            row(main),
            row(side),
            row(tail),
        ],
        batch,
    )


def finish_kernel(main, part, norm, lengths, scaled_out, like_out):
    total = part[...]
    z = lane_pick(norm[...], 0)
    mass1 = lane_pick(total, 0) / z
    mass2 = (lane_pick(total, 1) + mass1 * lane_pick(total, 2)) / z
    full = lane_pick(total, 3) + mass1 * lane_pick(total, 4) + mass2 * lane_pick(total, 5)
    values = main[0] + mass1 * main[1] + mass2 * main[2]
    scaled_out[...] = values / full
    steps = lengths[...].astype(F32)
    like = jnp.log(full) - jnp.log(z) - steps * math.log(EMIT_SCALE)
    like_out[...] = jnp.broadcast_to(like, like_out.shape)


def per_device(
    state_emb,
    from_weight,
    to_weight,
    emit_weight,
    code_emb,
    init_vec,
    restart_logit,
    block_mask,
    codes,
    lengths,
):
    states, width = state_emb.shape
    vocab = code_emb.shape[0]
    cluster = block_mask.shape[1]
    batch, steps = codes.shape
    cols = lax.axis_size("col")
    parts = lax.axis_size("grp")
    dev = lax.axis_index("col")
    place = dev % cluster
    logit = restart_logit.reshape(1, states)
    length_col = lengths.reshape(batch, 1)

    to_own = vmem_call(project_kernel, shape((states, width), BF16), "to_part")(
        state_emb, to_weight
    )
    to_y = across(to_own, 2)
    to_z = across(to_own, 4)

    from_own, query, prior = vmem_call(
        sources_kernel,
        (
            shape((states, width), BF16),
            shape((states, width), BF16),
            shape((1, states), F32),
        ),
        "sources",
    )(state_emb, from_weight, emit_weight, init_vec.reshape(1, width))
    from_sib = across(from_own, 1)

    tile = 512
    tiles = vocab // tile
    flat_codes = codes.T.reshape(batch * steps, 1)
    pick, total = pl.pallas_call(
        lambda *refs: emission_kernel(tiles // parts, *refs),
        out_shape=(shape((batch * steps, states), F32), shape((1, states), F32)),
        grid_spec=pltpu.PrefetchScalarGridSpec(
            num_scalar_prefetch=1,
            grid=(tiles,),
            in_specs=[
                pl.BlockSpec((tile, width), lambda k, place: (k, 0)),
                pl.BlockSpec((states, width), lambda k, place: (0, 0)),
                pl.BlockSpec((batch * steps, 1), lambda k, place: (0, 0)),
            ],
            out_specs=(
                pl.BlockSpec((batch * steps, states), lambda k, place: (0, 0)),
                pl.BlockSpec((1, states), lambda k, place: (0, 0)),
            ),
            scratch_shapes=[
                pltpu.VMEM((batch * steps, width), F32),
                pltpu.VMEM((8, states), F32),
            ],
        ),
        name="emission",
        compiler_params=pltpu.CompilerParams(vmem_limit_bytes=40 << 20),
    )(lax.axis_index("grp").reshape(1), code_emb, query, flat_codes)
    total_other = across(total, 1, "grp")

    emit, msg = vmem_call(
        hidden_kernel,
        (shape((batch * steps, states), F32), shape((2 * batch, states + 128), F32)),
        "hidden",
    )(pick, total, total_other, prior, logit)
    msg_sib = across(msg, 1)
    mass = msg[:batch, states:] + msg_sib[:batch, states:]
    apart = cluster
    while apart < cols:
        mass = mass + across(mass, apart)
        apart *= 2

    half = states // 2
    to_d0 = across(to_z[:half], 2)
    to_d1 = across(to_y[half:], 4)
    to_d = jnp.concatenate([to_d0, to_d1], axis=0)

    scale = 2.0 / math.sqrt(width)
    row_sums = None
    wts = []
    for k, block in enumerate((to_own, to_y, to_z, to_d)):
        allow = lax.dynamic_slice(block_mask, (dev ^ (2 * k), 0), (1, cluster))[0]
        pair = jnp.stack([allow[place], allow[place ^ 1]]).astype(F32)
        wt, sums = vmem_call(
            lambda *refs: weights_kernel(scale, *refs),
            (shape((states, 2 * states), BF16), shape((1, 2 * states), F32)),
            "weights",
            smem=(3,),
        )(block, from_own, from_sib, pair)
        wts.append(wt)
        row_sums = sums if row_sums is None else row_sums + sums
    row_sums_sib = across(row_sums, 1)

    out = vmem_call(
        first_kernel,
        (shape((2 * batch, states), F32),)
        + (shape((2 * batch, states + 128), BF16),) * 3
        + (shape((1, states), F32),),
        "first",
    )(msg, msg_sib, row_sums, row_sums_sib, mass, *wts)
    own, sends, inv = out[0], out[1:4], out[4]
    received = [across(s, 2 * (k + 1)) for k, s in enumerate(sends)]
    f1, chain, u1, part = vmem_call(
        combine_first_kernel,
        (
            shape((batch, states), F32),
            shape((batch, states), F32),
            shape((batch, states), BF16),
            shape((batch, 128), F32),
        ),
        "combine_first",
    )(own, *received, mass, emit, prior, logit, inv)

    def step(u):
        u_sib = across(u, 1)
        own, *sends = vmem_call(
            step_kernel,
            (shape((batch, states), F32),) + (shape((batch, states), BF16),) * 3,
            "step",
        )(u, u_sib, *wts)
        return [own] + [across(s, 2 * (k + 1)) for k, s in enumerate(sends)]

    g2, u2 = vmem_call(
        combine_kernel, (shape((batch, states), F32), shape((batch, states), BF16)), "combine"
    )(*step(u1), emit, logit, inv)
    main, sums = vmem_call(
        last_kernel, (shape((3, batch, states), F32), shape((batch, 128), F32)), "last"
    )(*step(u2), emit, prior, logit, f1, g2, chain, part, length_col)
    apart = 1
    while apart < cols:
        sums = sums + across(sums, apart)
        apart *= 2
    scaled, like = vmem_call(
        finish_kernel, (shape((batch, states), F32), shape((batch, 128), F32)), "finish"
    )(main, sums, part, length_col)
    return scaled, like[:, 0]


def solution(mesh):
    in_specs = (P("col", None), P(), P(), P(), P(), P(), P("col"), P(), P("grp", None), P("grp"))
    out_specs = (P("grp", "col"), P("grp"))
    return jax.shard_map(
        per_device, mesh=mesh, in_specs=in_specs, out_specs=out_specs, check_vma=False
    )
```

time: 289 us -> 88.3 us (0.31)
  blocking collectives: 163 us -> 0 us
  waiting for transfers between devices: 59 us -> 26 us
  matrix products: 25.8 us -> 0 us
  Pallas kernels: 0 us -> 21.2 us
  starting transfers between devices: 7.26 us -> 23.4 us
  other arithmetic: 14.6 us -> 5.43 us
  local copies, waits for them, and re-layouts: 17.4 us -> 10.9 us
    psum x5 -> x0, blocking collectives: 163 us -> none  [the longest x4 118 us: both_of(): lax.psum((jnp.sum(forward, axis=1), jnp.sum(forward * restart_prob[None,...]
    ppermute x18 -> x24, waiting for transfers between devices: 59 us -> 26 us  [across(): lax.ppermute(shard, axis, [(i, i ^ apart) for i in range(lax.axis_size(ax...]
    dot_general x7 -> x0, matrix products: 25.8 us -> none  [the longest x3 8.79 us: per_device(): jnp.dot(gathered, trans, preferred_element_type=jnp.float32)]
    pallas_call x0 -> x15, Pallas kernels: none -> 21.2 us  [the longest x14 15 us: run(): pl.pallas_call(body, out_shape=out_shape, in_specs=in_specs, out_specs=ou...]
    ppermute x18 -> x24, starting transfers between devices: 7.26 us -> 23.4 us  [across(): lax.ppermute(shard, axis, [(i, i ^ apart) for i in range(lax.axis_size(ax...]
    exp x1 -> x0, local copies, waits for them, and re-layouts: 9.02 us -> none  [per_device(): jnp.exp(soft_cap(3.0 * jnp.einsum('se,ve->sv', query_part, code_emb, pref...]
    select_n x18 -> x0, other arithmetic: 7.56 us -> none  [the longest x11 6.81 us: collect(): jnp.where(is_upper, jnp.concatenate([received, stacked], axis=0), jnp.con...]
    gather x2 -> x0, local copies, waits for them, and re-layouts: 4.33 us -> none  [per_device(): jnp.take(emit_full, codes.reshape(-1), axis=1) / emit_total[:, None]]
  transfers between devices with their start and end apart: 18 -> 24, of which waited for: 13 -> 16; matrix products, arithmetic and copies ran while one was open for 8% -> 9% of each run, Pallas kernels for 0% -> 18%
where the time goes in v1:
time: 88.3 us; the launch traced here: 87.8 us
  waiting for transfers between devices  26 us (29%)
  starting transfers between devices  23.4 us (27%)
  Pallas kernels  21.2 us (24%)
  local copies, waits for them, and re-layouts  10.9 us (12%)
  other arithmetic  5.43 us (6%)
    ppermute x24, waiting for transfers between devices, across(): lax.ppermute(shard, axis, [(i, i ^ apart) for i in range(lax.axis_size(ax...  26 us
    ppermute x24, starting transfers between devices, across(): lax.ppermute(shard, axis, [(i, i ^ apart) for i in range(lax.axis_size(ax...  23.4 us
    pallas_call x14, Pallas kernels, run(): pl.pallas_call(body, out_shape=out_shape, in_specs=in_specs, out_specs=ou...  15 us
    unnamed x20, local copies, waits for them, and re-layouts  8.01 us
    pallas_call x1, Pallas kernels, per_device(): pl.pallas_call(lambda *refs: emission_kernel(tiles // parts, *refs), out_...  6.2 us
    convert_element_type x4, other arithmetic, per_device(): pair = jnp.stack([allow[place], allow[place ^ 1]]).astype(F32)  5.36 us
  transfers between devices with their start and end apart: 24, of which 16 were waited for; matrix products, arithmetic and copies ran while one was open for 9% of the time, Pallas kernels for 18%

profile of v1, /device:TPU:0, one launch (start us, length us, event | category | flops | bytes accessed | tf_op | source)
XLA Modules:
  0.0 87.8 jit_solution(11753844179465350454)
XLA Ops:
  3.2 3.1 %collective-permute-start.4 = (bf16[512,512]{1,0:T(8,128)(2,1)S(1)}, bf16[512,512]{1,0:T(8,128)(2,1)S(1)}, u32[]{:S(2)}, u32[]{:S(2)}) collective-permute-start(bf16[512,512]{1,0:T(8,128)(2,1)S(1)} %to_part.1.refs_0_), channel_id=1, source_target_pairs={{0,4},{1,5},{2,6},{3,7},{4,0},{5,1},{6,2},{7,3},{8,12},{9,13},{10,... | collective-permute-start | bytes 1572872 | tf_op jit(solution)/shard_map/ppermute | solution.py:27
  6.2 1.5 %collective-permute-start.3 = (bf16[512,512]{1,0:T(8,128)(2,1)S(1)}, bf16[512,512]{1,0:T(8,128)(2,1)S(1)}, u32[]{:S(2)}, u32[]{:S(2)}) collective-permute-start(bf16[512,512]{1,0:T(8,128)(2,1)S(1)} %to_part.1.refs_0_), channel_id=1, source_target_pairs={{0,2},{1,3},{2,0},{3,1},{4,6},{5,7},{6,4},{7,5},{8,10},{9,11},{10,... | collective-permute-start | bytes 1572872 | tf_op jit(solution)/shard_map/ppermute | solution.py:27
  12.2 2.2 %copy-done = bf16[4096,512]{1,0:T(8,128)(2,1)S(1)} copy-done((bf16[4096,512]{1,0:T(8,128)(2,1)S(1)}, bf16[4096,512]{1,0:T(8,128)(2,1)}, u32[]{:S(2)}) %copy-start) | copy-done | bytes 4194328
  14.4 6.2 %emission.1 = (f32[128,512]{1,0:T(8,128)S(1)}, f32[1,512]{1,0:T(1,128)S(1)}) custom-call(s32[1]{0:T(128)} %bitcast.refs_0_, bf16[4096,512]{1,0:T(8,128)(2,1)S(1)} %copy-done, bf16[512,512]{1,0:T(8,128)(2,1)S(1)} %get-tuple-element.40.refs_2_, s32[128,1]{1,0:T(8,128)S(1)} %reshape.32.refs_3_), custom_call_target="tpu_custom_call" | custom-call | tf_op jit(solution)/shard_map/emission/pallas_call | solution.py:304
  21.3 1.5 %collective-permute-start = (f32[1,512]{1,0:T(1,128)S(1)}, f32[1,512]{1,0:T(1,128)S(1)}, u32[]{:S(2)}, u32[]{:S(2)}) collective-permute-start(f32[1,512]{1,0:T(1,128)S(1)} %get-tuple-element.42.total_a), channel_id=1, source_target_pairs={{0,16},{16,0},{1,17},{17,1},{2,18},{18,2},{3,19},{19,3},{4,20},{20... | collective-permute-start | bytes 6152 | tf_op jit(solution)/shard_map/ppermute | solution.py:27
  27.4 1.4 %add_convert_fusion.2.refs_3_ = f32[2]{0:T(128)S(1)} fusion(s32[1]{0:T(128)} %bitcast.8, s32[1]{0:T(128)} %bitcast.7), kind=kLoop, calls=%fused_computation.6 | loop fusion | flops 4 | bytes 16 | tf_op jit(solution)/shard_map/convert_element_type | solution.py:351
  31.3 2.7 %collective-permute-start.8 = (f32[32,128]{1,0:T(8,128)S(1)}, f32[32,128]{1,0:T(8,128)S(1)}, u32[]{:S(2)}, u32[]{:S(2)}) collective-permute-start(f32[32,128]{1,0:T(8,128)S(1)} %slice_add_fusion), channel_id=1, source_target_pairs={{0,8},{1,9},{2,10},{3,11},{4,12},{5,13},{6,14},{7,15},{8,0},{9,1},... | collective-permute-start | bytes 49160 | tf_op jit(solution)/shard_map/ppermute | solution.py:27
  34.0 2.1 %weights.5 = (bf16[512,1024]{1,0:T(8,128)(2,1)S(1)}, f32[1,1024]{1,0:T(1,128)S(1)}) custom-call(bf16[512,512]{1,0:T(8,128)(2,1)S(1)} %collective-permute-done.3.refs_0_, bf16[512,512]{1,0:T(8,128)(2,1)S(1)} %get-tuple-element.45.refs_1_, bf16[512,512]{1,0:T(8,128)(2,1)S(1)} %collective-permute-done.2.refs_2_, f32[2]{0:T(128)S(1)} %add_convert_fusion.1.refs_3_), custom_call_target="tpu_custom_call" | custom-call | tf_op jit(solution)/shard_map/weights/pallas_call | solution.py:37
  36.1 2.1 %weights.6 = (bf16[512,1024]{1,0:T(8,128)(2,1)S(1)}, f32[1,1024]{1,0:T(1,128)S(1)}) custom-call(bf16[512,512]{1,0:T(8,128)(2,1)S(1)} %collective-permute-done.4.refs_0_, bf16[512,512]{1,0:T(8,128)(2,1)S(1)} %get-tuple-element.45.refs_1_, bf16[512,512]{1,0:T(8,128)(2,1)S(1)} %collective-permute-done.2.refs_2_, f32[2]{0:T(128)S(1)} %add_convert_fusion.2.refs_3_), custom_call_target="tpu_custom_call" | custom-call | tf_op jit(solution)/shard_map/weights/pallas_call | solution.py:37
  38.2 2.1 %weights.4 = (bf16[512,1024]{1,0:T(8,128)(2,1)S(1)}, f32[1,1024]{1,0:T(1,128)S(1)}) custom-call(bf16[512,512]{1,0:T(8,128)(2,1)S(1)} %to_part.1.refs_0_, bf16[512,512]{1,0:T(8,128)(2,1)S(1)} %get-tuple-element.45.refs_1_, bf16[512,512]{1,0:T(8,128)(2,1)S(1)} %collective-permute-done.2.refs_2_, f32[2]{0:T(128)S(1)} %add_convert_fusion.refs_3_), custom_call_target="tpu_custom_call" | custom-call | tf_op jit(solution)/shard_map/weights/pallas_call | solution.py:37
  40.4 2.1 %weights.7 = (bf16[512,1024]{1,0:T(8,128)(2,1)S(1)}, f32[1,1024]{1,0:T(1,128)S(1)}) custom-call(bf16[512,512]{1,0:T(8,128)(2,1)S(1)} %pad_maximum_fusion.refs_0_, bf16[512,512]{1,0:T(8,128)(2,1)S(1)} %get-tuple-element.45.refs_1_, bf16[512,512]{1,0:T(8,128)(2,1)S(1)} %collective-permute-done.2.refs_2_, f32[2]{0:T(128)S(1)} %add_convert_fusion.3.refs_3_), custom_call_target="tpu_custom_call" | custom-call | tf_op jit(solution)/shard_map/weights/pallas_call | solution.py:37
  45.1 1.6 %collective-permute-start.10 = (bf16[64,640]{1,0:T(8,128)(2,1)S(1)}, bf16[64,640]{1,0:T(8,128)(2,1)S(1)}, u32[]{:S(2)}, u32[]{:S(2)}) collective-permute-start(bf16[64,640]{1,0:T(8,128)(2,1)S(1)} %get-tuple-element.56), channel_id=1, source_target_pairs={{0,4},{1,5},{2,6},{3,7},{4,0},{5,1},{6,2},{7,3},{8,12},{9,13},{10,... | collective-permute-start | bytes 245768 | tf_op jit(solution)/shard_map/ppermute | solution.py:27
  49.7 2.8 %collective-permute-done.11.r3 = bf16[64,640]{1,0:T(8,128)(2,1)S(1)} collective-permute-done((bf16[64,640]{1,0:T(8,128)(2,1)S(1)}, bf16[64,640]{1,0:T(8,128)(2,1)S(1)}, u32[]{:S(2)}, u32[]{:S(2)}) %collective-permute-start.11) | collective-permute-done | bytes 81952 | tf_op jit(solution)/shard_map/ppermute | solution.py:27
  57.2 1.4 %collective-permute-start.14 = (bf16[32,512]{1,0:T(8,128)(2,1)S(1)}, bf16[32,512]{1,0:T(8,128)(2,1)S(1)}, u32[]{:S(2)}, u32[]{:S(2)}) collective-permute-start(bf16[32,512]{1,0:T(8,128)(2,1)S(1)} %get-tuple-element.63), channel_id=1, source_target_pairs={{0,4},{1,5},{2,6},{3,7},{4,0},{5,1},{6,2},{7,3},{8,12},{9,13},{10,... | collective-permute-start | bytes 98312 | tf_op jit(solution)/shard_map/ppermute | solution.py:27
  58.6 1.4 %collective-permute-start.15 = (bf16[32,512]{1,0:T(8,128)(2,1)S(1)}, bf16[32,512]{1,0:T(8,128)(2,1)S(1)}, u32[]{:S(2)}, u32[]{:S(2)}) collective-permute-start(bf16[32,512]{1,0:T(8,128)(2,1)S(1)} %get-tuple-element.64), channel_id=1, source_target_pairs={{0,6},{1,7},{2,4},{3,5},{4,2},{5,3},{6,0},{7,1},{8,14},{9,15},{10,... | collective-permute-start | bytes 98312 | tf_op jit(solution)/shard_map/ppermute | solution.py:27
  61.1 2.3 %collective-permute-done.15.r3 = bf16[32,512]{1,0:T(8,128)(2,1)S(1)} collective-permute-done((bf16[32,512]{1,0:T(8,128)(2,1)S(1)}, bf16[32,512]{1,0:T(8,128)(2,1)S(1)}, u32[]{:S(2)}, u32[]{:S(2)}) %collective-permute-start.15) | collective-permute-done | bytes 32800 | tf_op jit(solution)/shard_map/ppermute | solution.py:27
  66.1 1.5 %collective-permute-start.17 = (bf16[32,512]{1,0:T(8,128)(2,1)S(1)}, bf16[32,512]{1,0:T(8,128)(2,1)S(1)}, u32[]{:S(2)}, u32[]{:S(2)}) collective-permute-start(bf16[32,512]{1,0:T(8,128)(2,1)S(1)} %get-tuple-element.67), channel_id=1, source_target_pairs={{0,2},{1,3},{2,0},{3,1},{4,6},{5,7},{6,4},{7,5},{8,10},{9,11},{10,... | collective-permute-start | bytes 98312 | tf_op jit(solution)/shard_map/ppermute | solution.py:27
  68.1 1.5 %collective-permute-start.19 = (bf16[32,512]{1,0:T(8,128)(2,1)S(1)}, bf16[32,512]{1,0:T(8,128)(2,1)S(1)}, u32[]{:S(2)}, u32[]{:S(2)}) collective-permute-start(bf16[32,512]{1,0:T(8,128)(2,1)S(1)} %get-tuple-element.69), channel_id=1, source_target_pairs={{0,6},{1,7},{2,4},{3,5},{4,2},{5,3},{6,0},{7,1},{8,14},{9,15},{10,... | collective-permute-start | bytes 98312 | tf_op jit(solution)/shard_map/ppermute | solution.py:27
  70.0 1.4 %collective-permute-done.18.r2 = bf16[32,512]{1,0:T(8,128)(2,1)S(1)} collective-permute-done((bf16[32,512]{1,0:T(8,128)(2,1)S(1)}, bf16[32,512]{1,0:T(8,128)(2,1)S(1)}, u32[]{:S(2)}, u32[]{:S(2)}) %collective-permute-start.18) | collective-permute-done | bytes 32800 | tf_op jit(solution)/shard_map/ppermute | solution.py:27
  71.4 1.4 %collective-permute-done.19.r3 = bf16[32,512]{1,0:T(8,128)(2,1)S(1)} collective-permute-done((bf16[32,512]{1,0:T(8,128)(2,1)S(1)}, bf16[32,512]{1,0:T(8,128)(2,1)S(1)}, u32[]{:S(2)}, u32[]{:S(2)}) %collective-permute-start.19) | collective-permute-done | bytes 32800 | tf_op jit(solution)/shard_map/ppermute | solution.py:27
  75.0 3.1 %collective-permute-done.21 = f32[32,128]{1,0:T(8,128)S(1)} collective-permute-done((f32[32,128]{1,0:T(8,128)S(1)}, f32[32,128]{1,0:T(8,128)S(1)}, u32[]{:S(2)}, u32[]{:S(2)}) %collective-permute-start.21) | collective-permute-done | bytes 16416 | tf_op jit(solution)/shard_map/ppermute | solution.py:27
  78.1 1.5 %collective-permute-start.22 = (f32[32,128]{1,0:T(8,128)S(1)}, f32[32,128]{1,0:T(8,128)S(1)}, u32[]{:S(2)}, u32[]{:S(2)}) collective-permute-start(f32[32,128]{1,0:T(8,128)S(1)} %add.84), channel_id=1, source_target_pairs={{0,4},{1,5},{2,6},{3,7},{4,0},{5,1},{6,2},{7,3},{8,12},{9,13},{10,... | collective-permute-start | bytes 49160 | tf_op jit(solution)/shard_map/ppermute | solution.py:27
  79.5 2.2 %collective-permute-done.22 = f32[32,128]{1,0:T(8,128)S(1)} collective-permute-done((f32[32,128]{1,0:T(8,128)S(1)}, f32[32,128]{1,0:T(8,128)S(1)}, u32[]{:S(2)}, u32[]{:S(2)}) %collective-permute-start.22) | collective-permute-done | bytes 16416 | tf_op jit(solution)/shard_map/ppermute | solution.py:27
  82.1 4.3 %collective-permute-done.23 = f32[32,128]{1,0:T(8,128)S(1)} collective-permute-done((f32[32,128]{1,0:T(8,128)S(1)}, f32[32,128]{1,0:T(8,128)S(1)}, u32[]{:S(2)}, u32[]{:S(2)}) %collective-permute-start.23) | collective-permute-done | bytes 16416 | tf_op jit(solution)/shard_map/ppermute | solution.py:27
  (78 shorter events, 33.4 us)
Async XLA Ops:
  3.2 25.7 %collective-permute-start.4 = (bf16[512,512]{1,0:T(8,128)(2,1)S(1)}, bf16[512,512]{1,0:T(8,128)(2,1)S(1)}, u32[]{:S(2)}, u32[]{:S(2)}) collective-permute-start(bf16[512,512]{1,0:T(8,128)(2,1)S(1)} %to_part.1.refs_0_), channel_id=1, source_target_pairs={{0,4},{1,5},{2,6},{3,7},{4,0},{5,1},{6,2},{7,3},{8,12},{9,13},{10,... | collective-permute-start | bytes 1572872 | tf_op jit(solution)/shard_map/ppermute | solution.py:27
  6.2 23.2 %collective-permute-start.3 = (bf16[512,512]{1,0:T(8,128)(2,1)S(1)}, bf16[512,512]{1,0:T(8,128)(2,1)S(1)}, u32[]{:S(2)}, u32[]{:S(2)}) collective-permute-start(bf16[512,512]{1,0:T(8,128)(2,1)S(1)} %to_part.1.refs_0_), channel_id=1, source_target_pairs={{0,2},{1,3},{2,0},{3,1},{4,6},{5,7},{6,4},{7,5},{8,10},{9,11},{10,... | collective-permute-start | bytes 1572872 | tf_op jit(solution)/shard_map/ppermute | solution.py:27
  11.3 22.6 %collective-permute-start.2 = (bf16[512,512]{1,0:T(8,128)(2,1)S(1)}, bf16[512,512]{1,0:T(8,128)(2,1)S(1)}, u32[]{:S(2)}, u32[]{:S(2)}) collective-permute-start(bf16[512,512]{1,0:T(8,128)(2,1)S(1)} %get-tuple-element.45.refs_1_), channel_id=1, source_target_pairs={{0,1},{1,0},{2,3},{3,2},{4,5},{5,4},{6,7},{7,6},{8,9},{9,8},{10,11... | collective-permute-start | bytes 1572872 | tf_op jit(solution)/shard_map/ppermute | solution.py:27
  21.3 4.8 %collective-permute-start = (f32[1,512]{1,0:T(1,128)S(1)}, f32[1,512]{1,0:T(1,128)S(1)}, u32[]{:S(2)}, u32[]{:S(2)}) collective-permute-start(f32[1,512]{1,0:T(1,128)S(1)} %get-tuple-element.42.total_a), channel_id=1, source_target_pairs={{0,16},{16,0},{1,17},{17,1},{2,18},{18,2},{3,19},{19,3},{4,20},{20... | collective-permute-start | bytes 6152 | tf_op jit(solution)/shard_map/ppermute | solution.py:27
  27.2 4.1 %collective-permute-start.1 = (f32[64,640]{1,0:T(8,128)S(1)}, f32[64,640]{1,0:T(8,128)S(1)}, u32[]{:S(2)}, u32[]{:S(2)}) collective-permute-start(f32[64,640]{1,0:T(8,128)S(1)} %get-tuple-element.44.msg_a), channel_id=1, source_target_pairs={{0,1},{1,0},{2,3},{3,2},{4,5},{5,4},{6,7},{7,6},{8,9},{9,8},{10,11... | collective-permute-start | bytes 491528 | tf_op jit(solution)/shard_map/ppermute | solution.py:27
  28.9 11.5 %collective-permute-start.5 = (bf16[256,512]{1,0:T(8,128)(2,1)S(1)}, bf16[256,512]{1,0:T(8,128)(2,1)S(1)}, u32[]{:S(2)}, u32[]{:S(2)}) collective-permute-start(bf16[256,512]{1,0:T(8,128)(2,1)S(1)} %slice.20), channel_id=1, source_target_pairs={{0,2},{1,3},{2,0},{3,1},{4,6},{5,7},{6,4},{7,5},{8,10},{9,11},{10,... | collective-permute-start | bytes 786440 | tf_op jit(solution)/shard_map/ppermute | solution.py:27
  29.5 10.9 %collective-permute-start.6 = (bf16[256,512]{1,0:T(8,128)(2,1)S(1)}, bf16[256,512]{1,0:T(8,128)(2,1)S(1)}, u32[]{:S(2)}, u32[]{:S(2)}) collective-permute-start(bf16[256,512]{1,0:T(8,128)(2,1)S(1)} %slice.21), channel_id=1, source_target_pairs={{0,4},{1,5},{2,6},{3,7},{4,0},{5,1},{6,2},{7,3},{8,12},{9,13},{10,... | collective-permute-start | bytes 786440 | tf_op jit(solution)/shard_map/ppermute | solution.py:27
  31.3 11.3 %collective-permute-start.8 = (f32[32,128]{1,0:T(8,128)S(1)}, f32[32,128]{1,0:T(8,128)S(1)}, u32[]{:S(2)}, u32[]{:S(2)}) collective-permute-start(f32[32,128]{1,0:T(8,128)S(1)} %slice_add_fusion), channel_id=1, source_target_pairs={{0,8},{1,9},{2,10},{3,11},{4,12},{5,13},{6,14},{7,15},{8,0},{9,1},... | collective-permute-start | bytes 49160 | tf_op jit(solution)/shard_map/ppermute | solution.py:27
  42.5 1.2 %collective-permute-start.7 = (f32[1,1024]{1,0:T(1,128)S(1)}, f32[1,1024]{1,0:T(1,128)S(1)}, u32[]{:S(2)}, u32[]{:S(2)}) collective-permute-start(f32[1,1024]{1,0:T(1,128)S(1)} %add_add_fusion.sums_own), channel_id=1, source_target_pairs={{0,1},{1,0},{2,3},{3,2},{4,5},{5,4},{6,7},{7,6},{8,9},{9,8},{10,11... | collective-permute-start | bytes 12296 | tf_op jit(solution)/shard_map/ppermute | solution.py:27
  45.1 4.6 %collective-permute-start.10 = (bf16[64,640]{1,0:T(8,128)(2,1)S(1)}, bf16[64,640]{1,0:T(8,128)(2,1)S(1)}, u32[]{:S(2)}, u32[]{:S(2)}) collective-permute-start(bf16[64,640]{1,0:T(8,128)(2,1)S(1)} %get-tuple-element.56), channel_id=1, source_target_pairs={{0,4},{1,5},{2,6},{3,7},{4,0},{5,1},{6,2},{7,3},{8,12},{9,13},{10,... | collective-permute-start | bytes 245768 | tf_op jit(solution)/shard_map/ppermute | solution.py:27
  46.8 5.8 %collective-permute-start.11 = (bf16[64,640]{1,0:T(8,128)(2,1)S(1)}, bf16[64,640]{1,0:T(8,128)(2,1)S(1)}, u32[]{:S(2)}, u32[]{:S(2)}) collective-permute-start(bf16[64,640]{1,0:T(8,128)(2,1)S(1)} %get-tuple-element.57), channel_id=1, source_target_pairs={{0,6},{1,7},{2,4},{3,5},{4,2},{5,3},{6,0},{7,1},{8,14},{9,15},{10,... | collective-permute-start | bytes 245768 | tf_op jit(solution)/shard_map/ppermute | solution.py:27
  48.2 5.6 %collective-permute-start.9 = (bf16[64,640]{1,0:T(8,128)(2,1)S(1)}, bf16[64,640]{1,0:T(8,128)(2,1)S(1)}, u32[]{:S(2)}, u32[]{:S(2)}) collective-permute-start(bf16[64,640]{1,0:T(8,128)(2,1)S(1)} %get-tuple-element.55), channel_id=1, source_target_pairs={{0,2},{1,3},{2,0},{3,1},{4,6},{5,7},{6,4},{7,5},{8,10},{9,11},{10,... | collective-permute-start | bytes 245768 | tf_op jit(solution)/shard_map/ppermute | solution.py:27
  53.9 1.2 %collective-permute-start.12 = (bf16[32,512]{1,0:T(8,128)(2,1)S(1)}, bf16[32,512]{1,0:T(8,128)(2,1)S(1)}, u32[]{:S(2)}, u32[]{:S(2)}) collective-permute-start(bf16[32,512]{1,0:T(8,128)(2,1)S(1)} %get-tuple-element.60.u_a), channel_id=1, source_target_pairs={{0,1},{1,0},{2,3},{3,2},{4,5},{5,4},{6,7},{7,6},{8,9},{9,8},{10,11... | collective-permute-start | bytes 98312 | tf_op jit(solution)/shard_map/ppermute | solution.py:27
  56.5 3.9 %collective-permute-start.13 = (bf16[32,512]{1,0:T(8,128)(2,1)S(1)}, bf16[32,512]{1,0:T(8,128)(2,1)S(1)}, u32[]{:S(2)}, u32[]{:S(2)}) collective-permute-start(bf16[32,512]{1,0:T(8,128)(2,1)S(1)} %get-tuple-element.62), channel_id=1, source_target_pairs={{0,2},{1,3},{2,0},{3,1},{4,6},{5,7},{6,4},{7,5},{8,10},{9,11},{10,... | collective-permute-start | bytes 98312 | tf_op jit(solution)/shard_map/ppermute | solution.py:27
  57.2 3.9 %collective-permute-start.14 = (bf16[32,512]{1,0:T(8,128)(2,1)S(1)}, bf16[32,512]{1,0:T(8,128)(2,1)S(1)}, u32[]{:S(2)}, u32[]{:S(2)}) collective-permute-start(bf16[32,512]{1,0:T(8,128)(2,1)S(1)} %get-tuple-element.63), channel_id=1, source_target_pairs={{0,4},{1,5},{2,6},{3,7},{4,0},{5,1},{6,2},{7,3},{8,12},{9,13},{10,... | collective-permute-start | bytes 98312 | tf_op jit(solution)/shard_map/ppermute | solution.py:27
  58.6 4.8 %collective-permute-start.15 = (bf16[32,512]{1,0:T(8,128)(2,1)S(1)}, bf16[32,512]{1,0:T(8,128)(2,1)S(1)}, u32[]{:S(2)}, u32[]{:S(2)}) collective-permute-start(bf16[32,512]{1,0:T(8,128)(2,1)S(1)} %get-tuple-element.64), channel_id=1, source_target_pairs={{0,6},{1,7},{2,4},{3,5},{4,2},{5,3},{6,0},{7,1},{8,14},{9,15},{10,... | collective-permute-start | bytes 98312 | tf_op jit(solution)/shard_map/ppermute | solution.py:27
  63.5 1.3 %collective-permute-start.16 = (bf16[32,512]{1,0:T(8,128)(2,1)S(1)}, bf16[32,512]{1,0:T(8,128)(2,1)S(1)}, u32[]{:S(2)}, u32[]{:S(2)}) collective-permute-start(bf16[32,512]{1,0:T(8,128)(2,1)S(1)} %get-tuple-element.65.u_a), channel_id=1, source_target_pairs={{0,1},{1,0},{2,3},{3,2},{4,5},{5,4},{6,7},{7,6},{8,9},{9,8},{10,11... | collective-permute-start | bytes 98312 | tf_op jit(solution)/shard_map/ppermute | solution.py:27
  66.1 3.9 %collective-permute-start.17 = (bf16[32,512]{1,0:T(8,128)(2,1)S(1)}, bf16[32,512]{1,0:T(8,128)(2,1)S(1)}, u32[]{:S(2)}, u32[]{:S(2)}) collective-permute-start(bf16[32,512]{1,0:T(8,128)(2,1)S(1)} %get-tuple-element.67), channel_id=1, source_target_pairs={{0,2},{1,3},{2,0},{3,1},{4,6},{5,7},{6,4},{7,5},{8,10},{9,11},{10,... | collective-permute-start | bytes 98312 | tf_op jit(solution)/shard_map/ppermute | solution.py:27
  67.5 3.9 %collective-permute-start.18 = (bf16[32,512]{1,0:T(8,128)(2,1)S(1)}, bf16[32,512]{1,0:T(8,128)(2,1)S(1)}, u32[]{:S(2)}, u32[]{:S(2)}) collective-permute-start(bf16[32,512]{1,0:T(8,128)(2,1)S(1)} %get-tuple-element.68), channel_id=1, source_target_pairs={{0,4},{1,5},{2,6},{3,7},{4,0},{5,1},{6,2},{7,3},{8,12},{9,13},{10,... | collective-permute-start | bytes 98312 | tf_op jit(solution)/shard_map/ppermute | solution.py:27
  68.1 4.8 %collective-permute-start.19 = (bf16[32,512]{1,0:T(8,128)(2,1)S(1)}, bf16[32,512]{1,0:T(8,128)(2,1)S(1)}, u32[]{:S(2)}, u32[]{:S(2)}) collective-permute-start(bf16[32,512]{1,0:T(8,128)(2,1)S(1)} %get-tuple-element.69), channel_id=1, source_target_pairs={{0,6},{1,7},{2,4},{3,5},{4,2},{5,3},{6,0},{7,1},{8,14},{9,15},{10,... | collective-permute-start | bytes 98312 | tf_op jit(solution)/shard_map/ppermute | solution.py:27
  73.1 1.2 %collective-permute-start.20 = (f32[32,128]{1,0:T(8,128)S(1)}, f32[32,128]{1,0:T(8,128)S(1)}, u32[]{:S(2)}, u32[]{:S(2)}) collective-permute-start(f32[32,128]{1,0:T(8,128)S(1)} %get-tuple-element.75), channel_id=1, source_target_pairs={{0,1},{1,0},{2,3},{3,2},{4,5},{5,4},{6,7},{7,6},{8,9},{9,8},{10,11... | collective-permute-start | bytes 49160 | tf_op jit(solution)/shard_map/ppermute | solution.py:27
  74.3 3.7 %collective-permute-start.21 = (f32[32,128]{1,0:T(8,128)S(1)}, f32[32,128]{1,0:T(8,128)S(1)}, u32[]{:S(2)}, u32[]{:S(2)}) collective-permute-start(f32[32,128]{1,0:T(8,128)S(1)} %add.83), channel_id=1, source_target_pairs={{0,2},{1,3},{2,0},{3,1},{4,6},{5,7},{6,4},{7,5},{8,10},{9,11},{10,... | collective-permute-start | bytes 49160 | tf_op jit(solution)/shard_map/ppermute | solution.py:27
  78.1 3.7 %collective-permute-start.22 = (f32[32,128]{1,0:T(8,128)S(1)}, f32[32,128]{1,0:T(8,128)S(1)}, u32[]{:S(2)}, u32[]{:S(2)}) collective-permute-start(f32[32,128]{1,0:T(8,128)S(1)} %add.84), channel_id=1, source_target_pairs={{0,4},{1,5},{2,6},{3,7},{4,0},{5,1},{6,2},{7,3},{8,12},{9,13},{10,... | collective-permute-start | bytes 49160 | tf_op jit(solution)/shard_map/ppermute | solution.py:27
  81.8 4.6 %collective-permute-start.23 = (f32[32,128]{1,0:T(8,128)S(1)}, f32[32,128]{1,0:T(8,128)S(1)}, u32[]{:S(2)}, u32[]{:S(2)}) collective-permute-start(f32[32,128]{1,0:T(8,128)S(1)} %add.85), channel_id=1, source_target_pairs={{0,8},{1,9},{2,10},{3,11},{4,12},{5,13},{6,14},{7,15},{8,0},{9,1},... | collective-permute-start | bytes 49160 | tf_op jit(solution)/shard_map/ppermute | solution.py:27
  (10 other events, 67.2 us)

commit v2 on v0

v2 whole, which is shorter than its diff:
```python
import math

import jax
import jax.numpy as jnp
from jax import lax
from jax.experimental import pallas as pl
from jax.experimental.pallas import tpu as pltpu
from jax.sharding import PartitionSpec as P

SOFT_CAP = 10.0
EMIT_SCALE = 2.0**20
F32 = jnp.float32
BF16 = jnp.bfloat16
NT = (((1,), (1,)), ((), ()))
NN = (((1,), (0,)), ((), ()))


def dot(lhs, rhs, dims):
    return lax.dot_general(lhs, rhs, dims, preferred_element_type=F32)


def across(shard, apart, axis="col"):
    return lax.ppermute(shard, axis, [(i, i ^ apart) for i in range(lax.axis_size(axis))])


def call(body, out_shape, name, smem=(), hbm=(), scratch=(), limit=16, aliases=None):
    def run(*args):
        def space(k):
            if k in smem:
                return pltpu.SMEM
            return pltpu.HBM if k in hbm else pltpu.VMEM

        return pl.pallas_call(
            body,
            out_shape=out_shape,
            in_specs=[pl.BlockSpec(memory_space=space(k)) for k in range(len(args))],
            out_specs=jax.tree.map(lambda s: pl.BlockSpec(memory_space=pltpu.VMEM), out_shape),
            scratch_shapes=scratch,
            input_output_aliases=aliases or {},
            name=name,
            compiler_params=pltpu.CompilerParams(vmem_limit_bytes=limit << 20),
        )(
            *(
                pltpu.with_memory_space_constraint(arg, pltpu.HBM) if k in hbm else arg
                for k, arg in enumerate(args)
            )
        )

    return run


def shape(dims, dtype):
    return jax.ShapeDtypeStruct(dims, dtype)


def capped_exp(values, scale):
    return jnp.exp2((SOFT_CAP / math.log(2.0)) * jnp.tanh(values * (scale / SOFT_CAP)))


def project_kernel(emb_hbm, weight_hbm, out, emb, weight, sem):
    copies = [
        pltpu.make_async_copy(emb_hbm, emb, sem.at[0]),
        pltpu.make_async_copy(weight_hbm, weight, sem.at[1]),
    ]
    for copy in copies:
        copy.start()
    for copy in copies:
        copy.wait()
    out[...] = dot(emb[...], weight[...], NN).astype(BF16)


def emission_kernel(
    tile,
    emb_hbm,
    from_hbm,
    emit_hbm,
    code_hbm,
    init_vec,
    codes,
    from_out,
    prior_out,
    pick_out,
    total_out,
    emb,
    from_w,
    emit_w,
    code,
    sem,
    code_sem,
):
    vocab = code.shape[0]
    tiles = vocab // tile
    own_tiles = tiles // lax.axis_size("grp")
    first = lax.axis_index("grp") * own_tiles
    copies = [
        pltpu.make_async_copy(src, dst, sem.at[k])
        for k, (src, dst) in enumerate(
            ((emb_hbm, emb), (emit_hbm, emit_w), (from_hbm, from_w))
        )
    ]
    starts = []
    for k in range(tiles):
        start = lax.rem(first + k, tiles) * tile
        start = pl.multiple_of(start, tile)
        starts.append(start)
        copies.append(
            pltpu.make_async_copy(
                code_hbm.at[pl.ds(start, tile)], code.at[pl.ds(k * tile, tile)], code_sem.at[k]
            )
        )
    for copy in copies:
        copy.start()
    copies[0].wait()
    copies[1].wait()
    query = dot(emb[...], emit_w[...], NN).astype(BF16)
    states = emb.shape[0]
    prior = dot(jnp.broadcast_to(init_vec[...].reshape(1, -1), (8, emb.shape[1])), emb[...], NT)
    prior_out[...] = capped_exp(prior, 2.0)[:1]
    copies[2].wait()
    from_out[...] = dot(emb[...], from_w[...], NN).astype(BF16)
    steps, batch = codes.shape
    ids = jnp.concatenate([column(codes[t : t + 1, :]) for t in range(steps)], axis=0)
    rows = jnp.zeros((batch * steps, code.shape[1]), F32)
    total = jnp.zeros((8, states), F32)
    for k in range(tiles):
        copies[3 + k].wait()
        block = code[k * tile : (k + 1) * tile, :]
        lanes = lax.broadcasted_iota(jnp.int32, (batch * steps, tile), 1) + starts[k]
        lanes = lanes.astype(F32)
        one_hot = jnp.where(lanes == ids, 1.0, 0.0).astype(BF16)
        rows = rows + dot(one_hot, block, NN)
        if k < own_tiles:
            weights = capped_exp(dot(block, query, NT), 3.0)
            total = total + jnp.sum(weights.reshape(tile // 8, 8, states), axis=0)
    total_out[...] = jnp.sum(total, axis=0, keepdims=True)
    pick_out[...] = capped_exp(dot(rows.astype(BF16), query, NT), 3.0)


def column(row):
    count = row.shape[1]
    at_row = lax.broadcasted_iota(jnp.int32, (count, count), 0)
    at_lane = lax.broadcasted_iota(jnp.int32, (count, count), 1)
    return row_sum(jnp.where(at_row == at_lane, row.astype(F32), 0.0))


def lane_pack(columns, rows):
    lane = lax.broadcasted_iota(jnp.int32, (rows, 128), 1)
    packed = jnp.zeros((rows, 128), F32)
    for k, column in enumerate(columns):
        packed = jnp.where(lane == k, column, packed)
    return packed


def lane_pick(packed, k):
    lane = lax.broadcasted_iota(jnp.int32, packed.shape, 1)
    return jnp.sum(jnp.where(lane == k, packed, 0.0), axis=1, keepdims=True)


def split(packed):
    high = packed.astype(BF16).astype(F32)
    return (high + pltpu.roll(packed - high, 64, 1)).astype(BF16)


def joined(pair):
    pair = pair.astype(F32)
    return pair + pltpu.roll(pair, 64, 1)


def row_sum(values):
    return jnp.sum(values, axis=1, keepdims=True)


def hidden_kernel(pick, total_a, total_b, prior, logit, emit_out, msg_out, mass_out):
    batch = pick.shape[0] // 4
    factor = EMIT_SCALE / (total_a[...] + total_b[...])
    emit = pick[...] * factor
    emit_out[...] = emit
    p = prior[...]
    restart = jax.nn.sigmoid(logit[...])
    first = p * emit[:batch]
    third = p * emit[2 * batch : 3 * batch]
    states = p.shape[1]
    msg_out[:batch, :states] = first * (1.0 - restart)
    msg_out[batch:, :states] = third * (1.0 - restart)
    mass = row_sum(first * restart)
    norm = jnp.broadcast_to(row_sum(p), mass.shape)
    packed = lane_pack([mass, norm], batch)
    msg_out[:batch, states:] = packed
    msg_out[batch:, states:] = jnp.zeros((batch, 128), F32)
    mass_out[...] = packed


def weights_kernel(scale, shifts, mask, from_a, from_b, *refs):
    states = from_a.shape[0]
    count = len(shifts)
    blocks, outs = refs[:count], refs[len(refs) - count - 1 : -1]
    before, sum_out = refs[count : len(refs) - count - 1], refs[-1]
    place = lax.rem(lax.axis_index("col"), mask.shape[0])
    tile = states // 2
    for side, source in ((0, from_a), (1, from_b)):
        lanes = slice(side * states, (side + 1) * states)
        sums = jnp.zeros((8, states), F32)
        for shift, block, out in zip(shifts, blocks, outs):
            row = lax.axis_index("col") ^ shift
            keep = mask[place ^ side, row].astype(F32)
            for k in range(2):
                rows = slice(k * tile, (k + 1) * tile)
                weights = capped_exp(dot(block[rows, :], source[...], NT), scale) * keep
                out[rows, lanes] = weights.astype(BF16)
                sums = sums + jnp.sum(weights.reshape(tile // 8, 8, states), axis=0)
        summed = jnp.sum(sums, axis=0, keepdims=True)
        for other in before:
            summed = summed + other[:, lanes]
        sum_out[:, lanes] = summed


def first_kernel(
    msg_a, msg_b, sums_own, sums_sib, mass, emit, w0, w1, w2, w3, own, s1, s2, s3, inv_out
):
    states = w0.shape[0]
    batch = mass.shape[0]
    inv_a = 1.0 / (sums_own[:, :states] + sums_sib[:, states:])
    inv_b = 1.0 / (sums_own[:, states:] + sums_sib[:, :states])
    inv_out[...] = inv_a
    u_a = (msg_a[:, :states] * inv_a).astype(BF16)
    u_b = (msg_b[:, :states] * inv_b).astype(BF16)
    u = jnp.concatenate([u_a, u_b], axis=1)
    own[...] = dot(u, w0[...], NT)
    pair = split(mass[...])
    last = emit[3 * batch :].astype(BF16)
    for w, s in ((w1, s1), (w2, s2), (w3, s3)):
        s[: 2 * batch, :states] = dot(u, w[...], NT).astype(BF16)
        s[2 * batch :, :states] = last
        s[:batch, states:] = pair
        s[batch:, states:] = jnp.zeros((2 * batch, 128), BF16)


def combine_first_kernel(
    own, r1, r2, r3, mass, emit, prior, logit, inv, f_out, chain_out, u_out, part_out
):
    states = own.shape[1]
    batch = mass.shape[0]
    summed = own[...]
    total = mass[...]
    for r in (r1, r2, r3):
        summed = summed + r[: 2 * batch, :states].astype(F32)
        total = total + joined(r[:batch, states:])
    norm = lane_pick(total, 1)
    ratio = lane_pick(total, 0) / norm
    p = prior[...]
    restart = jax.nn.sigmoid(logit[...])
    f = emit[batch : 2 * batch] * (summed[:batch] + p * ratio)
    f_out[...] = f
    chain_out[...] = emit[3 * batch :] * summed[batch:]
    u_out[...] = (f * (1.0 - restart) * inv[...]).astype(BF16)
    part_out[...] = lane_pack([norm, row_sum(f * restart)], batch)


def backward_kernel(emit, r1, r2, r3, w0, w1, w2, w3, out):
    states = w0.shape[0]
    batch = out.shape[0]
    acc = dot(emit[3 * batch :].astype(BF16), w0[...], NN)
    for r, w in ((r1, w1), (r2, w2), (r3, w3)):
        acc = acc + dot(r[2 * batch :, :states], w[...], NN)
    out[...] = acc


def step_kernel(u_a, u_b, w0, w1, w2, w3, own, s1, s2, s3):
    states = w0.shape[0]
    u_a = u_a[:, :states]
    u_b = u_b[:, :states]
    u = jnp.concatenate([u_a, u_b], axis=1)
    own[...] = dot(u, w0[...], NT)
    for w, s in ((w1, s1), (w2, s2), (w3, s3)):
        s[:, :states] = dot(u, w[...], NT).astype(BF16)


def combine_kernel(
    own, r1, r2, r3, emit, prior, logit, inv, f1, chain, part, lengths, g_out, msg_out
):
    batch, states = own.shape
    summed = own[...]
    for r in (r1, r2, r3):
        summed = summed + r[...].astype(F32)
    restart = jax.nn.sigmoid(logit[...])
    p = prior[...]
    e = emit[...]
    length = column(lengths[...])
    g = e[2 * batch : 3 * batch] * summed
    g_out[...] = g
    msg_out[:, :states] = (g * (1.0 - restart) * inv[...]).astype(BF16)
    h2 = p * e[2 * batch : 3 * batch]
    main = jnp.where(length == 1, p * e[:batch], jnp.where(length == 2, f1[...], g))
    side = jnp.where(length == 3, h2, chain[...])
    packed = lane_pack(
        [
            lane_pick(part[...], 1),
            row_sum(g * restart),
            row_sum(h2 * restart),
            jnp.where(length < 4, row_sum(main), 0.0),
            jnp.where(length >= 3, row_sum(side), 0.0),
            jnp.where(length >= 4, row_sum(p * e[3 * batch :]), 0.0),
        ],
        batch,
    )
    msg_out[:, states:] = split(packed)


def totals_kernel(msg_a, msg_b, back_a, back_b, lengths, out):
    states = msg_a.shape[1] - 128
    u_a = msg_a[:, :states].astype(F32)
    u_b = msg_b[:, :states].astype(F32)
    total = joined(msg_a[:, states:]) + joined(msg_b[:, states:])
    last = u_a * (back_a[:, :states] + back_b[:, states:])
    last = row_sum(last + u_b * (back_a[:, states:] + back_b[:, :states]))
    lane = lax.broadcasted_iota(jnp.int32, total.shape, 1)
    total = jnp.where(lane < 6, total, 0.0)
    out[...] = total + jnp.where((lane == 3) & (column(lengths[...]) == 4), last, 0.0)


def attach_kernel(total, s1, s2, s3, o1, o2, o3):
    states = s1.shape[1] - 128
    pair = split(total[...])
    for out in (o1, o2, o3):
        out[:, states:] = pair


def finish_kernel(
    own, r1, r2, r3, totals, emit, prior, f1, g2, chain, part, lengths, scaled_out, like_out
):
    batch, states = own.shape
    summed = own[...]
    total = totals[...]
    for r in (r1, r2, r3):
        summed = summed + r[:, :states].astype(F32)
        total = total + joined(r[:, states:])
    p = prior[...]
    e = emit[...]
    length = column(lengths[...])
    z = lane_pick(part[...], 0)
    mass1 = lane_pick(total, 0) / z
    mass2 = (lane_pick(total, 1) + mass1 * lane_pick(total, 2)) / z
    full = lane_pick(total, 3) + mass1 * lane_pick(total, 4) + mass2 * lane_pick(total, 5)
    f2 = g2[...] + mass1 * (p * e[2 * batch : 3 * batch])
    f3 = e[3 * batch :] * (summed + p * mass2) + mass1 * chain[...]
    values = jnp.where(
        length == 1,
        p * e[:batch],
        jnp.where(length == 2, f1[...], jnp.where(length == 3, f2, f3)),
    )
    scaled_out[...] = values / full
    like = jnp.log(full) - jnp.log(z) - length * math.log(EMIT_SCALE)
    diagonal = lax.broadcasted_iota(jnp.int32, (batch, batch), 0) == lax.broadcasted_iota(
        jnp.int32, (batch, batch), 1
    )
    like_out[...] = jnp.sum(jnp.where(diagonal, like, 0.0), axis=0, keepdims=True)


def per_device(
    state_emb,
    from_weight,
    to_weight,
    emit_weight,
    code_emb,
    init_vec,
    restart_logit,
    block_mask,
    codes,
    lengths,
):
    states, width = state_emb.shape
    vocab = code_emb.shape[0]
    cluster = block_mask.shape[1]
    batch, steps = codes.shape
    cols = lax.axis_size("col")
    logit = restart_logit.reshape(1, states)
    length_row = lengths.reshape(1, batch)
    square = shape((states, width), BF16)
    plane = shape((batch, states), F32)
    lanes = shape((batch, 128), F32)
    half_plane = shape((batch, states), BF16)
    message = shape((batch, states + 128), BF16)

    to_own = call(
        project_kernel,
        square,
        "to_part",
        hbm=(0, 1),
        scratch=[
            pltpu.VMEM((states, width), BF16),
            pltpu.VMEM((width, width), BF16),
            pltpu.SemaphoreType.DMA((2,)),
        ],
        limit=32,
    )(state_emb, to_weight)
    to_y = across(to_own, 2)
    to_z = across(to_own, 4)

    tile = 512
    from_own, prior, pick, total = call(
        lambda *refs: emission_kernel(tile, *refs),
        (
            square,
            shape((1, states), F32),
            shape((batch * steps, states), F32),
            shape((1, states), F32),
        ),
        "emission",
        hbm=(0, 1, 2, 3),
        scratch=[
            pltpu.VMEM((states, width), BF16),
            pltpu.VMEM((width, width), BF16),
            pltpu.VMEM((width, width), BF16),
            pltpu.VMEM((vocab, width), BF16),
            pltpu.SemaphoreType.DMA((3,)),
            pltpu.SemaphoreType.DMA((vocab // tile,)),
        ],
        limit=32,
    )(state_emb, from_weight, emit_weight, code_emb, init_vec, codes.T)
    from_sib = across(from_own, 1)
    total_other = across(total, 1, "grp")

    half = states // 2
    to_d0 = across(to_z[:half], 2)
    to_d1 = across(to_y[half:], 4)

    emit, msg, mass_own = call(
        hidden_kernel,
        (shape((batch * steps, states), F32), shape((2 * batch, states + 128), F32), lanes),
        "hidden",
    )(pick, total, total_other, prior, logit)
    msg_sib = across(msg, 1)

    scale = 2.0 / math.sqrt(width)
    sums_shape = shape((1, 2 * states), F32)
    wt_shape = shape((states, 2 * states), BF16)
    w0, sums0 = call(
        lambda *refs: weights_kernel(scale, (0,), *refs), (wt_shape, sums_shape), "weights", (0,)
    )(block_mask.T, from_own, from_sib, to_own)
    w1, w2, sums1 = call(
        lambda *refs: weights_kernel(scale, (2, 4), *refs),
        (wt_shape, wt_shape, sums_shape),
        "weights",
        (0,),
    )(block_mask.T, from_own, from_sib, to_y, to_z, sums0)
    mass = mass_own + msg_sib[:batch, states:]
    apart = cluster
    while apart < cols:
        mass = mass + across(mass, apart)
        apart *= 2
    to_d = jnp.concatenate([to_d0, to_d1], axis=0)
    w3, row_sums = call(
        lambda *refs: weights_kernel(scale, (6,), *refs), (wt_shape, sums_shape), "weights", (0,)
    )(block_mask.T, from_own, from_sib, to_d, sums1)
    wts = (w0, w1, w2, w3)
    row_sums_sib = across(row_sums, 1)

    out = call(
        first_kernel,
        (shape((2 * batch, states), F32),)
        + (shape((3 * batch, states + 128), BF16),) * 3
        + (shape((1, states), F32),),
        "first",
    )(msg, msg_sib, row_sums, row_sums_sib, mass, emit, *wts)
    own, sends, inv = out[0], out[1:4], out[4]
    received = [across(s, 2 * (k + 1)) for k, s in enumerate(sends)]
    f1, chain, u1, part = call(
        combine_first_kernel, (plane, plane, half_plane, lanes), "combine_first"
    )(own, *received, mass, emit, prior, logit, inv)
    u1_sib = across(u1, 1)
    held, _ = lax.optimization_barrier((tuple(received), u1))
    back = call(backward_kernel, shape((batch, 2 * states), F32), "backward")(emit, *held, *wts)
    own, *sends = call(step_kernel, (plane,) + (half_plane,) * 3, "step")(u1, u1_sib, *wts)
    back_sib = across(back, 1)
    received = [across(s, 2 * (k + 1)) for k, s in enumerate(sends)]
    g2, msg2 = call(combine_kernel, (plane, message), "combine")(
        own, *received, emit, prior, logit, inv, f1, chain, part, length_row
    )
    msg2_sib = across(msg2, 1)
    totals = call(totals_kernel, lanes, "totals")(msg2, msg2_sib, back, back_sib, length_row)
    own, *sends = call(step_kernel, (plane,) + (message,) * 3, "step")(msg2, msg2_sib, *wts)
    apart = cluster
    while apart < cols:
        totals = totals + across(totals, apart)
        apart *= 2
    sends = call(attach_kernel, (message,) * 3, "attach", aliases={1: 0, 2: 1, 3: 2})(
        totals, *sends
    )
    received = [across(s, 2 * (k + 1)) for k, s in enumerate(sends)]
    scaled, like = call(finish_kernel, (plane, shape((1, batch), F32)), "finish")(
        own, *received, totals, emit, prior, f1, g2, chain, part, length_row
    )
    return scaled, like.reshape(batch)


def solution(mesh):
    in_specs = (P("col", None), P(), P(), P(), P(), P(), P("col"), P(), P("grp", None), P("grp"))
    out_specs = (P("grp", "col"), P("grp"))
    return jax.shard_map(
        per_device, mesh=mesh, in_specs=in_specs, out_specs=out_specs, check_vma=False
    )
```

time: 289 us -> 66.5 us (0.23)
  blocking collectives: 163 us -> 0 us
  waiting for transfers between devices: 59 us -> 19.6 us
  matrix products: 25.8 us -> 0 us
  Pallas kernels: 0 us -> 19.9 us
  starting transfers between devices: 7.26 us -> 24.5 us
  local copies, waits for them, and re-layouts: 17.4 us -> 1.41 us
  other arithmetic: 14.6 us -> 0.05 us
    psum x5 -> x0, blocking collectives: 163 us -> none  [the longest x4 118 us: both_of(): lax.psum((jnp.sum(forward, axis=1), jnp.sum(forward * restart_prob[None,...]
    ppermute x18 -> x22, waiting for transfers between devices: 59 us -> 19.6 us  [across(): lax.ppermute(shard, axis, [(i, i ^ apart) for i in range(lax.axis_size(ax...]
    dot_general x7 -> x0, matrix products: 25.8 us -> none  [the longest x3 8.79 us: per_device(): jnp.dot(gathered, trans, preferred_element_type=jnp.float32)]
    pallas_call x0 -> x15, Pallas kernels: none -> 19.9 us  [run(): pl.pallas_call(body, out_shape=out_shape, in_specs=[pl.BlockSpec(memory_s...]
    ppermute x18 -> x22, starting transfers between devices: 7.26 us -> 24.5 us  [across(): lax.ppermute(shard, axis, [(i, i ^ apart) for i in range(lax.axis_size(ax...]
    exp x1 -> x0, local copies, waits for them, and re-layouts: 9.02 us -> none  [per_device(): jnp.exp(soft_cap(3.0 * jnp.einsum('se,ve->sv', query_part, code_emb, pref...]
    select_n x18 -> x0, other arithmetic: 7.56 us -> none  [the longest x11 6.81 us: collect(): jnp.where(is_upper, jnp.concatenate([received, stacked], axis=0), jnp.con...]
    convert_element_type x2 -> x0, other arithmetic: 4.45 us -> none  [the longest x1 4.37 us: per_device(): trans = (weights_exp / row_sum[:, None]).astype(jnp.bfloat16)]
  transfers between devices with their start and end apart: 18 -> 22, of which waited for: 13 -> 15; matrix products, arithmetic and copies ran while one was open for 8% -> 0% of each run, Pallas kernels for 0% -> 22%
where the time goes in v2:
time: 66.5 us; the launch traced here: 66.3 us
  starting transfers between devices  24.5 us (37%)
  Pallas kernels  19.9 us (30%)
  waiting for transfers between devices  19.6 us (29%)
  local copies, waits for them, and re-layouts  1.41 us (2%)
  between operations  0.8 us (1%)
    ppermute x22, starting transfers between devices, across(): lax.ppermute(shard, axis, [(i, i ^ apart) for i in range(lax.axis_size(ax...  24.5 us
    pallas_call x15, Pallas kernels, run(): pl.pallas_call(body, out_shape=out_shape, in_specs=[pl.BlockSpec(memory_s...  19.9 us
    ppermute x22, waiting for transfers between devices, across(): lax.ppermute(shard, axis, [(i, i ^ apart) for i in range(lax.axis_size(ax...  19.6 us
    unnamed x10, local copies, waits for them, and re-layouts  1.37 us
  transfers between devices with their start and end apart: 22, of which 15 were waited for; matrix products, arithmetic and copies ran while one was open for 0% of the time, Pallas kernels for 22%

profile of v2, /device:TPU:0, one launch (start us, length us, event | category | flops | bytes accessed | tf_op | source)
XLA Modules:
  0.0 66.3 jit_solution(14076267327258977318)
XLA Ops:
  0.7 1.7 %to_part.1.refs_3_ = bf16[512,512]{1,0:T(8,128)(2,1)S(1)} custom-call(bf16[512,512]{1,0:T(8,128)(2,1)} %emb_hbm.1, bf16[512,512]{1,0:T(8,128)(2,1)} %weight_hbm.1), custom_call_target="tpu_custom_call" | custom-call | tf_op jit(solution)/shard_map/to_part/pallas_call | solution.py:33
  2.3 3.0 %collective-permute-start.5 = (bf16[512,512]{1,0:T(8,128)(2,1)S(1)}, bf16[512,512]{1,0:T(8,128)(2,1)S(1)}, u32[]{:S(2)}, u32[]{:S(2)}) collective-permute-start(bf16[512,512]{1,0:T(8,128)(2,1)S(1)} %to_part.1.refs_3_), channel_id=1, source_target_pairs={{0,2},{1,3},{2,0},{3,1},{4,6},{5,7},{6,4},{7,5},{8,10},{9,11},{10,... | collective-permute-start | bytes 1572872 | tf_op jit(solution)/shard_map/ppermute | solution.py:23
  5.4 1.6 %collective-permute-start.3 = (bf16[512,512]{1,0:T(8,128)(2,1)S(1)}, bf16[512,512]{1,0:T(8,128)(2,1)S(1)}, u32[]{:S(2)}, u32[]{:S(2)}) collective-permute-start(bf16[512,512]{1,0:T(8,128)(2,1)S(1)} %to_part.1.refs_3_), channel_id=1, source_target_pairs={{0,4},{1,5},{2,6},{3,7},{4,0},{5,1},{6,2},{7,3},{8,12},{9,13},{10,... | collective-permute-start | bytes 1572872 | tf_op jit(solution)/shard_map/ppermute | solution.py:23
  8.3 6.7 %emission.1 = (bf16[512,512]{1,0:T(8,128)(2,1)S(1)}, f32[1,512]{1,0:T(1,128)S(1)}, f32[128,512]{1,0:T(8,128)S(1)}, f32[1,512]{1,0:T(1,128)S(1)}) custom-call(bf16[512,512]{1,0:T(8,128)(2,1)} %emb_hbm.1, bf16[512,512]{1,0:T(8,128)(2,1)} %refs_1_.1, bf16[512,512]{1,0:T(8,128)(2,1)} %refs_2_.1, bf16[4096,512]{1,0:T(8,128)(2,1)} %refs_3_.1, ...), custom_call_target="tpu_custom_call" | custom-call | tf_op jit(solution)/shard_map/emission/pallas_call | solution.py:33
  15.1 1.6 %collective-permute-start = (f32[1,512]{1,0:T(1,128)S(1)}, f32[1,512]{1,0:T(1,128)S(1)}, u32[]{:S(2)}, u32[]{:S(2)}) collective-permute-start(f32[1,512]{1,0:T(1,128)S(1)} %get-tuple-element.44.total_a), channel_id=1, source_target_pairs={{0,16},{16,0},{1,17},{17,1},{2,18},{18,2},{3,19},{19,3},{4,20},{20... | collective-permute-start | bytes 6152 | tf_op jit(solution)/shard_map/ppermute | solution.py:23
  16.7 2.1 %collective-permute-done.total_b = f32[1,512]{1,0:T(1,128)S(1)} collective-permute-done((f32[1,512]{1,0:T(1,128)S(1)}, f32[1,512]{1,0:T(1,128)S(1)}, u32[]{:S(2)}, u32[]{:S(2)}) %collective-permute-start) | collective-permute-done | bytes 2080 | tf_op jit(solution)/shard_map/ppermute | solution.py:23
  20.8 2.6 %collective-permute-start.8 = (f32[32,128]{1,0:T(8,128)S(1)}, f32[32,128]{1,0:T(8,128)S(1)}, u32[]{:S(2)}, u32[]{:S(2)}) collective-permute-start(f32[32,128]{1,0:T(8,128)S(1)} %slice_add_fusion), channel_id=1, source_target_pairs={{0,8},{1,9},{2,10},{3,11},{4,12},{5,13},{6,14},{7,15},{8,0},{9,1},... | collective-permute-start | bytes 49160 | tf_op jit(solution)/shard_map/ppermute | solution.py:23
  23.4 1.5 %weights.3 = (bf16[512,1024]{1,0:T(8,128)(2,1)S(1)}, f32[1,1024]{1,0:T(1,128)S(1)}) custom-call(s32[8,16]{1,0:T(8,128)S(1)} %bitcast.5, bf16[512,512]{1,0:T(8,128)(2,1)S(1)} %get-tuple-element.47.refs_1_, bf16[512,512]{1,0:T(8,128)(2,1)S(1)} %collective-permute-done.2.refs_2_, bf16[512,512]{1,0:T(8,128)(2,1)S(1)} %to_part.1.refs_3_), custom_call_target="tpu_custom_call" | custom-call | tf_op jit(solution)/shard_map/weights/pallas_call | solution.py:33
  24.9 2.1 %weights.4 = (bf16[512,1024]{1,0:T(8,128)(2,1)S(1)}, bf16[512,1024]{1,0:T(8,128)(2,1)S(1)}, f32[1,1024]{1,0:T(1,128)S(1)}) custom-call(s32[8,16]{1,0:T(8,128)S(1)} %bitcast.6, bf16[512,512]{1,0:T(8,128)(2,1)S(1)} %get-tuple-element.47.refs_1_, bf16[512,512]{1,0:T(8,128)(2,1)S(1)} %collective-permute-done.2.refs_2_, ...), custom_call_target="tpu_custom_call" | custom-call | tf_op jit(solution)/shard_map/weights/pallas_call | solution.py:33
  28.1 1.5 %weights.5 = (bf16[512,1024]{1,0:T(8,128)(2,1)S(1)}, f32[1,1024]{1,0:T(1,128)S(1)}) custom-call(s32[8,16]{1,0:T(8,128)S(1)} %bitcast.7, bf16[512,512]{1,0:T(8,128)(2,1)S(1)} %get-tuple-element.47.refs_1_, bf16[512,512]{1,0:T(8,128)(2,1)S(1)} %collective-permute-done.2.refs_2_, bf16[512,512]{1,0:T(8,128)(2,1)S(1)} %pad_maximum_fusion.refs_3_, ...), custom_call_target="tpu_custom_call" | custom-call | tf_op jit(solution)/shard_map/weights/pallas_call | solution.py:33
  30.8 1.4 %first.1 = (f32[64,512]{1,0:T(8,128)S(1)}, bf16[96,640]{1,0:T(8,128)(2,1)S(1)}, bf16[96,640]{1,0:T(8,128)(2,1)S(1)}, bf16[96,640]{1,0:T(8,128)(2,1)S(1)}, f32[1,512]{1,0:T(1,128)S(1)}) custom-call(f32[64,640]{1,0:T(8,128)S(1)} %get-tuple-element.46.msg_a, f32[64,640]{1,0:T(8,128)S(1)} %collective-permute-done.1.msg_b, ...), custom_call_target="tpu_custom_call" | custom-call | tf_op jit(solution)/shard_map/first/pallas_call | solution.py:33
  32.7 1.5 %collective-permute-start.10 = (bf16[96,640]{1,0:T(8,128)(2,1)S(1)}, bf16[96,640]{1,0:T(8,128)(2,1)S(1)}, u32[]{:S(2)}, u32[]{:S(2)}) collective-permute-start(bf16[96,640]{1,0:T(8,128)(2,1)S(1)} %get-tuple-element.59), channel_id=1, source_target_pairs={{0,4},{1,5},{2,6},{3,7},{4,0},{5,1},{6,2},{7,3},{8,12},{9,13},{10,... | collective-permute-start | bytes 368648 | tf_op jit(solution)/shard_map/ppermute | solution.py:23
  34.2 1.5 %collective-permute-start.11 = (bf16[96,640]{1,0:T(8,128)(2,1)S(1)}, bf16[96,640]{1,0:T(8,128)(2,1)S(1)}, u32[]{:S(2)}, u32[]{:S(2)}) collective-permute-start(bf16[96,640]{1,0:T(8,128)(2,1)S(1)} %get-tuple-element.60), channel_id=1, source_target_pairs={{0,6},{1,7},{2,4},{3,5},{4,2},{5,3},{6,0},{7,1},{8,14},{9,15},{10,... | collective-permute-start | bytes 368648 | tf_op jit(solution)/shard_map/ppermute | solution.py:23
  35.7 1.9 %collective-permute-done.9.r1 = bf16[96,640]{1,0:T(8,128)(2,1)S(1)} collective-permute-done((bf16[96,640]{1,0:T(8,128)(2,1)S(1)}, bf16[96,640]{1,0:T(8,128)(2,1)S(1)}, u32[]{:S(2)}, u32[]{:S(2)}) %collective-permute-start.9) | collective-permute-done | bytes 122912 | tf_op jit(solution)/shard_map/ppermute | solution.py:23
  38.3 3.1 %collective-permute-done.11.r3 = bf16[96,640]{1,0:T(8,128)(2,1)S(1)} collective-permute-done((bf16[96,640]{1,0:T(8,128)(2,1)S(1)}, bf16[96,640]{1,0:T(8,128)(2,1)S(1)}, u32[]{:S(2)}, u32[]{:S(2)}) %collective-permute-start.11) | collective-permute-done | bytes 122912 | tf_op jit(solution)/shard_map/ppermute | solution.py:23
  44.0 1.3 %step.2 = (f32[32,512]{1,0:T(8,128)S(1)}, bf16[32,512]{1,0:T(8,128)(2,1)S(1)}, bf16[32,512]{1,0:T(8,128)(2,1)S(1)}, bf16[32,512]{1,0:T(8,128)(2,1)S(1)}) custom-call(bf16[32,512]{1,0:T(8,128)(2,1)S(1)} %get-tuple-element.62.u_a, bf16[32,512]{1,0:T(8,128)(2,1)S(1)} %collective-permute-done.12.u_b, bf16[512,1024]{1,0:T(8,128)(2,1)S(1)} %get-tuple-element.53.w0, ...), custom_call_target="tpu_custom_call" | custom-call | tf_op jit(solution)/shard_map/step/pallas_call | solution.py:33
  45.8 1.5 %collective-permute-start.14 = (bf16[32,512]{1,0:T(8,128)(2,1)S(1)}, bf16[32,512]{1,0:T(8,128)(2,1)S(1)}, u32[]{:S(2)}, u32[]{:S(2)}) collective-permute-start(bf16[32,512]{1,0:T(8,128)(2,1)S(1)} %get-tuple-element.65), channel_id=1, source_target_pairs={{0,4},{1,5},{2,6},{3,7},{4,0},{5,1},{6,2},{7,3},{8,12},{9,13},{10,... | collective-permute-start | bytes 98312 | tf_op jit(solution)/shard_map/ppermute | solution.py:23
  47.3 1.5 %collective-permute-start.15 = (bf16[32,512]{1,0:T(8,128)(2,1)S(1)}, bf16[32,512]{1,0:T(8,128)(2,1)S(1)}, u32[]{:S(2)}, u32[]{:S(2)}) collective-permute-start(bf16[32,512]{1,0:T(8,128)(2,1)S(1)} %get-tuple-element.66), channel_id=1, source_target_pairs={{0,6},{1,7},{2,4},{3,5},{4,2},{5,3},{6,0},{7,1},{8,14},{9,15},{10,... | collective-permute-start | bytes 98312 | tf_op jit(solution)/shard_map/ppermute | solution.py:23
  49.7 2.4 %collective-permute-done.15.r3 = bf16[32,512]{1,0:T(8,128)(2,1)S(1)} collective-permute-done((bf16[32,512]{1,0:T(8,128)(2,1)S(1)}, bf16[32,512]{1,0:T(8,128)(2,1)S(1)}, u32[]{:S(2)}, u32[]{:S(2)}) %collective-permute-start.15) | collective-permute-done | bytes 32800 | tf_op jit(solution)/shard_map/ppermute | solution.py:23
  53.7 2.7 %collective-permute-start.18 = (f32[32,128]{1,0:T(8,128)S(1)}, f32[32,128]{1,0:T(8,128)S(1)}, u32[]{:S(2)}, u32[]{:S(2)}) collective-permute-start(f32[32,128]{1,0:T(8,128)S(1)} %totals.1), channel_id=1, source_target_pairs={{0,8},{1,9},{2,10},{3,11},{4,12},{5,13},{6,14},{7,15},{8,0},{9,1},... | collective-permute-start | bytes 49160 | tf_op jit(solution)/shard_map/ppermute | solution.py:23
  56.4 1.3 %step.3 = (f32[32,512]{1,0:T(8,128)S(1)}, bf16[32,640]{1,0:T(8,128)(2,1)S(1)}, bf16[32,640]{1,0:T(8,128)(2,1)S(1)}, bf16[32,640]{1,0:T(8,128)(2,1)S(1)}) custom-call(bf16[32,640]{1,0:T(8,128)(2,1)S(1)} %get-tuple-element.70.u_a.msg_a, bf16[32,640]{1,0:T(8,128)(2,1)S(1)} %collective-permute-done.16.u_b.msg_b, bf16[512,1024]{1,0:T(8,128)(2,1)S(1)} %get-tuple-element.53.w0, ...), custom_call_target="tpu_custom_call" | custom-call | tf_op jit(solution)/shard_map/step/pallas_call | solution.py:33
  58.6 1.5 %collective-permute-start.19 = (bf16[32,640]{1,0:T(8,128)(2,1)S(1)}, bf16[32,640]{1,0:T(8,128)(2,1)S(1)}, u32[]{:S(2)}, u32[]{:S(2)}) collective-permute-start(bf16[32,640]{1,0:T(8,128)(2,1)S(1)} %get-tuple-element.78), channel_id=1, source_target_pairs={{0,2},{1,3},{2,0},{3,1},{4,6},{5,7},{6,4},{7,5},{8,10},{9,11},{10,... | collective-permute-start | bytes 122888 | tf_op jit(solution)/shard_map/ppermute | solution.py:23
  60.6 1.6 %collective-permute-start.21 = (bf16[32,640]{1,0:T(8,128)(2,1)S(1)}, bf16[32,640]{1,0:T(8,128)(2,1)S(1)}, u32[]{:S(2)}, u32[]{:S(2)}) collective-permute-start(bf16[32,640]{1,0:T(8,128)(2,1)S(1)} %get-tuple-element.80), channel_id=1, source_target_pairs={{0,6},{1,7},{2,4},{3,5},{4,2},{5,3},{6,0},{7,1},{8,14},{9,15},{10,... | collective-permute-start | bytes 122888 | tf_op jit(solution)/shard_map/ppermute | solution.py:23
  62.7 1.5 %collective-permute-done.20.r2 = bf16[32,640]{1,0:T(8,128)(2,1)S(1)} collective-permute-done((bf16[32,640]{1,0:T(8,128)(2,1)S(1)}, bf16[32,640]{1,0:T(8,128)(2,1)S(1)}, u32[]{:S(2)}, u32[]{:S(2)}) %collective-permute-start.20) | collective-permute-done | bytes 40992 | tf_op jit(solution)/shard_map/ppermute | solution.py:23
  (51 shorter events, 16.6 us)
Async XLA Ops:
  0.6 18.1 %copy-start.1 = (f32[512]{0:T(512)S(1)}, f32[512]{0:T(512)}, u32[]{:S(2)}) copy-start(f32[512]{0:T(512)} %param.16) | copy-start | bytes 6148
  0.6 22.8 %copy-start = (s32[16,8]{0,1:T(8,128)S(1)}, s32[16,8]{0,1:T(8,128)}, u32[]{:S(2)}) copy-start(s32[16,8]{0,1:T(8,128)} %param.17) | copy-start | bytes 1540
  2.3 16.6 %collective-permute-start.5 = (bf16[512,512]{1,0:T(8,128)(2,1)S(1)}, bf16[512,512]{1,0:T(8,128)(2,1)S(1)}, u32[]{:S(2)}, u32[]{:S(2)}) collective-permute-start(bf16[512,512]{1,0:T(8,128)(2,1)S(1)} %to_part.1.refs_3_), channel_id=1, source_target_pairs={{0,2},{1,3},{2,0},{3,1},{4,6},{5,7},{6,4},{7,5},{8,10},{9,11},{10,... | collective-permute-start | bytes 1572872 | tf_op jit(solution)/shard_map/ppermute | solution.py:23
  5.4 14.1 %collective-permute-start.3 = (bf16[512,512]{1,0:T(8,128)(2,1)S(1)}, bf16[512,512]{1,0:T(8,128)(2,1)S(1)}, u32[]{:S(2)}, u32[]{:S(2)}) collective-permute-start(bf16[512,512]{1,0:T(8,128)(2,1)S(1)} %to_part.1.refs_3_), channel_id=1, source_target_pairs={{0,4},{1,5},{2,6},{3,7},{4,0},{5,1},{6,2},{7,3},{8,12},{9,13},{10,... | collective-permute-start | bytes 1572872 | tf_op jit(solution)/shard_map/ppermute | solution.py:23
  15.0 8.4 %collective-permute-start.2 = (bf16[512,512]{1,0:T(8,128)(2,1)S(1)}, bf16[512,512]{1,0:T(8,128)(2,1)S(1)}, u32[]{:S(2)}, u32[]{:S(2)}) collective-permute-start(bf16[512,512]{1,0:T(8,128)(2,1)S(1)} %get-tuple-element.47.refs_1_), channel_id=1, source_target_pairs={{0,1},{1,0},{2,3},{3,2},{4,5},{5,4},{6,7},{7,6},{8,9},{9,8},{10,11... | collective-permute-start | bytes 1572872 | tf_op jit(solution)/shard_map/ppermute | solution.py:23
  15.1 3.7 %collective-permute-start = (f32[1,512]{1,0:T(1,128)S(1)}, f32[1,512]{1,0:T(1,128)S(1)}, u32[]{:S(2)}, u32[]{:S(2)}) collective-permute-start(f32[1,512]{1,0:T(1,128)S(1)} %get-tuple-element.44.total_a), channel_id=1, source_target_pairs={{0,16},{16,0},{1,17},{17,1},{2,18},{18,2},{3,19},{19,3},{4,20},{20... | collective-permute-start | bytes 6152 | tf_op jit(solution)/shard_map/ppermute | solution.py:23
  18.9 1.9 %collective-permute-start.1 = (f32[64,640]{1,0:T(8,128)S(1)}, f32[64,640]{1,0:T(8,128)S(1)}, u32[]{:S(2)}, u32[]{:S(2)}) collective-permute-start(f32[64,640]{1,0:T(8,128)S(1)} %get-tuple-element.46.msg_a), channel_id=1, source_target_pairs={{0,1},{1,0},{2,3},{3,2},{4,5},{5,4},{6,7},{7,6},{8,9},{9,8},{10,11... | collective-permute-start | bytes 491528 | tf_op jit(solution)/shard_map/ppermute | solution.py:23
  18.9 9.1 %collective-permute-start.6 = (bf16[256,512]{1,0:T(8,128)(2,1)S(1)}, bf16[256,512]{1,0:T(8,128)(2,1)S(1)}, u32[]{:S(2)}, u32[]{:S(2)}) collective-permute-start(bf16[256,512]{1,0:T(8,128)(2,1)S(1)} %slice.13), channel_id=1, source_target_pairs={{0,4},{1,5},{2,6},{3,7},{4,0},{5,1},{6,2},{7,3},{8,12},{9,13},{10,... | collective-permute-start | bytes 786440 | tf_op jit(solution)/shard_map/ppermute | solution.py:23
  19.5 8.6 %collective-permute-start.4 = (bf16[256,512]{1,0:T(8,128)(2,1)S(1)}, bf16[256,512]{1,0:T(8,128)(2,1)S(1)}, u32[]{:S(2)}, u32[]{:S(2)}) collective-permute-start(bf16[256,512]{1,0:T(8,128)(2,1)S(1)} %slice.12), channel_id=1, source_target_pairs={{0,2},{1,3},{2,0},{3,1},{4,6},{5,7},{6,4},{7,5},{8,10},{9,11},{10,... | collective-permute-start | bytes 786440 | tf_op jit(solution)/shard_map/ppermute | solution.py:23
  20.8 8.9 %collective-permute-start.8 = (f32[32,128]{1,0:T(8,128)S(1)}, f32[32,128]{1,0:T(8,128)S(1)}, u32[]{:S(2)}, u32[]{:S(2)}) collective-permute-start(f32[32,128]{1,0:T(8,128)S(1)} %slice_add_fusion), channel_id=1, source_target_pairs={{0,8},{1,9},{2,10},{3,11},{4,12},{5,13},{6,14},{7,15},{8,0},{9,1},... | collective-permute-start | bytes 49160 | tf_op jit(solution)/shard_map/ppermute | solution.py:23
  29.6 1.2 %collective-permute-start.7 = (f32[1,1024]{1,0:T(1,128)S(1)}, f32[1,1024]{1,0:T(1,128)S(1)}, u32[]{:S(2)}, u32[]{:S(2)}) collective-permute-start(f32[1,1024]{1,0:T(1,128)S(1)} %get-tuple-element.50.sums_own), channel_id=1, source_target_pairs={{0,1},{1,0},{2,3},{3,2},{4,5},{5,4},{6,7},{7,6},{8,9},{9,8},{10,11... | collective-permute-start | bytes 12296 | tf_op jit(solution)/shard_map/ppermute | solution.py:23
  32.2 5.5 %collective-permute-start.9 = (bf16[96,640]{1,0:T(8,128)(2,1)S(1)}, bf16[96,640]{1,0:T(8,128)(2,1)S(1)}, u32[]{:S(2)}, u32[]{:S(2)}) collective-permute-start(bf16[96,640]{1,0:T(8,128)(2,1)S(1)} %get-tuple-element.58), channel_id=1, source_target_pairs={{0,2},{1,3},{2,0},{3,1},{4,6},{5,7},{6,4},{7,5},{8,10},{9,11},{10,... | collective-permute-start | bytes 368648 | tf_op jit(solution)/shard_map/ppermute | solution.py:23
  32.7 5.6 %collective-permute-start.10 = (bf16[96,640]{1,0:T(8,128)(2,1)S(1)}, bf16[96,640]{1,0:T(8,128)(2,1)S(1)}, u32[]{:S(2)}, u32[]{:S(2)}) collective-permute-start(bf16[96,640]{1,0:T(8,128)(2,1)S(1)} %get-tuple-element.59), channel_id=1, source_target_pairs={{0,4},{1,5},{2,6},{3,7},{4,0},{5,1},{6,2},{7,3},{8,12},{9,13},{10,... | collective-permute-start | bytes 368648 | tf_op jit(solution)/shard_map/ppermute | solution.py:23
  34.2 7.2 %collective-permute-start.11 = (bf16[96,640]{1,0:T(8,128)(2,1)S(1)}, bf16[96,640]{1,0:T(8,128)(2,1)S(1)}, u32[]{:S(2)}, u32[]{:S(2)}) collective-permute-start(bf16[96,640]{1,0:T(8,128)(2,1)S(1)} %get-tuple-element.60), channel_id=1, source_target_pairs={{0,6},{1,7},{2,4},{3,5},{4,2},{5,3},{6,0},{7,1},{8,14},{9,15},{10,... | collective-permute-start | bytes 368648 | tf_op jit(solution)/shard_map/ppermute | solution.py:23
  42.5 11.1 %collective-permute-start.17 = (f32[32,1024]{1,0:T(8,128)S(1)}, f32[32,1024]{1,0:T(8,128)S(1)}, u32[]{:S(2)}, u32[]{:S(2)}) collective-permute-start(f32[32,1024]{1,0:T(8,128)S(1)} %backward.1.back_a), channel_id=1, source_target_pairs={{0,1},{1,0},{2,3},{3,2},{4,5},{5,4},{6,7},{7,6},{8,9},{9,8},{10,11... | collective-permute-start | bytes 393224 | tf_op jit(solution)/shard_map/ppermute | solution.py:23
  42.6 1.4 %collective-permute-start.12 = (bf16[32,512]{1,0:T(8,128)(2,1)S(1)}, bf16[32,512]{1,0:T(8,128)(2,1)S(1)}, u32[]{:S(2)}, u32[]{:S(2)}) collective-permute-start(bf16[32,512]{1,0:T(8,128)(2,1)S(1)} %get-tuple-element.62.u_a), channel_id=1, source_target_pairs={{0,1},{1,0},{2,3},{3,2},{4,5},{5,4},{6,7},{7,6},{8,9},{9,8},{10,11... | collective-permute-start | bytes 98312 | tf_op jit(solution)/shard_map/ppermute | solution.py:23
  45.3 3.9 %collective-permute-start.13 = (bf16[32,512]{1,0:T(8,128)(2,1)S(1)}, bf16[32,512]{1,0:T(8,128)(2,1)S(1)}, u32[]{:S(2)}, u32[]{:S(2)}) collective-permute-start(bf16[32,512]{1,0:T(8,128)(2,1)S(1)} %get-tuple-element.64), channel_id=1, source_target_pairs={{0,2},{1,3},{2,0},{3,1},{4,6},{5,7},{6,4},{7,5},{8,10},{9,11},{10,... | collective-permute-start | bytes 98312 | tf_op jit(solution)/shard_map/ppermute | solution.py:23
  45.8 3.9 %collective-permute-start.14 = (bf16[32,512]{1,0:T(8,128)(2,1)S(1)}, bf16[32,512]{1,0:T(8,128)(2,1)S(1)}, u32[]{:S(2)}, u32[]{:S(2)}) collective-permute-start(bf16[32,512]{1,0:T(8,128)(2,1)S(1)} %get-tuple-element.65), channel_id=1, source_target_pairs={{0,4},{1,5},{2,6},{3,7},{4,0},{5,1},{6,2},{7,3},{8,12},{9,13},{10,... | collective-permute-start | bytes 98312 | tf_op jit(solution)/shard_map/ppermute | solution.py:23
  47.3 4.8 %collective-permute-start.15 = (bf16[32,512]{1,0:T(8,128)(2,1)S(1)}, bf16[32,512]{1,0:T(8,128)(2,1)S(1)}, u32[]{:S(2)}, u32[]{:S(2)}) collective-permute-start(bf16[32,512]{1,0:T(8,128)(2,1)S(1)} %get-tuple-element.66), channel_id=1, source_target_pairs={{0,6},{1,7},{2,4},{3,5},{4,2},{5,3},{6,0},{7,1},{8,14},{9,15},{10,... | collective-permute-start | bytes 98312 | tf_op jit(solution)/shard_map/ppermute | solution.py:23
  52.4 1.2 %collective-permute-start.16 = (bf16[32,640]{1,0:T(8,128)(2,1)S(1)}, bf16[32,640]{1,0:T(8,128)(2,1)S(1)}, u32[]{:S(2)}, u32[]{:S(2)}) collective-permute-start(bf16[32,640]{1,0:T(8,128)(2,1)S(1)} %get-tuple-element.70.u_a.msg_a), channel_id=1, source_target_pairs={{0,1},{1,0},{2,3},{3,2},{4,5},{5,4},{6,7},{7,6},{8,9},{9,8},{10,11... | collective-permute-start | bytes 122888 | tf_op jit(solution)/shard_map/ppermute | solution.py:23
  53.7 4.9 %collective-permute-start.18 = (f32[32,128]{1,0:T(8,128)S(1)}, f32[32,128]{1,0:T(8,128)S(1)}, u32[]{:S(2)}, u32[]{:S(2)}) collective-permute-start(f32[32,128]{1,0:T(8,128)S(1)} %totals.1), channel_id=1, source_target_pairs={{0,8},{1,9},{2,10},{3,11},{4,12},{5,13},{6,14},{7,15},{8,0},{9,1},... | collective-permute-start | bytes 49160 | tf_op jit(solution)/shard_map/ppermute | solution.py:23
  58.6 4.0 %collective-permute-start.19 = (bf16[32,640]{1,0:T(8,128)(2,1)S(1)}, bf16[32,640]{1,0:T(8,128)(2,1)S(1)}, u32[]{:S(2)}, u32[]{:S(2)}) collective-permute-start(bf16[32,640]{1,0:T(8,128)(2,1)S(1)} %get-tuple-element.78), channel_id=1, source_target_pairs={{0,2},{1,3},{2,0},{3,1},{4,6},{5,7},{6,4},{7,5},{8,10},{9,11},{10,... | collective-permute-start | bytes 122888 | tf_op jit(solution)/shard_map/ppermute | solution.py:23
  60.2 4.0 %collective-permute-start.20 = (bf16[32,640]{1,0:T(8,128)(2,1)S(1)}, bf16[32,640]{1,0:T(8,128)(2,1)S(1)}, u32[]{:S(2)}, u32[]{:S(2)}) collective-permute-start(bf16[32,640]{1,0:T(8,128)(2,1)S(1)} %get-tuple-element.79), channel_id=1, source_target_pairs={{0,4},{1,5},{2,6},{3,7},{4,0},{5,1},{6,2},{7,3},{8,12},{9,13},{10,... | collective-permute-start | bytes 122888 | tf_op jit(solution)/shard_map/ppermute | solution.py:23
  60.6 4.9 %collective-permute-start.21 = (bf16[32,640]{1,0:T(8,128)(2,1)S(1)}, bf16[32,640]{1,0:T(8,128)(2,1)S(1)}, u32[]{:S(2)}, u32[]{:S(2)}) collective-permute-start(bf16[32,640]{1,0:T(8,128)(2,1)S(1)} %get-tuple-element.80), channel_id=1, source_target_pairs={{0,6},{1,7},{2,4},{3,5},{4,2},{5,3},{6,0},{7,1},{8,14},{9,15},{10,... | collective-permute-start | bytes 122888 | tf_op jit(solution)/shard_map/ppermute | solution.py:23
  (3 other events, 11.8 us)

commit v3 on v2

v3 whole, which is shorter than its diff:
```python
import math

import jax
import jax.numpy as jnp
from jax import lax
from jax.experimental import pallas as pl
from jax.experimental.pallas import tpu as pltpu
from jax.sharding import PartitionSpec as P

SOFT_CAP = 10.0
EMIT_SCALE = 2.0**20
F32 = jnp.float32
BF16 = jnp.bfloat16
NT = (((1,), (1,)), ((), ()))
NN = (((1,), (0,)), ((), ()))


def dot(lhs, rhs, dims):
    return lax.dot_general(lhs, rhs, dims, preferred_element_type=F32)


def across(shard, apart, axis="col"):
    return lax.ppermute(shard, axis, [(i, i ^ apart) for i in range(lax.axis_size(axis))])


def call(body, out_shape, name, smem=(), hbm=(), scratch=(), limit=32, aliases=None, micros=0.2):
    def run(*args):
        def space(k):
            if k in smem:
                return pltpu.SMEM
            return pltpu.HBM if k in hbm else pltpu.VMEM

        return pl.pallas_call(
            body,
            out_shape=out_shape,
            in_specs=[pl.BlockSpec(memory_space=space(k)) for k in range(len(args))],
            out_specs=jax.tree.map(lambda s: pl.BlockSpec(memory_space=pltpu.VMEM), out_shape),
            scratch_shapes=scratch,
            input_output_aliases=aliases or {},
            name=name,
            cost_estimate=pl.CostEstimate(
                flops=int(micros * 1e9), bytes_accessed=int(micros * 3e6), transcendentals=0
            ),
            compiler_params=pltpu.CompilerParams(vmem_limit_bytes=limit << 20),
        )(
            *(
                pltpu.with_memory_space_constraint(arg, pltpu.HBM) if k in hbm else arg
                for k, arg in enumerate(args)
            )
        )

    return run


def shape(dims, dtype):
    return jax.ShapeDtypeStruct(dims, dtype)


def capped_exp(values, scale):
    return jnp.exp2((SOFT_CAP / math.log(2.0)) * jnp.tanh(values * (scale / SOFT_CAP)))


def project_kernel(
    emb_hbm, weight_hbm, emit_hbm, from_hbm, top, bottom, emb, emit_w, from_out, weight, from_w, sem
):
    pairs = ((emb_hbm, emb), (weight_hbm, weight), (emit_hbm, emit_w), (from_hbm, from_w))
    copies = [pltpu.make_async_copy(src, dst, sem.at[k]) for k, (src, dst) in enumerate(pairs)]
    for copy in copies:
        copy.start()
    copies[0].wait()
    copies[1].wait()
    half = top.shape[0]
    bottom[...] = dot(emb[half:, :], weight[...], NN).astype(BF16)
    top[...] = dot(emb[:half, :], weight[...], NN).astype(BF16)
    copies[3].wait()
    from_out[...] = dot(emb[...], from_w[...], NN).astype(BF16)
    copies[2].wait()


def emission_kernel(
    tile,
    emb,
    emit_w,
    code,
    logit,
    init_hbm,
    ids_hbm,
    prior_out,
    emit_out,
    msg_out,
    mass_out,
    one_hot,
    init_vec,
    codes,
    sem,
):
    copies = [
        pltpu.make_async_copy(init_hbm, init_vec, sem.at[0]),
        pltpu.make_async_copy(ids_hbm, codes, sem.at[1]),
    ]
    for copy in copies:
        copy.start()
    query = dot(emb[...], emit_w[...], NN).astype(BF16)
    states = emb.shape[0]
    tiles = code.shape[0] // tile
    total = jnp.zeros((8, states), F32)
    for k in range(tiles):
        weights = capped_exp(dot(code[k * tile : (k + 1) * tile, :], query, NT), 3.0)
        total = total + jnp.sum(weights.reshape(tile // 8, 8, states), axis=0)
    for copy in copies:
        copy.wait()
    prior = dot(jnp.broadcast_to(init_vec[...].reshape(1, -1), (8, emb.shape[1])), emb[...], NT)
    p = capped_exp(prior, 2.0)[:1]
    prior_out[...] = p
    steps, batch = codes.shape
    ids = jnp.concatenate([column(codes[t : t + 1, :]) for t in range(steps)], axis=0)
    lanes = lax.broadcasted_iota(jnp.int32, (batch * steps, tile), 1).astype(F32)
    for k in range(tiles):
        hit = lanes == ids - float(k * tile)
        one_hot[:, k * tile : (k + 1) * tile] = jnp.where(hit, 1.0, 0.0).astype(BF16)
    rows = dot(one_hot[...], code[...], NN)
    factor = EMIT_SCALE / jnp.sum(total, axis=0, keepdims=True)
    emit = capped_exp(dot(rows.astype(BF16), query, NT), 3.0) * factor
    emit_out[...] = emit
    restart = jax.nn.sigmoid(logit[...])
    first = p * emit[:batch]
    third = p * emit[2 * batch : 3 * batch]
    msg_out[:batch, :states] = first * (1.0 - restart)
    msg_out[batch:, :states] = third * (1.0 - restart)
    mass = row_sum(first * restart)
    packed = lane_pack([mass, jnp.broadcast_to(row_sum(p), mass.shape)], batch)
    msg_out[:batch, states:] = packed
    msg_out[batch:, states:] = jnp.zeros((batch, 128), F32)
    mass_out[...] = packed


def column(row):
    count = row.shape[1]
    at_row = lax.broadcasted_iota(jnp.int32, (count, count), 0)
    at_lane = lax.broadcasted_iota(jnp.int32, (count, count), 1)
    return row_sum(jnp.where(at_row == at_lane, row.astype(F32), 0.0))


def lane_pack(columns, rows):
    lane = lax.broadcasted_iota(jnp.int32, (rows, 128), 1)
    packed = jnp.zeros((rows, 128), F32)
    for k, column in enumerate(columns):
        packed = jnp.where(lane == k, column, packed)
    return packed


def lane_pick(packed, k):
    lane = lax.broadcasted_iota(jnp.int32, packed.shape, 1)
    return jnp.sum(jnp.where(lane == k, packed, 0.0), axis=1, keepdims=True)


def split(packed):
    high = packed.astype(BF16).astype(F32)
    rest = packed - high
    middle = rest.astype(BF16).astype(F32)
    return (high + pltpu.roll(middle, 32, 1) + pltpu.roll(rest - middle, 64, 1)).astype(BF16)


def joined(parts):
    parts = parts.astype(F32)
    return parts + pltpu.roll(parts, 96, 1) + pltpu.roll(parts, 64, 1)


def row_sum(values):
    return jnp.sum(values, axis=1, keepdims=True)


def weights_kernel(scale, shifts, mask, from_a, from_b, *refs):
    states = from_a.shape[0]
    count = len(shifts)
    blocks, outs = refs[: 2 * count], refs[len(refs) - count - 1 : -1]
    before, sum_out = refs[2 * count : len(refs) - count - 1], refs[-1]
    place = lax.rem(lax.axis_index("col"), mask.shape[0])
    tile = states // 2
    for side, source in ((0, from_a), (1, from_b)):
        rows = slice(side * states, (side + 1) * states)
        sums = before[0][rows, :] if before else jnp.zeros((states, 128), F32)
        for n, (shift, out) in enumerate(zip(shifts, outs)):
            row = lax.axis_index("col") ^ shift
            keep = mask[place ^ side, row].astype(F32)
            for k in range(2):
                block = blocks[2 * n + k]
                weights = capped_exp(dot(source[...], block[...], NT), scale) * keep
                out[rows, k * tile : (k + 1) * tile] = weights.astype(BF16)
                for lane in range(0, tile, 128):
                    sums = sums + weights[:, lane : lane + 128]
        if sum_out.shape[0] == 1:
            sum_out[:, rows] = jnp.sum(sums.T, axis=0, keepdims=True)
        else:
            sum_out[rows, :] = sums


def first_kernel(
    msg_a, msg_b, sums_own, sums_sib, mass, emit, w0, w1, w2, w3, own, s1, s2, s3, inv_out, u_out
):
    states = w0.shape[1]
    batch = mass.shape[0]
    inv_a = 1.0 / (sums_own[:, :states] + sums_sib[:, states:])
    inv_b = 1.0 / (sums_own[:, states:] + sums_sib[:, :states])
    inv_out[...] = inv_a
    u_a = (msg_a[:, :states] * inv_a).astype(BF16)
    u_b = (msg_b[:, :states] * inv_b).astype(BF16)
    u = jnp.concatenate([u_a, u_b], axis=1)
    u_out[...] = u[batch:]
    u = u[:batch]
    own[...] = dot(u, w0[...], NN)
    parts = split(mass[...])
    last = emit[3 * batch :].astype(BF16)
    for w, s in ((w1, s1), (w2, s2), (w3, s3)):
        s[:batch, :states] = dot(u, w[...], NN).astype(BF16)
        s[batch:, :states] = last
        s[:batch, states:] = parts
        s[batch:, states:] = jnp.zeros((batch, 128), BF16)


def combine_first_kernel(own, r1, r2, r3, mass, emit, prior, logit, inv, f_out, u_out, part_out):
    batch, states = own.shape
    summed = own[...]
    total = mass[...]
    for r in (r1, r2, r3):
        summed = summed + r[:batch, :states].astype(F32)
        total = total + joined(r[:batch, states:])
    norm = lane_pick(total, 1)
    ratio = lane_pick(total, 0) / norm
    restart = jax.nn.sigmoid(logit[...])
    f = emit[batch : 2 * batch] * (summed + prior[...] * ratio)
    f_out[...] = f
    u_out[...] = (f * (1.0 - restart) * inv[...]).astype(BF16)
    part_out[...] = lane_pack([norm, row_sum(f * restart)], batch)


def backward_kernel(emit, r1, r2, r3, w0, w1, w2, w3, out):
    states = w0.shape[1]
    batch = out.shape[0]
    acc = dot(emit[3 * batch :].astype(BF16), w0[...], NT)
    for r, w in ((r1, w1), (r2, w2), (r3, w3)):
        acc = acc + dot(r[batch:, :states], w[...], NT)
    out[...] = acc


def second_kernel(u_a, u_b, u_chain, w0, w1, w2, w3, own, s1, s2, s3):
    u = jnp.concatenate([jnp.concatenate([u_a[...], u_b[...]], axis=1), u_chain[...]], axis=0)
    own[...] = dot(u, w0[...], NN)
    for w, s in ((w1, s1), (w2, s2), (w3, s3)):
        s[...] = dot(u, w[...], NN).astype(BF16)


def third_kernel(u_a, u_b, w0, w1, w2, w3, own, s1, s2, s3):
    states = w0.shape[1]
    u = jnp.concatenate([u_a[:, :states], u_b[:, :states]], axis=1)
    own[...] = dot(u, w0[...], NN)
    for w, s in ((w1, s1), (w2, s2), (w3, s3)):
        s[:, :states] = dot(u, w[...], NN).astype(BF16)


def combine_kernel(
    own,
    r1,
    r2,
    r3,
    emit,
    prior,
    logit,
    inv,
    f1,
    part,
    back_a,
    back_b,
    lengths,
    g_out,
    chain_out,
    msg_out,
    pack_out,
):
    batch, states = f1.shape
    summed = own[...]
    for r in (r1, r2, r3):
        summed = summed + r[...].astype(F32)
    restart = jax.nn.sigmoid(logit[...])
    p = prior[...]
    e = emit[...]
    length = column(lengths[...])
    g = e[2 * batch : 3 * batch] * summed[:batch]
    g_out[...] = g
    chain = e[3 * batch :] * summed[batch:]
    chain_out[...] = chain
    u = (g * (1.0 - restart) * inv[...]).astype(BF16)
    msg_out[:, :states] = u
    last = row_sum(u.astype(F32) * (back_a[:, :states] + back_b[:, states:]))
    h2 = p * e[2 * batch : 3 * batch]
    main = jnp.where(length == 1, p * e[:batch], jnp.where(length == 2, f1[...], g))
    side = jnp.where(length == 3, h2, chain)
    packed = lane_pack(
        [
            lane_pick(part[...], 1),
            row_sum(g * restart),
            row_sum(h2 * restart),
            jnp.where(length < 4, row_sum(main), last),
            jnp.where(length >= 3, row_sum(side), 0.0),
            jnp.where(length >= 4, row_sum(p * e[3 * batch :]), 0.0),
        ],
        batch,
    )
    msg_out[:, states:] = split(packed)
    pack_out[...] = packed


def clean(packed):
    lane = lax.broadcasted_iota(jnp.int32, packed.shape, 1)
    return jnp.where(lane < 6, packed, 0.0)


def totals_kernel(msg_sib, pack, other_a, other_b, out):
    states = msg_sib.shape[1] - 128
    here = pack[...] + joined(msg_sib[:, states:])
    out[...] = clean(here + (other_a[...] + other_b[...]))


def attach_kernel(total, s1, s2, s3, o1, o2, o3):
    states = s1.shape[1] - 128
    parts = split(total[...])
    for out in (o1, o2, o3):
        out[:, states:] = parts


def attach_sum_kernel(msg_sib, pack, other_a, other_b, s1, s2, s3, total, o1, o2, o3):
    totals_kernel(msg_sib, pack, other_a, other_b, total)
    attach_kernel(total, s1, s2, s3, o1, o2, o3)


def finish_kernel(
    own, r1, r2, r3, totals, emit, prior, f1, g2, chain, part, lengths, scaled_out, like_out
):
    batch, states = own.shape
    summed = own[...]
    total = totals[...]
    for r in (r1, r2, r3):
        summed = summed + r[:, :states].astype(F32)
        total = total + joined(r[:, states:])
    p = prior[...]
    e = emit[...]
    length = column(lengths[...])
    z = lane_pick(part[...], 0)
    mass1 = lane_pick(total, 0) / z
    mass2 = (lane_pick(total, 1) + mass1 * lane_pick(total, 2)) / z
    full = lane_pick(total, 3) + mass1 * lane_pick(total, 4) + mass2 * lane_pick(total, 5)
    f2 = g2[...] + mass1 * (p * e[2 * batch : 3 * batch])
    f3 = e[3 * batch :] * (summed + p * mass2) + mass1 * chain[...]
    values = jnp.where(
        length == 1,
        p * e[:batch],
        jnp.where(length == 2, f1[...], jnp.where(length == 3, f2, f3)),
    )
    scaled_out[...] = values / full
    like = jnp.log(full) - jnp.log(z) - length * math.log(EMIT_SCALE)
    diagonal = lax.broadcasted_iota(jnp.int32, (batch, batch), 0) == lax.broadcasted_iota(
        jnp.int32, (batch, batch), 1
    )
    like_out[...] = jnp.sum(jnp.where(diagonal, like, 0.0), axis=0, keepdims=True)


def per_device(
    state_emb,
    from_weight,
    to_weight,
    emit_weight,
    code_emb,
    init_vec,
    restart_logit,
    block_mask,
    codes,
    lengths,
):
    states, width = state_emb.shape
    vocab = code_emb.shape[0]
    cluster = block_mask.shape[1]
    batch, steps = codes.shape
    cols = lax.axis_size("col")
    logit = restart_logit.reshape(1, states)
    length_row = lengths.reshape(1, batch)
    square = shape((states, width), BF16)
    plane = shape((batch, states), F32)
    lanes = shape((batch, 128), F32)
    half_plane = shape((batch, states), BF16)
    message = shape((batch, states + 128), BF16)

    half = states // 2
    half_block = shape((half, width), BF16)
    top, bottom, emb, emit_w, from_own = call(
        project_kernel,
        (half_block, half_block) + (square,) * 3,
        "to_part",
        hbm=(0, 1, 2, 3),
        micros=6,
        scratch=[
            pltpu.VMEM((width, width), BF16),
            pltpu.VMEM((width, width), BF16),
            pltpu.SemaphoreType.DMA((4,)),
        ],
    )(state_emb, to_weight, emit_weight, from_weight)
    y_bottom = across(bottom, 2)
    z_top = across(top, 4)
    y_top = across(top, 2)
    z_bottom = across(bottom, 4)

    from_sib = across(from_own, 1)
    prior, emit, msg, mass_own = call(
        lambda *refs: emission_kernel(512, *refs),
        (
            shape((1, states), F32),
            shape((batch * steps, states), F32),
            shape((2 * batch, states + 128), F32),
            lanes,
        ),
        "emission",
        hbm=(4, 5),
        micros=0.5,
        scratch=[
            pltpu.VMEM((batch * steps, vocab), BF16),
            pltpu.VMEM((width,), BF16),
            pltpu.VMEM((steps, batch), jnp.int32),
            pltpu.SemaphoreType.DMA((2,)),
        ],
    )(emb, emit_w, code_emb, logit, init_vec, codes.T)

    scale = 2.0 / math.sqrt(width)
    sums_shape = shape((2 * states, 128), F32)
    wt_shape = shape((2 * states, states), BF16)
    w0, sums0 = call(
        lambda *refs: weights_kernel(scale, (0,), *refs),
        (wt_shape, sums_shape),
        "weights",
        (0,),
        micros=1.5,
    )(block_mask.T, from_own, from_sib, top, bottom)
    d_top = across(z_top, 2)
    d_bottom = across(y_bottom, 4)
    y_top, z_bottom, sums0 = lax.optimization_barrier((y_top, z_bottom, sums0))
    msg, mass_own, *_ = lax.optimization_barrier((msg, mass_own, y_top, z_bottom))
    msg_sib = across(msg, 1)
    w1, w2, sums1 = call(
        lambda *refs: weights_kernel(scale, (2, 4), *refs),
        (wt_shape, wt_shape, sums_shape),
        "weights",
        (0,),
        micros=2,
    )(block_mask.T, from_own, from_sib, y_top, y_bottom, z_top, z_bottom, sums0)
    mass = mass_own + msg_sib[:batch, states:]
    apart = cluster
    while apart < cols:
        mass = mass + across(mass, apart)
        apart *= 2
    w3, row_sums = call(
        lambda *refs: weights_kernel(scale, (6,), *refs),
        (wt_shape, shape((1, 2 * states), F32)),
        "weights",
        (0,),
        micros=1.5,
    )(block_mask.T, from_own, from_sib, d_top, d_bottom, sums1)
    wts = (w0, w1, w2, w3)
    row_sums_sib = across(row_sums, 1)

    out = call(
        first_kernel,
        (plane,)
        + (shape((2 * batch, states + 128), BF16),) * 3
        + (shape((1, states), F32), shape((batch, 2 * states), BF16)),
        "first",
        micros=1,
    )(msg, msg_sib, row_sums, row_sums_sib, mass, emit, *wts)
    own, sends, inv, u_chain = out[0], out[1:4], out[4], out[5]
    received = [across(s, 2 * (k + 1)) for k, s in enumerate(sends)]
    f1, u1, part = call(combine_first_kernel, (plane, half_plane, lanes), "combine_first")(
        own, *received, mass, emit, prior, logit, inv
    )
    u1_sib = across(u1, 1)
    held, _ = lax.optimization_barrier((tuple(received), u1))
    back = call(backward_kernel, shape((batch, 2 * states), F32), "backward", micros=1)(emit, *held, *wts)
    own, *sends = call(
        second_kernel,
        (shape((2 * batch, states), F32),) + (shape((2 * batch, states), BF16),) * 3,
        "second",
        micros=1,
    )(u1, u1_sib, u_chain, *wts)
    back_sib = across(back, 1)
    received = [across(s, 2 * (k + 1)) for k, s in enumerate(sends)]
    g2, chain, msg2, pack = call(combine_kernel, (plane, plane, message, lanes), "combine")(
        own,
        *received,
        emit,
        prior,
        logit,
        inv,
        f1,
        part,
        back,
        back_sib,
        length_row,
    )
    msg2_sib = across(msg2, 1)
    others = [across(pack, cluster), across(pack, cluster + 1)]
    own, *sends = call(third_kernel, (plane,) + (message,) * 3, "third", micros=1)(
        msg2, msg2_sib, *wts
    )
    if cols == 2 * cluster:
        totals, *sends = call(
            attach_sum_kernel, (lanes,) + (message,) * 3, "attach", aliases={4: 1, 5: 2, 6: 3}
        )(msg2_sib, pack, *others, *sends)
    else:
        totals = call(totals_kernel, lanes, "totals")(msg2_sib, pack, *others)
        apart = 2 * cluster
        while apart < cols:
            totals = totals + across(totals, apart)
            apart *= 2
        sends = call(attach_kernel, (message,) * 3, "attach", aliases={1: 0, 2: 1, 3: 2})(
            totals, *sends
        )
    received = [across(s, 2 * (k + 1)) for k, s in enumerate(sends)]
    scaled, like = call(finish_kernel, (plane, shape((1, batch), F32)), "finish")(
        own, *received, totals, emit, prior, f1, g2, chain, part, length_row
    )
    return scaled, like.reshape(batch)


def solution(mesh):
    in_specs = (P("col", None), P(), P(), P(), P(), P(), P("col"), P(), P("grp", None), P("grp"))
    out_specs = (P("grp", "col"), P("grp"))
    return jax.shard_map(
        per_device, mesh=mesh, in_specs=in_specs, out_specs=out_specs, check_vma=False
    )
```

time: 66.5 us -> 62.4 us (0.938)
  Pallas kernels: 19.9 us -> 17.1 us
  local copies, waits for them, and re-layouts: 1.41 us -> 0.02 us
  starting transfers between devices: 24.5 us -> 25.5 us
  waiting for transfers between devices: 19.6 us -> 18.9 us
    pallas_call x15 -> x13, Pallas kernels: 19.9 us -> 17.1 us  [run(): pl.pallas_call(body, out_shape=out_shape, in_specs=[pl.BlockSpec(memory_s...]
    unnamed x10 -> x8, local copies, waits for them, and re-layouts: 1.37 us -> 0.02 us
    ppermute x22 -> x24, starting transfers between devices: 24.5 us -> 25.5 us  [across(): lax.ppermute(shard, axis, [(i, i ^ apart) for i in range(lax.axis_size(ax...]
    ppermute x22 -> x24, waiting for transfers between devices: 19.6 us -> 18.9 us  [across(): lax.ppermute(shard, axis, [(i, i ^ apart) for i in range(lax.axis_size(ax...]
  transfers between devices with their start and end apart: 22 -> 24, of which waited for: 15 -> 16; matrix products, arithmetic and copies ran while one was open for 0% -> 0% of each run, Pallas kernels for 22% -> 20%
where the time goes in v3:
time: 62.4 us; the launch traced here: 62.3 us
  starting transfers between devices  25.5 us (41%)
  waiting for transfers between devices  18.9 us (30%)
  Pallas kernels  17.1 us (27%)
  between operations  0.76 us (1%)
    ppermute x24, starting transfers between devices, across(): lax.ppermute(shard, axis, [(i, i ^ apart) for i in range(lax.axis_size(ax...  25.5 us
    ppermute x24, waiting for transfers between devices, across(): lax.ppermute(shard, axis, [(i, i ^ apart) for i in range(lax.axis_size(ax...  18.9 us
    pallas_call x13, Pallas kernels, run(): pl.pallas_call(body, out_shape=out_shape, in_specs=[pl.BlockSpec(memory_s...  17.1 us
  transfers between devices with their start and end apart: 24, of which 16 were waited for; matrix products, arithmetic and copies ran while one was open for 0% of the time, Pallas kernels for 20%

profile of v3, /device:TPU:0, one launch (start us, length us, event | category | flops | bytes accessed | tf_op | source)
XLA Modules:
  0.0 62.3 jit_solution(4534642634391063854)
XLA Ops:
  0.7 2.3 %to_part.1 = (bf16[256,512]{1,0:T(8,128)(2,1)S(1)}, bf16[256,512]{1,0:T(8,128)(2,1)S(1)}, bf16[512,512]{1,0:T(8,128)(2,1)S(1)}, bf16[512,512]{1,0:T(8,128)(2,1)S(1)}, bf16[512,512]{1,0:T(8,128)(2,1)S(1)}) custom-call(bf16[512,512]{1,0:T(8,128)(2,1)} %emb_hbm.1, bf16[512,512]{1,0:T(8,128)(2,1)} %weight_hbm.1, bf16[512,512]{1,0:T(8,128)(2,1)} %emit_hbm.1, ...), custom_call_target="tpu_custom_call" | custom-call | flops 6000000000 | bytes 18000000 | tf_op jit(solution)/shard_map/to_part/pallas_call | solution.py:33
  3.5 2.6 %collective-permute-start.4 = (bf16[256,512]{1,0:T(8,128)(2,1)S(1)}, bf16[256,512]{1,0:T(8,128)(2,1)S(1)}, u32[]{:S(2)}, u32[]{:S(2)}) collective-permute-start(bf16[256,512]{1,0:T(8,128)(2,1)S(1)} %get-tuple-element.57.refs_3_), channel_id=1, source_target_pairs={{0,4},{1,5},{2,6},{3,7},{4,0},{5,1},{6,2},{7,3},{8,12},{9,13},{10,... | collective-permute-start | bytes 786440 | tf_op jit(solution)/shard_map/ppermute | solution.py:23
  6.1 1.6 %collective-permute-start.6 = (bf16[256,512]{1,0:T(8,128)(2,1)S(1)}, bf16[256,512]{1,0:T(8,128)(2,1)S(1)}, u32[]{:S(2)}, u32[]{:S(2)}) collective-permute-start(bf16[256,512]{1,0:T(8,128)(2,1)S(1)} %get-tuple-element.58.refs_4_), channel_id=1, source_target_pairs={{0,2},{1,3},{2,0},{3,1},{4,6},{5,7},{6,4},{7,5},{8,10},{9,11},{10,... | collective-permute-start | bytes 786440 | tf_op jit(solution)/shard_map/ppermute | solution.py:23
  8.2 4.1 %emission.1 = (f32[1,512]{1,0:T(1,128)S(1)}, f32[128,512]{1,0:T(8,128)S(1)}, f32[64,640]{1,0:T(8,128)S(1)}, f32[32,128]{1,0:T(8,128)S(1)}) custom-call(bf16[512,512]{1,0:T(8,128)(2,1)S(1)} %get-tuple-element.53.refs_0_, bf16[512,512]{1,0:T(8,128)(2,1)S(1)} %get-tuple-element.54.refs_1_, bf16[4096,512]{1,0:T(8,128)(2,1)S(1)} %copy-done, ...), custom_call_target="tpu_custom_call" | custom-call | flops 500000000 | bytes 1500000 | tf_op jit(solution)/shard_map/emission/pallas_call | solution.py:33
  13.3 1.9 %collective-permute-start.5 = (bf16[256,512]{1,0:T(8,128)(2,1)S(1)}, bf16[256,512]{1,0:T(8,128)(2,1)S(1)}, u32[]{:S(2)}, u32[]{:S(2)}) collective-permute-start(bf16[256,512]{1,0:T(8,128)(2,1)S(1)} %collective-permute-done.4.refs_5_), channel_id=1, source_target_pairs={{0,2},{1,3},{2,0},{3,1},{4,6},{5,7},{6,4},{7,5},{8,10},{9,11},{10,... | collective-permute-start | bytes 786440 | tf_op jit(solution)/shard_map/ppermute | solution.py:23
  15.3 1.5 %collective-permute-start.7 = (bf16[256,512]{1,0:T(8,128)(2,1)S(1)}, bf16[256,512]{1,0:T(8,128)(2,1)S(1)}, u32[]{:S(2)}, u32[]{:S(2)}) collective-permute-start(bf16[256,512]{1,0:T(8,128)(2,1)S(1)} %collective-permute-done.6.refs_4_), channel_id=1, source_target_pairs={{0,4},{1,5},{2,6},{3,7},{4,0},{5,1},{6,2},{7,3},{8,12},{9,13},{10,... | collective-permute-start | bytes 786440 | tf_op jit(solution)/shard_map/ppermute | solution.py:23
  16.7 1.6 %weights.3 = (bf16[1024,512]{1,0:T(8,128)(2,1)S(1)}, f32[1024,128]{1,0:T(8,128)S(1)}) custom-call(s32[8,16]{1,0:T(8,128)S(1)} %bitcast.10, bf16[512,512]{1,0:T(8,128)(2,1)S(1)} %get-tuple-element.59.refs_1_, bf16[512,512]{1,0:T(8,128)(2,1)S(1)} %collective-permute-done.2.refs_2_, bf16[256,512]{1,0:T(8,128)(2,1)S(1)} %get-tuple-element.57.refs_3_, ...), custom_call_target="tpu_custom_call" | custom-call | flops 1500000000 | bytes 4500000 | tf_op jit(solution)/shard_map/weights/pallas_call | solution.py:33
  18.3 2.6 %collective-permute-done.refs_3_ = bf16[256,512]{1,0:T(8,128)(2,1)S(1)} collective-permute-done((bf16[256,512]{1,0:T(8,128)(2,1)S(1)}, bf16[256,512]{1,0:T(8,128)(2,1)S(1)}, u32[]{:S(2)}, u32[]{:S(2)}) %collective-permute-start) | collective-permute-done | bytes 262176 | tf_op jit(solution)/shard_map/ppermute | solution.py:23
  20.9 2.3 %weights.4 = (bf16[1024,512]{1,0:T(8,128)(2,1)S(1)}, bf16[1024,512]{1,0:T(8,128)(2,1)S(1)}, f32[1024,128]{1,0:T(8,128)S(1)}) custom-call(s32[8,16]{1,0:T(8,128)S(1)} %bitcast.11, bf16[512,512]{1,0:T(8,128)(2,1)S(1)} %get-tuple-element.59.refs_1_, bf16[512,512]{1,0:T(8,128)(2,1)S(1)} %collective-permute-done.2.refs_2_, ...), custom_call_target="tpu_custom_call" | custom-call | flops 2000000000 | bytes 6000000 | tf_op jit(solution)/shard_map/weights/pallas_call | solution.py:33
  23.2 2.7 %collective-permute-start.9 = (f32[32,128]{1,0:T(8,128)S(1)}, f32[32,128]{1,0:T(8,128)S(1)}, u32[]{:S(2)}, u32[]{:S(2)}) collective-permute-start(f32[32,128]{1,0:T(8,128)S(1)} %slice_add_fusion), channel_id=1, source_target_pairs={{0,8},{1,9},{2,10},{3,11},{4,12},{5,13},{6,14},{7,15},{8,0},{9,1},... | collective-permute-start | bytes 49160 | tf_op jit(solution)/shard_map/ppermute | solution.py:23
  25.9 1.7 %weights.5 = (bf16[1024,512]{1,0:T(8,128)(2,1)S(1)}, f32[1,1024]{1,0:T(1,128)S(1)}) custom-call(s32[8,16]{1,0:T(8,128)S(1)} %bitcast.12, bf16[512,512]{1,0:T(8,128)(2,1)S(1)} %get-tuple-element.59.refs_1_, bf16[512,512]{1,0:T(8,128)(2,1)S(1)} %collective-permute-done.2.refs_2_, bf16[256,512]{1,0:T(8,128)(2,1)S(1)} %collective-permute-done.5.refs_3_, ...), custom_call_target="tpu_custom_call" | custom-call | flops 1500000000 | bytes 4500000 | tf_op jit(solution)/shard_map/weights/pallas_call | solution.py:33
  29.6 1.6 %collective-permute-start.10 = (bf16[64,640]{1,0:T(8,128)(2,1)S(1)}, bf16[64,640]{1,0:T(8,128)(2,1)S(1)}, u32[]{:S(2)}, u32[]{:S(2)}) collective-permute-start(bf16[64,640]{1,0:T(8,128)(2,1)S(1)} %get-tuple-element.74), channel_id=1, source_target_pairs={{0,2},{1,3},{2,0},{3,1},{4,6},{5,7},{6,4},{7,5},{8,10},{9,11},{10,... | collective-permute-start | bytes 245768 | tf_op jit(solution)/shard_map/ppermute | solution.py:23
  31.6 1.5 %collective-permute-start.12 = (bf16[64,640]{1,0:T(8,128)(2,1)S(1)}, bf16[64,640]{1,0:T(8,128)(2,1)S(1)}, u32[]{:S(2)}, u32[]{:S(2)}) collective-permute-start(bf16[64,640]{1,0:T(8,128)(2,1)S(1)} %get-tuple-element.76), channel_id=1, source_target_pairs={{0,6},{1,7},{2,4},{3,5},{4,2},{5,3},{6,0},{7,1},{8,14},{9,15},{10,... | collective-permute-start | bytes 245768 | tf_op jit(solution)/shard_map/ppermute | solution.py:23
  34.2 2.1 %collective-permute-done.11.r2 = bf16[64,640]{1,0:T(8,128)(2,1)S(1)} collective-permute-done((bf16[64,640]{1,0:T(8,128)(2,1)S(1)}, bf16[64,640]{1,0:T(8,128)(2,1)S(1)}, u32[]{:S(2)}, u32[]{:S(2)}) %collective-permute-start.11) | collective-permute-done | bytes 81952 | tf_op jit(solution)/shard_map/ppermute | solution.py:23
  37.6 1.3 %backward.1.back_a = f32[32,1024]{1,0:T(8,128)S(1)} custom-call(f32[128,512]{1,0:T(8,128)S(1)} %get-tuple-element.68.emit, bf16[64,640]{1,0:T(8,128)(2,1)S(1)} %collective-permute-done.10.r1, bf16[64,640]{1,0:T(8,128)(2,1)S(1)} %collective-permute-done.11.r2, bf16[64,640]{1,0:T(8,128)(2,1)S(1)} %collective-permute-done.12.r3, ...), custom_call_target="tpu_custom_call" | custom-call | flops 1000000000 | bytes 3000000 | tf_op jit(solution)/shard_map/backward/pallas_call | solution.py:33
  40.2 1.5 %collective-permute-start.14 = (bf16[64,512]{1,0:T(8,128)(2,1)S(1)}, bf16[64,512]{1,0:T(8,128)(2,1)S(1)}, u32[]{:S(2)}, u32[]{:S(2)}) collective-permute-start(bf16[64,512]{1,0:T(8,128)(2,1)S(1)} %get-tuple-element.82), channel_id=1, source_target_pairs={{0,2},{1,3},{2,0},{3,1},{4,6},{5,7},{6,4},{7,5},{8,10},{9,11},{10,... | collective-permute-start | bytes 196616 | tf_op jit(solution)/shard_map/ppermute | solution.py:23
  42.3 1.5 %collective-permute-start.16 = (bf16[64,512]{1,0:T(8,128)(2,1)S(1)}, bf16[64,512]{1,0:T(8,128)(2,1)S(1)}, u32[]{:S(2)}, u32[]{:S(2)}) collective-permute-start(bf16[64,512]{1,0:T(8,128)(2,1)S(1)} %get-tuple-element.84), channel_id=1, source_target_pairs={{0,6},{1,7},{2,4},{3,5},{4,2},{5,3},{6,0},{7,1},{8,14},{9,15},{10,... | collective-permute-start | bytes 196616 | tf_op jit(solution)/shard_map/ppermute | solution.py:23
  44.6 1.9 %collective-permute-done.15.r2 = bf16[64,512]{1,0:T(8,128)(2,1)S(1)} collective-permute-done((bf16[64,512]{1,0:T(8,128)(2,1)S(1)}, bf16[64,512]{1,0:T(8,128)(2,1)S(1)}, u32[]{:S(2)}, u32[]{:S(2)}) %collective-permute-start.15) | collective-permute-done | bytes 65568 | tf_op jit(solution)/shard_map/ppermute | solution.py:23
  47.8 2.5 %collective-permute-start.19 = (f32[32,128]{1,0:T(8,128)S(1)}, f32[32,128]{1,0:T(8,128)S(1)}, u32[]{:S(2)}, u32[]{:S(2)}) collective-permute-start(f32[32,128]{1,0:T(8,128)S(1)} %get-tuple-element.92.pack), channel_id=1, source_target_pairs={{0,8},{1,9},{2,10},{3,11},{4,12},{5,13},{6,14},{7,15},{8,0},{9,1},... | collective-permute-start | bytes 49160 | tf_op jit(solution)/shard_map/ppermute | solution.py:23
  52.5 1.8 %collective-permute-done.20.other_b = f32[32,128]{1,0:T(8,128)S(1)} collective-permute-done((f32[32,128]{1,0:T(8,128)S(1)}, f32[32,128]{1,0:T(8,128)S(1)}, u32[]{:S(2)}, u32[]{:S(2)}) %collective-permute-start.20) | collective-permute-done | bytes 16416 | tf_op jit(solution)/shard_map/ppermute | solution.py:23
  54.5 1.3 %collective-permute-start.21 = (bf16[32,640]{1,0:T(8,128)(2,1)S(1)}, bf16[32,640]{1,0:T(8,128)(2,1)S(1)}, u32[]{:S(2)}, u32[]{:S(2)}) collective-permute-start(bf16[32,640]{1,0:T(8,128)(2,1)S(1)} %get-tuple-element.96), channel_id=1, source_target_pairs={{0,2},{1,3},{2,0},{3,1},{4,6},{5,7},{6,4},{7,5},{8,10},{9,11},{10,... | collective-permute-start | bytes 122888 | tf_op jit(solution)/shard_map/ppermute | solution.py:23
  56.6 1.4 %collective-permute-start.23 = (bf16[32,640]{1,0:T(8,128)(2,1)S(1)}, bf16[32,640]{1,0:T(8,128)(2,1)S(1)}, u32[]{:S(2)}, u32[]{:S(2)}) collective-permute-start(bf16[32,640]{1,0:T(8,128)(2,1)S(1)} %get-tuple-element.98), channel_id=1, source_target_pairs={{0,6},{1,7},{2,4},{3,5},{4,2},{5,3},{6,0},{7,1},{8,14},{9,15},{10,... | collective-permute-start | bytes 122888 | tf_op jit(solution)/shard_map/ppermute | solution.py:23
  58.5 1.5 %collective-permute-done.22.r2 = bf16[32,640]{1,0:T(8,128)(2,1)S(1)} collective-permute-done((bf16[32,640]{1,0:T(8,128)(2,1)S(1)}, bf16[32,640]{1,0:T(8,128)(2,1)S(1)}, u32[]{:S(2)}, u32[]{:S(2)}) %collective-permute-start.22) | collective-permute-done | bytes 40992 | tf_op jit(solution)/shard_map/ppermute | solution.py:23
  60.0 1.4 %collective-permute-done.23.r3 = bf16[32,640]{1,0:T(8,128)(2,1)S(1)} collective-permute-done((bf16[32,640]{1,0:T(8,128)(2,1)S(1)}, bf16[32,640]{1,0:T(8,128)(2,1)S(1)}, u32[]{:S(2)}, u32[]{:S(2)}) %collective-permute-start.23) | collective-permute-done | bytes 40992 | tf_op jit(solution)/shard_map/ppermute | solution.py:23
  (47 shorter events, 15.5 us)
Async XLA Ops:
  2.9 13.8 %collective-permute-start.2 = (bf16[512,512]{1,0:T(8,128)(2,1)S(1)}, bf16[512,512]{1,0:T(8,128)(2,1)S(1)}, u32[]{:S(2)}, u32[]{:S(2)}) collective-permute-start(bf16[512,512]{1,0:T(8,128)(2,1)S(1)} %get-tuple-element.59.refs_1_), channel_id=1, source_target_pairs={{0,1},{1,0},{2,3},{3,2},{4,5},{5,4},{6,7},{7,6},{8,9},{9,8},{10,11... | collective-permute-start | bytes 1572872 | tf_op jit(solution)/shard_map/ppermute | solution.py:23
  3.5 9.8 %collective-permute-start.4 = (bf16[256,512]{1,0:T(8,128)(2,1)S(1)}, bf16[256,512]{1,0:T(8,128)(2,1)S(1)}, u32[]{:S(2)}, u32[]{:S(2)}) collective-permute-start(bf16[256,512]{1,0:T(8,128)(2,1)S(1)} %get-tuple-element.57.refs_3_), channel_id=1, source_target_pairs={{0,4},{1,5},{2,6},{3,7},{4,0},{5,1},{6,2},{7,3},{8,12},{9,13},{10,... | collective-permute-start | bytes 786440 | tf_op jit(solution)/shard_map/ppermute | solution.py:23
  6.1 9.2 %collective-permute-start.6 = (bf16[256,512]{1,0:T(8,128)(2,1)S(1)}, bf16[256,512]{1,0:T(8,128)(2,1)S(1)}, u32[]{:S(2)}, u32[]{:S(2)}) collective-permute-start(bf16[256,512]{1,0:T(8,128)(2,1)S(1)} %get-tuple-element.58.refs_4_), channel_id=1, source_target_pairs={{0,2},{1,3},{2,0},{3,1},{4,6},{5,7},{6,4},{7,5},{8,10},{9,11},{10,... | collective-permute-start | bytes 786440 | tf_op jit(solution)/shard_map/ppermute | solution.py:23
  7.7 13.2 %collective-permute-start = (bf16[256,512]{1,0:T(8,128)(2,1)S(1)}, bf16[256,512]{1,0:T(8,128)(2,1)S(1)}, u32[]{:S(2)}, u32[]{:S(2)}) collective-permute-start(bf16[256,512]{1,0:T(8,128)(2,1)S(1)} %get-tuple-element.57.refs_3_), channel_id=1, source_target_pairs={{0,2},{1,3},{2,0},{3,1},{4,6},{5,7},{6,4},{7,5},{8,10},{9,11},{10,... | collective-permute-start | bytes 786440 | tf_op jit(solution)/shard_map/ppermute | solution.py:23
  8.1 12.7 %collective-permute-start.1 = (bf16[256,512]{1,0:T(8,128)(2,1)S(1)}, bf16[256,512]{1,0:T(8,128)(2,1)S(1)}, u32[]{:S(2)}, u32[]{:S(2)}) collective-permute-start(bf16[256,512]{1,0:T(8,128)(2,1)S(1)} %get-tuple-element.58.refs_4_), channel_id=1, source_target_pairs={{0,4},{1,5},{2,6},{3,7},{4,0},{5,1},{6,2},{7,3},{8,12},{9,13},{10,... | collective-permute-start | bytes 786440 | tf_op jit(solution)/shard_map/ppermute | solution.py:23
  13.3 12.6 %collective-permute-start.5 = (bf16[256,512]{1,0:T(8,128)(2,1)S(1)}, bf16[256,512]{1,0:T(8,128)(2,1)S(1)}, u32[]{:S(2)}, u32[]{:S(2)}) collective-permute-start(bf16[256,512]{1,0:T(8,128)(2,1)S(1)} %collective-permute-done.4.refs_5_), channel_id=1, source_target_pairs={{0,2},{1,3},{2,0},{3,1},{4,6},{5,7},{6,4},{7,5},{8,10},{9,11},{10,... | collective-permute-start | bytes 786440 | tf_op jit(solution)/shard_map/ppermute | solution.py:23
  15.3 10.6 %collective-permute-start.7 = (bf16[256,512]{1,0:T(8,128)(2,1)S(1)}, bf16[256,512]{1,0:T(8,128)(2,1)S(1)}, u32[]{:S(2)}, u32[]{:S(2)}) collective-permute-start(bf16[256,512]{1,0:T(8,128)(2,1)S(1)} %collective-permute-done.6.refs_4_), channel_id=1, source_target_pairs={{0,4},{1,5},{2,6},{3,7},{4,0},{5,1},{6,2},{7,3},{8,12},{9,13},{10,... | collective-permute-start | bytes 786440 | tf_op jit(solution)/shard_map/ppermute | solution.py:23
  20.9 2.3 %collective-permute-start.3 = (f32[64,640]{1,0:T(8,128)S(1)}, f32[64,640]{1,0:T(8,128)S(1)}, u32[]{:S(2)}, u32[]{:S(2)}) collective-permute-start(f32[64,640]{1,0:T(8,128)S(1)} %get-tuple-element.63.msg_a), channel_id=1, source_target_pairs={{0,1},{1,0},{2,3},{3,2},{4,5},{5,4},{6,7},{7,6},{8,9},{9,8},{10,11... | collective-permute-start | bytes 491528 | tf_op jit(solution)/shard_map/ppermute | solution.py:23
  23.2 4.7 %collective-permute-start.9 = (f32[32,128]{1,0:T(8,128)S(1)}, f32[32,128]{1,0:T(8,128)S(1)}, u32[]{:S(2)}, u32[]{:S(2)}) collective-permute-start(f32[32,128]{1,0:T(8,128)S(1)} %slice_add_fusion), channel_id=1, source_target_pairs={{0,8},{1,9},{2,10},{3,11},{4,12},{5,13},{6,14},{7,15},{8,0},{9,1},... | collective-permute-start | bytes 49160 | tf_op jit(solution)/shard_map/ppermute | solution.py:23
  27.5 1.2 %collective-permute-start.8 = (f32[1,1024]{1,0:T(1,128)S(1)}, f32[1,1024]{1,0:T(1,128)S(1)}, u32[]{:S(2)}, u32[]{:S(2)}) collective-permute-start(f32[1,1024]{1,0:T(1,128)S(1)} %get-tuple-element.66.sums_own), channel_id=1, source_target_pairs={{0,1},{1,0},{2,3},{3,2},{4,5},{5,4},{6,7},{7,6},{8,9},{9,8},{10,11... | collective-permute-start | bytes 12296 | tf_op jit(solution)/shard_map/ppermute | solution.py:23
  29.6 4.6 %collective-permute-start.10 = (bf16[64,640]{1,0:T(8,128)(2,1)S(1)}, bf16[64,640]{1,0:T(8,128)(2,1)S(1)}, u32[]{:S(2)}, u32[]{:S(2)}) collective-permute-start(bf16[64,640]{1,0:T(8,128)(2,1)S(1)} %get-tuple-element.74), channel_id=1, source_target_pairs={{0,2},{1,3},{2,0},{3,1},{4,6},{5,7},{6,4},{7,5},{8,10},{9,11},{10,... | collective-permute-start | bytes 245768 | tf_op jit(solution)/shard_map/ppermute | solution.py:23
  31.1 5.2 %collective-permute-start.11 = (bf16[64,640]{1,0:T(8,128)(2,1)S(1)}, bf16[64,640]{1,0:T(8,128)(2,1)S(1)}, u32[]{:S(2)}, u32[]{:S(2)}) collective-permute-start(bf16[64,640]{1,0:T(8,128)(2,1)S(1)} %get-tuple-element.75), channel_id=1, source_target_pairs={{0,4},{1,5},{2,6},{3,7},{4,0},{5,1},{6,2},{7,3},{8,12},{9,13},{10,... | collective-permute-start | bytes 245768 | tf_op jit(solution)/shard_map/ppermute | solution.py:23
  31.6 5.7 %collective-permute-start.12 = (bf16[64,640]{1,0:T(8,128)(2,1)S(1)}, bf16[64,640]{1,0:T(8,128)(2,1)S(1)}, u32[]{:S(2)}, u32[]{:S(2)}) collective-permute-start(bf16[64,640]{1,0:T(8,128)(2,1)S(1)} %get-tuple-element.76), channel_id=1, source_target_pairs={{0,6},{1,7},{2,4},{3,5},{4,2},{5,3},{6,0},{7,1},{8,14},{9,15},{10,... | collective-permute-start | bytes 245768 | tf_op jit(solution)/shard_map/ppermute | solution.py:23
  37.5 1.9 %collective-permute-start.13 = (bf16[32,512]{1,0:T(8,128)(2,1)S(1)}, bf16[32,512]{1,0:T(8,128)(2,1)S(1)}, u32[]{:S(2)}, u32[]{:S(2)}) collective-permute-start(bf16[32,512]{1,0:T(8,128)(2,1)S(1)} %get-tuple-element.79.u_a), channel_id=1, source_target_pairs={{0,1},{1,0},{2,3},{3,2},{4,5},{5,4},{6,7},{7,6},{8,9},{9,8},{10,11... | collective-permute-start | bytes 98312 | tf_op jit(solution)/shard_map/ppermute | solution.py:23
  38.9 8.6 %collective-permute-start.17 = (f32[32,1024]{1,0:T(8,128)S(1)}, f32[32,1024]{1,0:T(8,128)S(1)}, u32[]{:S(2)}, u32[]{:S(2)}) collective-permute-start(f32[32,1024]{1,0:T(8,128)S(1)} %backward.1.back_a), channel_id=1, source_target_pairs={{0,1},{1,0},{2,3},{3,2},{4,5},{5,4},{6,7},{7,6},{8,9},{9,8},{10,11... | collective-permute-start | bytes 393224 | tf_op jit(solution)/shard_map/ppermute | solution.py:23
  40.2 4.3 %collective-permute-start.14 = (bf16[64,512]{1,0:T(8,128)(2,1)S(1)}, bf16[64,512]{1,0:T(8,128)(2,1)S(1)}, u32[]{:S(2)}, u32[]{:S(2)}) collective-permute-start(bf16[64,512]{1,0:T(8,128)(2,1)S(1)} %get-tuple-element.82), channel_id=1, source_target_pairs={{0,2},{1,3},{2,0},{3,1},{4,6},{5,7},{6,4},{7,5},{8,10},{9,11},{10,... | collective-permute-start | bytes 196616 | tf_op jit(solution)/shard_map/ppermute | solution.py:23
  41.7 4.8 %collective-permute-start.15 = (bf16[64,512]{1,0:T(8,128)(2,1)S(1)}, bf16[64,512]{1,0:T(8,128)(2,1)S(1)}, u32[]{:S(2)}, u32[]{:S(2)}) collective-permute-start(bf16[64,512]{1,0:T(8,128)(2,1)S(1)} %get-tuple-element.83), channel_id=1, source_target_pairs={{0,4},{1,5},{2,6},{3,7},{4,0},{5,1},{6,2},{7,3},{8,12},{9,13},{10,... | collective-permute-start | bytes 196616 | tf_op jit(solution)/shard_map/ppermute | solution.py:23
  42.3 5.2 %collective-permute-start.16 = (bf16[64,512]{1,0:T(8,128)(2,1)S(1)}, bf16[64,512]{1,0:T(8,128)(2,1)S(1)}, u32[]{:S(2)}, u32[]{:S(2)}) collective-permute-start(bf16[64,512]{1,0:T(8,128)(2,1)S(1)} %get-tuple-element.84), channel_id=1, source_target_pairs={{0,6},{1,7},{2,4},{3,5},{4,2},{5,3},{6,0},{7,1},{8,14},{9,15},{10,... | collective-permute-start | bytes 196616 | tf_op jit(solution)/shard_map/ppermute | solution.py:23
  47.7 2.8 %collective-permute-start.18 = (bf16[32,640]{1,0:T(8,128)(2,1)S(1)}, bf16[32,640]{1,0:T(8,128)(2,1)S(1)}, u32[]{:S(2)}, u32[]{:S(2)}) collective-permute-start(bf16[32,640]{1,0:T(8,128)(2,1)S(1)} %get-tuple-element.90.u_a), channel_id=1, source_target_pairs={{0,1},{1,0},{2,3},{3,2},{4,5},{5,4},{6,7},{7,6},{8,9},{9,8},{10,11... | collective-permute-start | bytes 122888 | tf_op jit(solution)/shard_map/ppermute | solution.py:23
  47.8 4.7 %collective-permute-start.19 = (f32[32,128]{1,0:T(8,128)S(1)}, f32[32,128]{1,0:T(8,128)S(1)}, u32[]{:S(2)}, u32[]{:S(2)}) collective-permute-start(f32[32,128]{1,0:T(8,128)S(1)} %get-tuple-element.92.pack), channel_id=1, source_target_pairs={{0,8},{1,9},{2,10},{3,11},{4,12},{5,13},{6,14},{7,15},{8,0},{9,1},... | collective-permute-start | bytes 49160 | tf_op jit(solution)/shard_map/ppermute | solution.py:23
  50.3 4.1 %collective-permute-start.20 = (f32[32,128]{1,0:T(8,128)S(1)}, f32[32,128]{1,0:T(8,128)S(1)}, u32[]{:S(2)}, u32[]{:S(2)}) collective-permute-start(f32[32,128]{1,0:T(8,128)S(1)} %get-tuple-element.92.pack), channel_id=1, source_target_pairs={{0,9},{1,8},{2,11},{3,10},{4,13},{5,12},{6,15},{7,14},{8,1},{9,0},... | collective-permute-start | bytes 49160 | tf_op jit(solution)/shard_map/ppermute | solution.py:23
  54.5 4.0 %collective-permute-start.21 = (bf16[32,640]{1,0:T(8,128)(2,1)S(1)}, bf16[32,640]{1,0:T(8,128)(2,1)S(1)}, u32[]{:S(2)}, u32[]{:S(2)}) collective-permute-start(bf16[32,640]{1,0:T(8,128)(2,1)S(1)} %get-tuple-element.96), channel_id=1, source_target_pairs={{0,2},{1,3},{2,0},{3,1},{4,6},{5,7},{6,4},{7,5},{8,10},{9,11},{10,... | collective-permute-start | bytes 122888 | tf_op jit(solution)/shard_map/ppermute | solution.py:23
  55.8 4.2 %collective-permute-start.22 = (bf16[32,640]{1,0:T(8,128)(2,1)S(1)}, bf16[32,640]{1,0:T(8,128)(2,1)S(1)}, u32[]{:S(2)}, u32[]{:S(2)}) collective-permute-start(bf16[32,640]{1,0:T(8,128)(2,1)S(1)} %get-tuple-element.97), channel_id=1, source_target_pairs={{0,4},{1,5},{2,6},{3,7},{4,0},{5,1},{6,2},{7,3},{8,12},{9,13},{10,... | collective-permute-start | bytes 122888 | tf_op jit(solution)/shard_map/ppermute | solution.py:23
  56.6 4.9 %collective-permute-start.23 = (bf16[32,640]{1,0:T(8,128)(2,1)S(1)}, bf16[32,640]{1,0:T(8,128)(2,1)S(1)}, u32[]{:S(2)}, u32[]{:S(2)}) collective-permute-start(bf16[32,640]{1,0:T(8,128)(2,1)S(1)} %get-tuple-element.98), channel_id=1, source_target_pairs={{0,6},{1,7},{2,4},{3,5},{4,2},{5,3},{6,0},{7,1},{8,14},{9,15},{10,... | collective-permute-start | bytes 122888 | tf_op jit(solution)/shard_map/ppermute | solution.py:23
  (4 other events, 38.9 us)

commit v4 on v3

--- a/solution.py
+++ b/solution.py
@@ -9,6 +9,7 @@
 
 SOFT_CAP = 10.0
 EMIT_SCALE = 2.0**20
+SHIFTS = (6, 2, 4)
 F32 = jnp.float32
 BF16 = jnp.bfloat16
 NT = (((1,), (1,)), ((), ()))
@@ -23,11 +24,9 @@
     return lax.ppermute(shard, axis, [(i, i ^ apart) for i in range(lax.axis_size(axis))])
 
 
-def call(body, out_shape, name, smem=(), hbm=(), scratch=(), limit=32, aliases=None, micros=0.2):
+def call(body, out_shape, name, hbm=(), scratch=(), limit=32, aliases=None, micros=0.2):
     def run(*args):
         def space(k):
-            if k in smem:
-                return pltpu.SMEM
             return pltpu.HBM if k in hbm else pltpu.VMEM
 
         return pl.pallas_call(
@@ -60,26 +59,22 @@
     return jnp.exp2((SOFT_CAP / math.log(2.0)) * jnp.tanh(values * (scale / SOFT_CAP)))
 
 
-def project_kernel(
-    emb_hbm, weight_hbm, emit_hbm, from_hbm, top, bottom, emb, emit_w, from_out, weight, from_w, sem
-):
-    pairs = ((emb_hbm, emb), (weight_hbm, weight), (emit_hbm, emit_w), (from_hbm, from_w))
-    copies = [pltpu.make_async_copy(src, dst, sem.at[k]) for k, (src, dst) in enumerate(pairs)]
+def halves_kernel(emb_hbm, top, bottom, sem):
+    half = top.shape[0]
+    copies = [
+        pltpu.make_async_copy(emb_hbm.at[pl.ds(half, half)], bottom, sem.at[0]),
+        pltpu.make_async_copy(emb_hbm.at[pl.ds(0, half)], top, sem.at[1]),
+    ]
     for copy in copies:
         copy.start()
-    copies[0].wait()
-    copies[1].wait()
-    half = top.shape[0]
-    bottom[...] = dot(emb[half:, :], weight[...], NN).astype(BF16)
-    top[...] = dot(emb[:half, :], weight[...], NN).astype(BF16)
-    copies[3].wait()
-    from_out[...] = dot(emb[...], from_w[...], NN).astype(BF16)
-    copies[2].wait()
+    for copy in copies:
+        copy.wait()
 
 
 def emission_kernel(
     tile,
-    emb,
+    top,
+    bottom,
     emit_w,
     code,
     logit,
@@ -100,7 +95,8 @@
     ]
     for copy in copies:
         copy.start()
-    query = dot(emb[...], emit_w[...], NN).astype(BF16)
+    emb = jnp.concatenate([top[...], bottom[...]], axis=0)
+    query = dot(emb, emit_w[...], NN).astype(BF16)
     states = emb.shape[0]
     tiles = code.shape[0] // tile
     total = jnp.zeros((8, states), F32)
@@ -109,7 +105,7 @@
         total = total + jnp.sum(weights.reshape(tile // 8, 8, states), axis=0)
     for copy in copies:
         copy.wait()
-    prior = dot(jnp.broadcast_to(init_vec[...].reshape(1, -1), (8, emb.shape[1])), emb[...], NT)
+    prior = dot(jnp.broadcast_to(init_vec[...].reshape(1, -1), (8, emb.shape[1])), emb, NT)
     p = capped_exp(prior, 2.0)[:1]
     prior_out[...] = p
     steps, batch = codes.shape
@@ -170,22 +166,34 @@
     return jnp.sum(values, axis=1, keepdims=True)
 
 
-def weights_kernel(scale, shifts, mask, from_a, from_b, *refs):
+def sources_kernel(scale, mask, to_w, top, bottom, sib, from_w, from_a, from_b, out, sum_out):
+    half = top.shape[0]
+    from_a[:half, :] = dot(top[...], from_w[...], NN).astype(BF16)
+    from_a[half:, :] = dot(bottom[...], from_w[...], NN).astype(BF16)
+    from_b[...] = dot(sib[...], from_w[...], NN).astype(BF16)
+    weights_kernel(scale, (0,), mask, to_w, from_a, from_b, top, bottom, out, sum_out)
+
+
+def weights_kernel(scale, shifts, mask, to_w, from_a, from_b, *refs):
     states = from_a.shape[0]
     count = len(shifts)
     blocks, outs = refs[: 2 * count], refs[len(refs) - count - 1 : -1]
     before, sum_out = refs[2 * count : len(refs) - count - 1], refs[-1]
     place = lax.rem(lax.axis_index("col"), mask.shape[0])
+    at_place = lax.broadcasted_iota(jnp.int32, mask.shape, 0)
+    at_col = lax.broadcasted_iota(jnp.int32, mask.shape, 1)
     tile = states // 2
+    targets = [dot(block[...], to_w[...], NN).astype(BF16) for block in blocks]
     for side, source in ((0, from_a), (1, from_b)):
         rows = slice(side * states, (side + 1) * states)
         sums = before[0][rows, :] if before else jnp.zeros((states, 128), F32)
         for n, (shift, out) in enumerate(zip(shifts, outs)):
             row = lax.axis_index("col") ^ shift
-            keep = mask[place ^ side, row].astype(F32)
+            keep = (at_place == place ^ side) & (at_col == row)
+            keep = jnp.sum(jnp.where(keep, mask[...], 0).astype(F32), axis=(0, 1), keepdims=True)
             for k in range(2):
-                block = blocks[2 * n + k]
-                weights = capped_exp(dot(source[...], block[...], NT), scale) * keep
+                target = targets[2 * n + k]
+                weights = capped_exp(dot(source[...], target, NT), scale) * keep
                 out[rows, k * tile : (k + 1) * tile] = weights.astype(BF16)
                 for lane in range(0, tile, 128):
                     sums = sums + weights[:, lane : lane + 128]
@@ -391,24 +399,20 @@
 
     half = states // 2
     half_block = shape((half, width), BF16)
-    top, bottom, emb, emit_w, from_own = call(
-        project_kernel,
-        (half_block, half_block) + (square,) * 3,
-        "to_part",
-        hbm=(0, 1, 2, 3),
+    top, bottom = call(
+        halves_kernel,
+        (half_block, half_block),
+        "halves",
+        hbm=(0,),
         micros=6,
-        scratch=[
-            pltpu.VMEM((width, width), BF16),
-            pltpu.VMEM((width, width), BF16),
-            pltpu.SemaphoreType.DMA((4,)),
-        ],
-    )(state_emb, to_weight, emit_weight, from_weight)
+        scratch=[pltpu.SemaphoreType.DMA((2,))],
+    )(state_emb)
     y_bottom = across(bottom, 2)
     z_top = across(top, 4)
     y_top = across(top, 2)
     z_bottom = across(bottom, 4)
 
-    from_sib = across(from_own, 1)
+    sib = across(state_emb, 1)
     prior, emit, msg, mass_own = call(
         lambda *refs: emission_kernel(512, *refs),
         (
@@ -418,7 +422,7 @@
             lanes,
         ),
         "emission",
-        hbm=(4, 5),
+        hbm=(5, 6),
         micros=0.5,
         scratch=[
             pltpu.VMEM((batch * steps, vocab), BF16),
@@ -426,18 +430,17 @@
             pltpu.VMEM((steps, batch), jnp.int32),
             pltpu.SemaphoreType.DMA((2,)),
         ],
-    )(emb, emit_w, code_emb, logit, init_vec, codes.T)
+    )(top, bottom, emit_weight, code_emb, logit, init_vec, codes.T)
 
     scale = 2.0 / math.sqrt(width)
     sums_shape = shape((2 * states, 128), F32)
     wt_shape = shape((2 * states, states), BF16)
-    w0, sums0 = call(
-        lambda *refs: weights_kernel(scale, (0,), *refs),
-        (wt_shape, sums_shape),
-        "weights",
-        (0,),
+    from_own, from_sib, w0, sums0 = call(
+        lambda *refs: sources_kernel(scale, *refs),
+        (square, square, wt_shape, sums_shape),
+        "sources",
         micros=1.5,
-    )(block_mask.T, from_own, from_sib, top, bottom)
+    )(block_mask.T, to_weight, top, bottom, sib, from_weight)
     d_top = across(z_top, 2)
     d_bottom = across(y_bottom, 4)
     y_top, z_bottom, sums0 = lax.optimization_barrier((y_top, z_bottom, sums0))
@@ -447,9 +450,8 @@
         lambda *refs: weights_kernel(scale, (2, 4), *refs),
         (wt_shape, wt_shape, sums_shape),
         "weights",
-        (0,),
         micros=2,
-    )(block_mask.T, from_own, from_sib, y_top, y_bottom, z_top, z_bottom, sums0)
+    )(block_mask.T, to_weight, from_own, from_sib, y_top, y_bottom, z_top, z_bottom, sums0)
     mass = mass_own + msg_sib[:batch, states:]
     apart = cluster
     while apart < cols:
@@ -459,10 +461,9 @@
         lambda *refs: weights_kernel(scale, (6,), *refs),
         (wt_shape, shape((1, 2 * states), F32)),
         "weights",
-        (0,),
         micros=1.5,
-    )(block_mask.T, from_own, from_sib, d_top, d_bottom, sums1)
-    wts = (w0, w1, w2, w3)
+    )(block_mask.T, to_weight, from_own, from_sib, d_top, d_bottom, sums1)
+    wts = (w0, w3, w1, w2)
     row_sums_sib = across(row_sums, 1)
 
     out = call(
@@ -474,7 +475,7 @@
         micros=1,
     )(msg, msg_sib, row_sums, row_sums_sib, mass, emit, *wts)
     own, sends, inv, u_chain = out[0], out[1:4], out[4], out[5]
-    received = [across(s, 2 * (k + 1)) for k, s in enumerate(sends)]
+    received = [across(s, shift) for shift, s in zip(SHIFTS, sends)]
     f1, u1, part = call(combine_first_kernel, (plane, half_plane, lanes), "combine_first")(
         own, *received, mass, emit, prior, logit, inv
     )
@@ -488,7 +489,7 @@
         micros=1,
     )(u1, u1_sib, u_chain, *wts)
     back_sib = across(back, 1)
-    received = [across(s, 2 * (k + 1)) for k, s in enumerate(sends)]
+    received = [across(s, shift) for shift, s in zip(SHIFTS, sends)]
     g2, chain, msg2, pack = call(combine_kernel, (plane, plane, message, lanes), "combine")(
         own,
         *received,
@@ -520,7 +521,7 @@
         sends = call(attach_kernel, (message,) * 3, "attach", aliases={1: 0, 2: 1, 3: 2})(
             totals, *sends
         )
-    received = [across(s, 2 * (k + 1)) for k, s in enumerate(sends)]
+    received = [across(s, shift) for shift, s in zip(SHIFTS, sends)]
     scaled, like = call(finish_kernel, (plane, shape((1, batch), F32)), "finish")(
         own, *received, totals, emit, prior, f1, g2, chain, part, length_row
     )

time: 62.4 us -> 60 us (0.962)
  Pallas kernels: 17.1 us -> 15.9 us
  waiting for transfers between devices: 18.9 us -> 17.7 us
    pallas_call x13, Pallas kernels: 17.1 us -> 15.9 us  [run(): pl.pallas_call(body, out_shape=out_shape, in_specs=[pl.BlockSpec(memory_s...]
    ppermute x24, waiting for transfers between devices: 18.9 us -> 17.7 us  [across(): lax.ppermute(shard, axis, [(i, i ^ apart) for i in range(lax.axis_size(ax...]
  transfers between devices with their start and end apart: 24 -> 24, of which waited for: 16 -> 16; matrix products, arithmetic and copies ran while one was open for 0% -> 0% of each run, Pallas kernels for 20% -> 23%
where the time goes in v4:
time: 60 us; the launch traced here: 59.8 us
  starting transfers between devices  25.4 us (42%)
  waiting for transfers between devices  17.7 us (30%)
  Pallas kernels  15.9 us (26%)
  between operations  0.79 us (1%)
    ppermute x24, starting transfers between devices, across(): lax.ppermute(shard, axis, [(i, i ^ apart) for i in range(lax.axis_size(ax...  25.4 us
    ppermute x24, waiting for transfers between devices, across(): lax.ppermute(shard, axis, [(i, i ^ apart) for i in range(lax.axis_size(ax...  17.7 us
    pallas_call x13, Pallas kernels, run(): pl.pallas_call(body, out_shape=out_shape, in_specs=[pl.BlockSpec(memory_s...  15.9 us
  transfers between devices with their start and end apart: 24, of which 16 were waited for; matrix products, arithmetic and copies ran while one was open for 0% of the time, Pallas kernels for 23%

profile of v4, /device:TPU:0, one launch (start us, length us, event | category | flops | bytes accessed | tf_op | source)
XLA Modules:
  0.0 59.8 jit_solution(13505246685971989322)
XLA Ops:
  1.2 1.3 %halves.1 = (bf16[256,512]{1,0:T(8,128)(2,1)S(1)}, bf16[256,512]{1,0:T(8,128)(2,1)S(1)}) custom-call(bf16[512,512]{1,0:T(8,128)(2,1)} %emb_hbm.1), custom_call_target="tpu_custom_call" | custom-call | flops 6000000000 | bytes 18000000 | tf_op jit(solution)/shard_map/halves/pallas_call | solution.py:32
  2.5 2.5 %collective-permute-start.4 = (bf16[256,512]{1,0:T(8,128)(2,1)S(1)}, bf16[256,512]{1,0:T(8,128)(2,1)S(1)}, u32[]{:S(2)}, u32[]{:S(2)}) collective-permute-start(bf16[256,512]{1,0:T(8,128)(2,1)S(1)} %get-tuple-element.52.refs_0_.refs_2_), channel_id=1, source_target_pairs={{0,4},{1,5},{2,6},{3,7},{4,0},{5,1},{6,2},{7,3},{8,12},{9,13},{10,... | collective-permute-start | bytes 786440 | tf_op jit(solution)/shard_map/ppermute | solution.py:24
  5.1 1.5 %collective-permute-start.6 = (bf16[256,512]{1,0:T(8,128)(2,1)S(1)}, bf16[256,512]{1,0:T(8,128)(2,1)S(1)}, u32[]{:S(2)}, u32[]{:S(2)}) collective-permute-start(bf16[256,512]{1,0:T(8,128)(2,1)S(1)} %get-tuple-element.53.refs_1_.refs_3_), channel_id=1, source_target_pairs={{0,2},{1,3},{2,0},{3,1},{4,6},{5,7},{6,4},{7,5},{8,10},{9,11},{10,... | collective-permute-start | bytes 786440 | tf_op jit(solution)/shard_map/ppermute | solution.py:24
  7.2 4.1 %emission.1 = (f32[1,512]{1,0:T(1,128)S(1)}, f32[128,512]{1,0:T(8,128)S(1)}, f32[64,640]{1,0:T(8,128)S(1)}, f32[32,128]{1,0:T(8,128)S(1)}) custom-call(bf16[256,512]{1,0:T(8,128)(2,1)S(1)} %get-tuple-element.52.refs_0_.refs_2_, bf16[256,512]{1,0:T(8,128)(2,1)S(1)} %get-tuple-element.53.refs_1_.refs_3_, bf16[512,512]{1,0:T(8,128)(2,1)S(1)} %copy-done.1, ...), custom_call_target="tpu_custom_call" | custom-call | flops 500000000 | bytes 1500000 | tf_op jit(solution)/shard_map/emission/pallas_call | solution.py:32
  12.2 2.0 %collective-permute-start.5 = (bf16[256,512]{1,0:T(8,128)(2,1)S(1)}, bf16[256,512]{1,0:T(8,128)(2,1)S(1)}, u32[]{:S(2)}, u32[]{:S(2)}) collective-permute-start(bf16[256,512]{1,0:T(8,128)(2,1)S(1)} %collective-permute-done.4.refs_6_), channel_id=1, source_target_pairs={{0,2},{1,3},{2,0},{3,1},{4,6},{5,7},{6,4},{7,5},{8,10},{9,11},{10,... | collective-permute-start | bytes 786440 | tf_op jit(solution)/shard_map/ppermute | solution.py:24
  14.2 1.6 %collective-permute-start.7 = (bf16[256,512]{1,0:T(8,128)(2,1)S(1)}, bf16[256,512]{1,0:T(8,128)(2,1)S(1)}, u32[]{:S(2)}, u32[]{:S(2)}) collective-permute-start(bf16[256,512]{1,0:T(8,128)(2,1)S(1)} %collective-permute-done.6.refs_5_), channel_id=1, source_target_pairs={{0,4},{1,5},{2,6},{3,7},{4,0},{5,1},{6,2},{7,3},{8,12},{9,13},{10,... | collective-permute-start | bytes 786440 | tf_op jit(solution)/shard_map/ppermute | solution.py:24
  15.8 1.7 %sources.1 = (bf16[512,512]{1,0:T(8,128)(2,1)S(1)}, bf16[512,512]{1,0:T(8,128)(2,1)S(1)}, bf16[1024,512]{1,0:T(8,128)(2,1)S(1)}, f32[1024,128]{1,0:T(8,128)S(1)}) custom-call(s32[8,16]{1,0:T(8,128)S(1)} %bitcast.10, bf16[512,512]{1,0:T(8,128)(2,1)S(1)} %copy-done.5, bf16[256,512]{1,0:T(8,128)(2,1)S(1)} %get-tuple-element.52.refs_0_.refs_2_, ...), custom_call_target="tpu_custom_call" | custom-call | flops 1500000000 | bytes 4500000 | tf_op jit(solution)/shard_map/sources/pallas_call | solution.py:32
  17.5 2.3 %collective-permute-done.refs_4_ = bf16[256,512]{1,0:T(8,128)(2,1)S(1)} collective-permute-done((bf16[256,512]{1,0:T(8,128)(2,1)S(1)}, bf16[256,512]{1,0:T(8,128)(2,1)S(1)}, u32[]{:S(2)}, u32[]{:S(2)}) %collective-permute-start) | collective-permute-done | bytes 262176 | tf_op jit(solution)/shard_map/ppermute | solution.py:24
  19.8 2.3 %weights.2 = (bf16[1024,512]{1,0:T(8,128)(2,1)S(1)}, bf16[1024,512]{1,0:T(8,128)(2,1)S(1)}, f32[1024,128]{1,0:T(8,128)S(1)}) custom-call(s32[8,16]{1,0:T(8,128)S(1)} %bitcast.11, bf16[512,512]{1,0:T(8,128)(2,1)S(1)} %copy-done.5, bf16[512,512]{1,0:T(8,128)(2,1)S(1)} %get-tuple-element.60.refs_2_, bf16[512,512]{1,0:T(8,128)(2,1)S(1)} %get-tuple-element.61.refs_3_, ...), custom_call_target="tpu_custom_call" | custom-call | flops 2000000000 | bytes 6000000 | tf_op jit(solution)/shard_map/weights/pallas_call | solution.py:32
  22.1 2.7 %collective-permute-start.9 = (f32[32,128]{1,0:T(8,128)S(1)}, f32[32,128]{1,0:T(8,128)S(1)}, u32[]{:S(2)}, u32[]{:S(2)}) collective-permute-start(f32[32,128]{1,0:T(8,128)S(1)} %slice_add_fusion), channel_id=1, source_target_pairs={{0,8},{1,9},{2,10},{3,11},{4,12},{5,13},{6,14},{7,15},{8,0},{9,1},... | collective-permute-start | bytes 49160 | tf_op jit(solution)/shard_map/ppermute | solution.py:24
  25.0 1.3 %weights.3 = (bf16[1024,512]{1,0:T(8,128)(2,1)S(1)}, f32[1,1024]{1,0:T(1,128)S(1)}) custom-call(s32[8,16]{1,0:T(8,128)S(1)} %bitcast.12, bf16[512,512]{1,0:T(8,128)(2,1)S(1)} %copy-done.5, bf16[512,512]{1,0:T(8,128)(2,1)S(1)} %get-tuple-element.60.refs_2_, bf16[512,512]{1,0:T(8,128)(2,1)S(1)} %get-tuple-element.61.refs_3_, ...), custom_call_target="tpu_custom_call" | custom-call | flops 1500000000 | bytes 4500000 | tf_op jit(solution)/shard_map/weights/pallas_call | solution.py:32
  28.3 1.4 %collective-permute-start.10 = (bf16[64,640]{1,0:T(8,128)(2,1)S(1)}, bf16[64,640]{1,0:T(8,128)(2,1)S(1)}, u32[]{:S(2)}, u32[]{:S(2)}) collective-permute-start(bf16[64,640]{1,0:T(8,128)(2,1)S(1)} %get-tuple-element.72), channel_id=1, source_target_pairs={{0,6},{1,7},{2,4},{3,5},{4,2},{5,3},{6,0},{7,1},{8,14},{9,15},{10,... | collective-permute-start | bytes 245768 | tf_op jit(solution)/shard_map/ppermute | solution.py:24
  30.1 1.7 %collective-permute-start.12 = (bf16[64,640]{1,0:T(8,128)(2,1)S(1)}, bf16[64,640]{1,0:T(8,128)(2,1)S(1)}, u32[]{:S(2)}, u32[]{:S(2)}) collective-permute-start(bf16[64,640]{1,0:T(8,128)(2,1)S(1)} %get-tuple-element.74), channel_id=1, source_target_pairs={{0,4},{1,5},{2,6},{3,7},{4,0},{5,1},{6,2},{7,3},{8,12},{9,13},{10,... | collective-permute-start | bytes 245768 | tf_op jit(solution)/shard_map/ppermute | solution.py:24
  31.8 2.3 %collective-permute-done.10.r1 = bf16[64,640]{1,0:T(8,128)(2,1)S(1)} collective-permute-done((bf16[64,640]{1,0:T(8,128)(2,1)S(1)}, bf16[64,640]{1,0:T(8,128)(2,1)S(1)}, u32[]{:S(2)}, u32[]{:S(2)}) %collective-permute-start.10) | collective-permute-done | bytes 81952 | tf_op jit(solution)/shard_map/ppermute | solution.py:24
  34.1 1.4 %collective-permute-done.11.r2 = bf16[64,640]{1,0:T(8,128)(2,1)S(1)} collective-permute-done((bf16[64,640]{1,0:T(8,128)(2,1)S(1)}, bf16[64,640]{1,0:T(8,128)(2,1)S(1)}, u32[]{:S(2)}, u32[]{:S(2)}) %collective-permute-start.11) | collective-permute-done | bytes 81952 | tf_op jit(solution)/shard_map/ppermute | solution.py:24
  35.8 1.3 %backward.1.back_a = f32[32,1024]{1,0:T(8,128)S(1)} custom-call(f32[128,512]{1,0:T(8,128)S(1)} %get-tuple-element.66.emit, bf16[64,640]{1,0:T(8,128)(2,1)S(1)} %collective-permute-done.10.r1, bf16[64,640]{1,0:T(8,128)(2,1)S(1)} %collective-permute-done.11.r2, bf16[64,640]{1,0:T(8,128)(2,1)S(1)} %collective-permute-done.12.r3, ...), custom_call_target="tpu_custom_call" | custom-call | flops 1000000000 | bytes 3000000 | tf_op jit(solution)/shard_map/backward/pallas_call | solution.py:32
  38.5 1.7 %collective-permute-start.14 = (bf16[64,512]{1,0:T(8,128)(2,1)S(1)}, bf16[64,512]{1,0:T(8,128)(2,1)S(1)}, u32[]{:S(2)}, u32[]{:S(2)}) collective-permute-start(bf16[64,512]{1,0:T(8,128)(2,1)S(1)} %get-tuple-element.80), channel_id=1, source_target_pairs={{0,6},{1,7},{2,4},{3,5},{4,2},{5,3},{6,0},{7,1},{8,14},{9,15},{10,... | collective-permute-start | bytes 196616 | tf_op jit(solution)/shard_map/ppermute | solution.py:24
  40.7 1.3 %collective-permute-start.16 = (bf16[64,512]{1,0:T(8,128)(2,1)S(1)}, bf16[64,512]{1,0:T(8,128)(2,1)S(1)}, u32[]{:S(2)}, u32[]{:S(2)}) collective-permute-start(bf16[64,512]{1,0:T(8,128)(2,1)S(1)} %get-tuple-element.82), channel_id=1, source_target_pairs={{0,4},{1,5},{2,6},{3,7},{4,0},{5,1},{6,2},{7,3},{8,12},{9,13},{10,... | collective-permute-start | bytes 196616 | tf_op jit(solution)/shard_map/ppermute | solution.py:24
  42.0 1.7 %collective-permute-done.14.r1 = bf16[64,512]{1,0:T(8,128)(2,1)S(1)} collective-permute-done((bf16[64,512]{1,0:T(8,128)(2,1)S(1)}, bf16[64,512]{1,0:T(8,128)(2,1)S(1)}, u32[]{:S(2)}, u32[]{:S(2)}) %collective-permute-start.14) | collective-permute-done | bytes 65568 | tf_op jit(solution)/shard_map/ppermute | solution.py:24
  45.3 2.6 %collective-permute-start.19 = (f32[32,128]{1,0:T(8,128)S(1)}, f32[32,128]{1,0:T(8,128)S(1)}, u32[]{:S(2)}, u32[]{:S(2)}) collective-permute-start(f32[32,128]{1,0:T(8,128)S(1)} %get-tuple-element.90.pack), channel_id=1, source_target_pairs={{0,8},{1,9},{2,10},{3,11},{4,12},{5,13},{6,14},{7,15},{8,0},{9,1},... | collective-permute-start | bytes 49160 | tf_op jit(solution)/shard_map/ppermute | solution.py:24
  50.0 2.0 %collective-permute-done.20.other_b = f32[32,128]{1,0:T(8,128)S(1)} collective-permute-done((f32[32,128]{1,0:T(8,128)S(1)}, f32[32,128]{1,0:T(8,128)S(1)}, u32[]{:S(2)}, u32[]{:S(2)}) %collective-permute-start.20) | collective-permute-done | bytes 16416 | tf_op jit(solution)/shard_map/ppermute | solution.py:24
  52.1 1.7 %collective-permute-start.21 = (bf16[32,640]{1,0:T(8,128)(2,1)S(1)}, bf16[32,640]{1,0:T(8,128)(2,1)S(1)}, u32[]{:S(2)}, u32[]{:S(2)}) collective-permute-start(bf16[32,640]{1,0:T(8,128)(2,1)S(1)} %get-tuple-element.94), channel_id=1, source_target_pairs={{0,6},{1,7},{2,4},{3,5},{4,2},{5,3},{6,0},{7,1},{8,14},{9,15},{10,... | collective-permute-start | bytes 122888 | tf_op jit(solution)/shard_map/ppermute | solution.py:24
  53.8 1.2 %collective-permute-start.22 = (bf16[32,640]{1,0:T(8,128)(2,1)S(1)}, bf16[32,640]{1,0:T(8,128)(2,1)S(1)}, u32[]{:S(2)}, u32[]{:S(2)}) collective-permute-start(bf16[32,640]{1,0:T(8,128)(2,1)S(1)} %get-tuple-element.95), channel_id=1, source_target_pairs={{0,2},{1,3},{2,0},{3,1},{4,6},{5,7},{6,4},{7,5},{8,10},{9,11},{10,... | collective-permute-start | bytes 122888 | tf_op jit(solution)/shard_map/ppermute | solution.py:24
  55.6 1.5 %collective-permute-done.21.r1 = bf16[32,640]{1,0:T(8,128)(2,1)S(1)} collective-permute-done((bf16[32,640]{1,0:T(8,128)(2,1)S(1)}, bf16[32,640]{1,0:T(8,128)(2,1)S(1)}, u32[]{:S(2)}, u32[]{:S(2)}) %collective-permute-start.21) | collective-permute-done | bytes 40992 | tf_op jit(solution)/shard_map/ppermute | solution.py:24
  (53 shorter events, 14.1 us)
Async XLA Ops:
  0.7 15.1 %collective-permute-start.2 = (bf16[512,512]{1,0:T(8,128)(2,1)}, bf16[512,512]{1,0:T(8,128)(2,1)S(1)}, u32[]{:S(2)}, u32[]{:S(2)}) collective-permute-start(bf16[512,512]{1,0:T(8,128)(2,1)} %emb_hbm.1), channel_id=1, source_target_pairs={{0,1},{1,0},{2,3},{3,2},{4,5},{5,4},{6,7},{7,6},{8,9},{9,8},{10,11... | collective-permute-start | bytes 1572872 | tf_op jit(solution)/shard_map/ppermute | solution.py:24
  2.5 9.7 %collective-permute-start.4 = (bf16[256,512]{1,0:T(8,128)(2,1)S(1)}, bf16[256,512]{1,0:T(8,128)(2,1)S(1)}, u32[]{:S(2)}, u32[]{:S(2)}) collective-permute-start(bf16[256,512]{1,0:T(8,128)(2,1)S(1)} %get-tuple-element.52.refs_0_.refs_2_), channel_id=1, source_target_pairs={{0,4},{1,5},{2,6},{3,7},{4,0},{5,1},{6,2},{7,3},{8,12},{9,13},{10,... | collective-permute-start | bytes 786440 | tf_op jit(solution)/shard_map/ppermute | solution.py:24
  5.1 9.1 %collective-permute-start.6 = (bf16[256,512]{1,0:T(8,128)(2,1)S(1)}, bf16[256,512]{1,0:T(8,128)(2,1)S(1)}, u32[]{:S(2)}, u32[]{:S(2)}) collective-permute-start(bf16[256,512]{1,0:T(8,128)(2,1)S(1)} %get-tuple-element.53.refs_1_.refs_3_), channel_id=1, source_target_pairs={{0,2},{1,3},{2,0},{3,1},{4,6},{5,7},{6,4},{7,5},{8,10},{9,11},{10,... | collective-permute-start | bytes 786440 | tf_op jit(solution)/shard_map/ppermute | solution.py:24
  6.6 13.2 %collective-permute-start = (bf16[256,512]{1,0:T(8,128)(2,1)S(1)}, bf16[256,512]{1,0:T(8,128)(2,1)S(1)}, u32[]{:S(2)}, u32[]{:S(2)}) collective-permute-start(bf16[256,512]{1,0:T(8,128)(2,1)S(1)} %get-tuple-element.52.refs_0_.refs_2_), channel_id=1, source_target_pairs={{0,2},{1,3},{2,0},{3,1},{4,6},{5,7},{6,4},{7,5},{8,10},{9,11},{10,... | collective-permute-start | bytes 786440 | tf_op jit(solution)/shard_map/ppermute | solution.py:24
  7.1 12.7 %collective-permute-start.1 = (bf16[256,512]{1,0:T(8,128)(2,1)S(1)}, bf16[256,512]{1,0:T(8,128)(2,1)S(1)}, u32[]{:S(2)}, u32[]{:S(2)}) collective-permute-start(bf16[256,512]{1,0:T(8,128)(2,1)S(1)} %get-tuple-element.53.refs_1_.refs_3_), channel_id=1, source_target_pairs={{0,4},{1,5},{2,6},{3,7},{4,0},{5,1},{6,2},{7,3},{8,12},{9,13},{10,... | collective-permute-start | bytes 786440 | tf_op jit(solution)/shard_map/ppermute | solution.py:24
  12.2 12.8 %collective-permute-start.5 = (bf16[256,512]{1,0:T(8,128)(2,1)S(1)}, bf16[256,512]{1,0:T(8,128)(2,1)S(1)}, u32[]{:S(2)}, u32[]{:S(2)}) collective-permute-start(bf16[256,512]{1,0:T(8,128)(2,1)S(1)} %collective-permute-done.4.refs_6_), channel_id=1, source_target_pairs={{0,2},{1,3},{2,0},{3,1},{4,6},{5,7},{6,4},{7,5},{8,10},{9,11},{10,... | collective-permute-start | bytes 786440 | tf_op jit(solution)/shard_map/ppermute | solution.py:24
  14.2 10.8 %collective-permute-start.7 = (bf16[256,512]{1,0:T(8,128)(2,1)S(1)}, bf16[256,512]{1,0:T(8,128)(2,1)S(1)}, u32[]{:S(2)}, u32[]{:S(2)}) collective-permute-start(bf16[256,512]{1,0:T(8,128)(2,1)S(1)} %collective-permute-done.6.refs_5_), channel_id=1, source_target_pairs={{0,4},{1,5},{2,6},{3,7},{4,0},{5,1},{6,2},{7,3},{8,12},{9,13},{10,... | collective-permute-start | bytes 786440 | tf_op jit(solution)/shard_map/ppermute | solution.py:24
  19.8 2.3 %collective-permute-start.3 = (f32[64,640]{1,0:T(8,128)S(1)}, f32[64,640]{1,0:T(8,128)S(1)}, u32[]{:S(2)}, u32[]{:S(2)}) collective-permute-start(f32[64,640]{1,0:T(8,128)S(1)} %get-tuple-element.59.msg_a), channel_id=1, source_target_pairs={{0,1},{1,0},{2,3},{3,2},{4,5},{5,4},{6,7},{7,6},{8,9},{9,8},{10,11... | collective-permute-start | bytes 491528 | tf_op jit(solution)/shard_map/ppermute | solution.py:24
  22.1 4.7 %collective-permute-start.9 = (f32[32,128]{1,0:T(8,128)S(1)}, f32[32,128]{1,0:T(8,128)S(1)}, u32[]{:S(2)}, u32[]{:S(2)}) collective-permute-start(f32[32,128]{1,0:T(8,128)S(1)} %slice_add_fusion), channel_id=1, source_target_pairs={{0,8},{1,9},{2,10},{3,11},{4,12},{5,13},{6,14},{7,15},{8,0},{9,1},... | collective-permute-start | bytes 49160 | tf_op jit(solution)/shard_map/ppermute | solution.py:24
  26.2 1.2 %collective-permute-start.8 = (f32[1,1024]{1,0:T(1,128)S(1)}, f32[1,1024]{1,0:T(1,128)S(1)}, u32[]{:S(2)}, u32[]{:S(2)}) collective-permute-start(f32[1,1024]{1,0:T(1,128)S(1)} %get-tuple-element.64.sums_own), channel_id=1, source_target_pairs={{0,1},{1,0},{2,3},{3,2},{4,5},{5,4},{6,7},{7,6},{8,9},{9,8},{10,11... | collective-permute-start | bytes 12296 | tf_op jit(solution)/shard_map/ppermute | solution.py:24
  28.3 5.8 %collective-permute-start.10 = (bf16[64,640]{1,0:T(8,128)(2,1)S(1)}, bf16[64,640]{1,0:T(8,128)(2,1)S(1)}, u32[]{:S(2)}, u32[]{:S(2)}) collective-permute-start(bf16[64,640]{1,0:T(8,128)(2,1)S(1)} %get-tuple-element.72), channel_id=1, source_target_pairs={{0,6},{1,7},{2,4},{3,5},{4,2},{5,3},{6,0},{7,1},{8,14},{9,15},{10,... | collective-permute-start | bytes 245768 | tf_op jit(solution)/shard_map/ppermute | solution.py:24
  29.7 5.8 %collective-permute-start.11 = (bf16[64,640]{1,0:T(8,128)(2,1)S(1)}, bf16[64,640]{1,0:T(8,128)(2,1)S(1)}, u32[]{:S(2)}, u32[]{:S(2)}) collective-permute-start(bf16[64,640]{1,0:T(8,128)(2,1)S(1)} %get-tuple-element.73), channel_id=1, source_target_pairs={{0,2},{1,3},{2,0},{3,1},{4,6},{5,7},{6,4},{7,5},{8,10},{9,11},{10,... | collective-permute-start | bytes 245768 | tf_op jit(solution)/shard_map/ppermute | solution.py:24
  30.1 5.4 %collective-permute-start.12 = (bf16[64,640]{1,0:T(8,128)(2,1)S(1)}, bf16[64,640]{1,0:T(8,128)(2,1)S(1)}, u32[]{:S(2)}, u32[]{:S(2)}) collective-permute-start(bf16[64,640]{1,0:T(8,128)(2,1)S(1)} %get-tuple-element.74), channel_id=1, source_target_pairs={{0,4},{1,5},{2,6},{3,7},{4,0},{5,1},{6,2},{7,3},{8,12},{9,13},{10,... | collective-permute-start | bytes 245768 | tf_op jit(solution)/shard_map/ppermute | solution.py:24
  35.8 1.9 %collective-permute-start.13 = (bf16[32,512]{1,0:T(8,128)(2,1)S(1)}, bf16[32,512]{1,0:T(8,128)(2,1)S(1)}, u32[]{:S(2)}, u32[]{:S(2)}) collective-permute-start(bf16[32,512]{1,0:T(8,128)(2,1)S(1)} %get-tuple-element.77.u_a), channel_id=1, source_target_pairs={{0,1},{1,0},{2,3},{3,2},{4,5},{5,4},{6,7},{7,6},{8,9},{9,8},{10,11... | collective-permute-start | bytes 98312 | tf_op jit(solution)/shard_map/ppermute | solution.py:24
  37.1 7.9 %collective-permute-start.17 = (f32[32,1024]{1,0:T(8,128)S(1)}, f32[32,1024]{1,0:T(8,128)S(1)}, u32[]{:S(2)}, u32[]{:S(2)}) collective-permute-start(f32[32,1024]{1,0:T(8,128)S(1)} %backward.1.back_a), channel_id=1, source_target_pairs={{0,1},{1,0},{2,3},{3,2},{4,5},{5,4},{6,7},{7,6},{8,9},{9,8},{10,11... | collective-permute-start | bytes 393224 | tf_op jit(solution)/shard_map/ppermute | solution.py:24
  38.5 5.3 %collective-permute-start.14 = (bf16[64,512]{1,0:T(8,128)(2,1)S(1)}, bf16[64,512]{1,0:T(8,128)(2,1)S(1)}, u32[]{:S(2)}, u32[]{:S(2)}) collective-permute-start(bf16[64,512]{1,0:T(8,128)(2,1)S(1)} %get-tuple-element.80), channel_id=1, source_target_pairs={{0,6},{1,7},{2,4},{3,5},{4,2},{5,3},{6,0},{7,1},{8,14},{9,15},{10,... | collective-permute-start | bytes 196616 | tf_op jit(solution)/shard_map/ppermute | solution.py:24
  40.2 4.7 %collective-permute-start.15 = (bf16[64,512]{1,0:T(8,128)(2,1)S(1)}, bf16[64,512]{1,0:T(8,128)(2,1)S(1)}, u32[]{:S(2)}, u32[]{:S(2)}) collective-permute-start(bf16[64,512]{1,0:T(8,128)(2,1)S(1)} %get-tuple-element.81), channel_id=1, source_target_pairs={{0,2},{1,3},{2,0},{3,1},{4,6},{5,7},{6,4},{7,5},{8,10},{9,11},{10,... | collective-permute-start | bytes 196616 | tf_op jit(solution)/shard_map/ppermute | solution.py:24
  40.7 4.3 %collective-permute-start.16 = (bf16[64,512]{1,0:T(8,128)(2,1)S(1)}, bf16[64,512]{1,0:T(8,128)(2,1)S(1)}, u32[]{:S(2)}, u32[]{:S(2)}) collective-permute-start(bf16[64,512]{1,0:T(8,128)(2,1)S(1)} %get-tuple-element.82), channel_id=1, source_target_pairs={{0,4},{1,5},{2,6},{3,7},{4,0},{5,1},{6,2},{7,3},{8,12},{9,13},{10,... | collective-permute-start | bytes 196616 | tf_op jit(solution)/shard_map/ppermute | solution.py:24
  45.2 2.8 %collective-permute-start.18 = (bf16[32,640]{1,0:T(8,128)(2,1)S(1)}, bf16[32,640]{1,0:T(8,128)(2,1)S(1)}, u32[]{:S(2)}, u32[]{:S(2)}) collective-permute-start(bf16[32,640]{1,0:T(8,128)(2,1)S(1)} %get-tuple-element.88.u_a), channel_id=1, source_target_pairs={{0,1},{1,0},{2,3},{3,2},{4,5},{5,4},{6,7},{7,6},{8,9},{9,8},{10,11... | collective-permute-start | bytes 122888 | tf_op jit(solution)/shard_map/ppermute | solution.py:24
  45.3 4.7 %collective-permute-start.19 = (f32[32,128]{1,0:T(8,128)S(1)}, f32[32,128]{1,0:T(8,128)S(1)}, u32[]{:S(2)}, u32[]{:S(2)}) collective-permute-start(f32[32,128]{1,0:T(8,128)S(1)} %get-tuple-element.90.pack), channel_id=1, source_target_pairs={{0,8},{1,9},{2,10},{3,11},{4,12},{5,13},{6,14},{7,15},{8,0},{9,1},... | collective-permute-start | bytes 49160 | tf_op jit(solution)/shard_map/ppermute | solution.py:24
  47.9 4.1 %collective-permute-start.20 = (f32[32,128]{1,0:T(8,128)S(1)}, f32[32,128]{1,0:T(8,128)S(1)}, u32[]{:S(2)}, u32[]{:S(2)}) collective-permute-start(f32[32,128]{1,0:T(8,128)S(1)} %get-tuple-element.90.pack), channel_id=1, source_target_pairs={{0,9},{1,8},{2,11},{3,10},{4,13},{5,12},{6,15},{7,14},{8,1},{9,0},... | collective-permute-start | bytes 49160 | tf_op jit(solution)/shard_map/ppermute | solution.py:24
  52.1 5.0 %collective-permute-start.21 = (bf16[32,640]{1,0:T(8,128)(2,1)S(1)}, bf16[32,640]{1,0:T(8,128)(2,1)S(1)}, u32[]{:S(2)}, u32[]{:S(2)}) collective-permute-start(bf16[32,640]{1,0:T(8,128)(2,1)S(1)} %get-tuple-element.94), channel_id=1, source_target_pairs={{0,6},{1,7},{2,4},{3,5},{4,2},{5,3},{6,0},{7,1},{8,14},{9,15},{10,... | collective-permute-start | bytes 122888 | tf_op jit(solution)/shard_map/ppermute | solution.py:24
  53.8 4.0 %collective-permute-start.22 = (bf16[32,640]{1,0:T(8,128)(2,1)S(1)}, bf16[32,640]{1,0:T(8,128)(2,1)S(1)}, u32[]{:S(2)}, u32[]{:S(2)}) collective-permute-start(bf16[32,640]{1,0:T(8,128)(2,1)S(1)} %get-tuple-element.95), channel_id=1, source_target_pairs={{0,2},{1,3},{2,0},{3,1},{4,6},{5,7},{6,4},{7,5},{8,10},{9,11},{10,... | collective-permute-start | bytes 122888 | tf_op jit(solution)/shard_map/ppermute | solution.py:24
  55.0 4.0 %collective-permute-start.23 = (bf16[32,640]{1,0:T(8,128)(2,1)S(1)}, bf16[32,640]{1,0:T(8,128)(2,1)S(1)}, u32[]{:S(2)}, u32[]{:S(2)}) collective-permute-start(bf16[32,640]{1,0:T(8,128)(2,1)S(1)} %get-tuple-element.96), channel_id=1, source_target_pairs={{0,4},{1,5},{2,6},{3,7},{4,0},{5,1},{6,2},{7,3},{8,12},{9,13},{10,... | collective-permute-start | bytes 122888 | tf_op jit(solution)/shard_map/ppermute | solution.py:24
  (7 other events, 68.7 us)

commit v5 on v4

--- a/solution.py
+++ b/solution.py
@@ -242,13 +242,14 @@
     part_out[...] = lane_pack([norm, row_sum(f * restart)], batch)
 
 
-def backward_kernel(emit, r1, r2, r3, w0, w1, w2, w3, out):
+def backward_kernel(emit, r1, r2, r3, w0, w1, w2, w3, own_out, sib_out):
     states = w0.shape[1]
-    batch = out.shape[0]
+    batch = own_out.shape[0]
     acc = dot(emit[3 * batch :].astype(BF16), w0[...], NT)
     for r, w in ((r1, w1), (r2, w2), (r3, w3)):
         acc = acc + dot(r[batch:, :states], w[...], NT)
-    out[...] = acc
+    own_out[...] = acc[:, :states]
+    sib_out[...] = acc[:, states:]
 
 
 def second_kernel(u_a, u_b, u_chain, w0, w1, w2, w3, own, s1, s2, s3):
@@ -299,7 +300,7 @@
     chain_out[...] = chain
     u = (g * (1.0 - restart) * inv[...]).astype(BF16)
     msg_out[:, :states] = u
-    last = row_sum(u.astype(F32) * (back_a[:, :states] + back_b[:, states:]))
+    last = row_sum(u.astype(F32) * (back_a[...] + back_b[...]))
     h2 = p * e[2 * batch : 3 * batch]
     main = jnp.where(length == 1, p * e[:batch], jnp.where(length == 2, f1[...], g))
     side = jnp.where(length == 3, h2, chain)
@@ -323,10 +324,9 @@
     return jnp.where(lane < 6, packed, 0.0)
 
 
-def totals_kernel(msg_sib, pack, other_a, other_b, out):
+def totals_kernel(msg_sib, pack, out):
     states = msg_sib.shape[1] - 128
-    here = pack[...] + joined(msg_sib[:, states:])
-    out[...] = clean(here + (other_a[...] + other_b[...]))
+    out[...] = clean(pack[...] + joined(msg_sib[:, states:]))
 
 
 def attach_kernel(total, s1, s2, s3, o1, o2, o3):
@@ -336,8 +336,8 @@
         out[:, states:] = parts
 
 
-def attach_sum_kernel(msg_sib, pack, other_a, other_b, s1, s2, s3, total, o1, o2, o3):
-    totals_kernel(msg_sib, pack, other_a, other_b, total)
+def attach_sum_kernel(here, other, s1, s2, s3, total, o1, o2, o3):
+    total[...] = here[...] + other[...]
     attach_kernel(total, s1, s2, s3, o1, o2, o3)
 
 
@@ -481,14 +481,17 @@
     )
     u1_sib = across(u1, 1)
     held, _ = lax.optimization_barrier((tuple(received), u1))
-    back = call(backward_kernel, shape((batch, 2 * states), F32), "backward", micros=1)(emit, *held, *wts)
+    back, back_sib = call(backward_kernel, (plane, plane), "backward", micros=1)(
+        emit, *held, *wts
+    )
     own, *sends = call(
         second_kernel,
         (shape((2 * batch, states), F32),) + (shape((2 * batch, states), BF16),) * 3,
         "second",
         micros=1,
     )(u1, u1_sib, u_chain, *wts)
-    back_sib = across(back, 1)
+    back_sib, own = lax.optimization_barrier((back_sib, own))
+    back_sib = across(back_sib, 1)
     received = [across(s, shift) for shift, s in zip(SHIFTS, sends)]
     g2, chain, msg2, pack = call(combine_kernel, (plane, plane, message, lanes), "combine")(
         own,
@@ -504,17 +507,18 @@
         length_row,
     )
     msg2_sib = across(msg2, 1)
-    others = [across(pack, cluster), across(pack, cluster + 1)]
+    totals = call(totals_kernel, lanes, "totals")(msg2_sib, pack)
     own, *sends = call(third_kernel, (plane,) + (message,) * 3, "third", micros=1)(
         msg2, msg2_sib, *wts
     )
+    other = across(totals, cluster)
+    apart = 2 * cluster
     if cols == 2 * cluster:
         totals, *sends = call(
-            attach_sum_kernel, (lanes,) + (message,) * 3, "attach", aliases={4: 1, 5: 2, 6: 3}
-        )(msg2_sib, pack, *others, *sends)
+            attach_sum_kernel, (lanes,) + (message,) * 3, "attach", aliases={2: 1, 3: 2, 4: 3}
+        )(totals, other, *sends)
     else:
-        totals = call(totals_kernel, lanes, "totals")(msg2_sib, pack, *others)
-        apart = 2 * cluster
+        totals = totals + other
         while apart < cols:
             totals = totals + across(totals, apart)
             apart *= 2

time: 60 us -> 59 us (0.983)
  waiting for transfers between devices: 17.7 us -> 17 us
    ppermute x24 -> x23, waiting for transfers between devices: 17.7 us -> 17 us  [across(): lax.ppermute(shard, axis, [(i, i ^ apart) for i in range(lax.axis_size(ax...]
    ppermute x24 -> x23, starting transfers between devices: 25.4 us -> 25.2 us  [across(): lax.ppermute(shard, axis, [(i, i ^ apart) for i in range(lax.axis_size(ax...]
    pallas_call x13 -> x14, Pallas kernels: 15.9 us -> 15.9 us  [run(): pl.pallas_call(body, out_shape=out_shape, in_specs=[pl.BlockSpec(memory_s...]
  transfers between devices with their start and end apart: 24 -> 23, of which waited for: 16 -> 16; matrix products, arithmetic and copies ran while one was open for 0% -> 0% of each run, Pallas kernels for 23% -> 22%
where the time goes in v5:
time: 59 us; the launch traced here: 58.9 us
  starting transfers between devices  25.2 us (43%)
  waiting for transfers between devices  17 us (29%)
  Pallas kernels  15.9 us (27%)
  between operations  0.8 us (1%)
    ppermute x23, starting transfers between devices, across(): lax.ppermute(shard, axis, [(i, i ^ apart) for i in range(lax.axis_size(ax...  25.2 us
    ppermute x23, waiting for transfers between devices, across(): lax.ppermute(shard, axis, [(i, i ^ apart) for i in range(lax.axis_size(ax...  17 us
    pallas_call x14, Pallas kernels, run(): pl.pallas_call(body, out_shape=out_shape, in_specs=[pl.BlockSpec(memory_s...  15.9 us
  transfers between devices with their start and end apart: 23, of which 16 were waited for; matrix products, arithmetic and copies ran while one was open for 0% of the time, Pallas kernels for 22%

profile of v5, /device:TPU:0, one launch (start us, length us, event | category | flops | bytes accessed | tf_op | source)
XLA Modules:
  0.0 58.9 jit_solution(13338673840998625202)
XLA Ops:
  1.2 1.3 %halves.1 = (bf16[256,512]{1,0:T(8,128)(2,1)S(1)}, bf16[256,512]{1,0:T(8,128)(2,1)S(1)}) custom-call(bf16[512,512]{1,0:T(8,128)(2,1)} %emb_hbm.1), custom_call_target="tpu_custom_call" | custom-call | flops 6000000000 | bytes 18000000 | tf_op jit(solution)/shard_map/halves/pallas_call | solution.py:32
  2.5 2.5 %collective-permute-start.4 = (bf16[256,512]{1,0:T(8,128)(2,1)S(1)}, bf16[256,512]{1,0:T(8,128)(2,1)S(1)}, u32[]{:S(2)}, u32[]{:S(2)}) collective-permute-start(bf16[256,512]{1,0:T(8,128)(2,1)S(1)} %get-tuple-element.56.refs_0_.refs_2_), channel_id=1, source_target_pairs={{0,4},{1,5},{2,6},{3,7},{4,0},{5,1},{6,2},{7,3},{8,12},{9,13},{10,... | collective-permute-start | bytes 786440 | tf_op jit(solution)/shard_map/ppermute | solution.py:24
  5.1 1.5 %collective-permute-start.6 = (bf16[256,512]{1,0:T(8,128)(2,1)S(1)}, bf16[256,512]{1,0:T(8,128)(2,1)S(1)}, u32[]{:S(2)}, u32[]{:S(2)}) collective-permute-start(bf16[256,512]{1,0:T(8,128)(2,1)S(1)} %get-tuple-element.57.refs_1_.refs_3_), channel_id=1, source_target_pairs={{0,2},{1,3},{2,0},{3,1},{4,6},{5,7},{6,4},{7,5},{8,10},{9,11},{10,... | collective-permute-start | bytes 786440 | tf_op jit(solution)/shard_map/ppermute | solution.py:24
  7.2 4.1 %emission.1 = (f32[1,512]{1,0:T(1,128)S(1)}, f32[128,512]{1,0:T(8,128)S(1)}, f32[64,640]{1,0:T(8,128)S(1)}, f32[32,128]{1,0:T(8,128)S(1)}) custom-call(bf16[256,512]{1,0:T(8,128)(2,1)S(1)} %get-tuple-element.56.refs_0_.refs_2_, bf16[256,512]{1,0:T(8,128)(2,1)S(1)} %get-tuple-element.57.refs_1_.refs_3_, bf16[512,512]{1,0:T(8,128)(2,1)S(1)} %copy-done.1, ...), custom_call_target="tpu_custom_call" | custom-call | flops 500000000 | bytes 1500000 | tf_op jit(solution)/shard_map/emission/pallas_call | solution.py:32
  12.2 2.0 %collective-permute-start.5 = (bf16[256,512]{1,0:T(8,128)(2,1)S(1)}, bf16[256,512]{1,0:T(8,128)(2,1)S(1)}, u32[]{:S(2)}, u32[]{:S(2)}) collective-permute-start(bf16[256,512]{1,0:T(8,128)(2,1)S(1)} %collective-permute-done.4.refs_6_), channel_id=1, source_target_pairs={{0,2},{1,3},{2,0},{3,1},{4,6},{5,7},{6,4},{7,5},{8,10},{9,11},{10,... | collective-permute-start | bytes 786440 | tf_op jit(solution)/shard_map/ppermute | solution.py:24
  14.2 1.6 %collective-permute-start.7 = (bf16[256,512]{1,0:T(8,128)(2,1)S(1)}, bf16[256,512]{1,0:T(8,128)(2,1)S(1)}, u32[]{:S(2)}, u32[]{:S(2)}) collective-permute-start(bf16[256,512]{1,0:T(8,128)(2,1)S(1)} %collective-permute-done.6.refs_5_), channel_id=1, source_target_pairs={{0,4},{1,5},{2,6},{3,7},{4,0},{5,1},{6,2},{7,3},{8,12},{9,13},{10,... | collective-permute-start | bytes 786440 | tf_op jit(solution)/shard_map/ppermute | solution.py:24
  15.8 1.7 %sources.1 = (bf16[512,512]{1,0:T(8,128)(2,1)S(1)}, bf16[512,512]{1,0:T(8,128)(2,1)S(1)}, bf16[1024,512]{1,0:T(8,128)(2,1)S(1)}, f32[1024,128]{1,0:T(8,128)S(1)}) custom-call(s32[8,16]{1,0:T(8,128)S(1)} %bitcast.10, bf16[512,512]{1,0:T(8,128)(2,1)S(1)} %copy-done.5, bf16[256,512]{1,0:T(8,128)(2,1)S(1)} %get-tuple-element.56.refs_0_.refs_2_, ...), custom_call_target="tpu_custom_call" | custom-call | flops 1500000000 | bytes 4500000 | tf_op jit(solution)/shard_map/sources/pallas_call | solution.py:32
  17.5 2.3 %collective-permute-done.refs_4_ = bf16[256,512]{1,0:T(8,128)(2,1)S(1)} collective-permute-done((bf16[256,512]{1,0:T(8,128)(2,1)S(1)}, bf16[256,512]{1,0:T(8,128)(2,1)S(1)}, u32[]{:S(2)}, u32[]{:S(2)}) %collective-permute-start) | collective-permute-done | bytes 262176 | tf_op jit(solution)/shard_map/ppermute | solution.py:24
  19.8 2.3 %weights.2 = (bf16[1024,512]{1,0:T(8,128)(2,1)S(1)}, bf16[1024,512]{1,0:T(8,128)(2,1)S(1)}, f32[1024,128]{1,0:T(8,128)S(1)}) custom-call(s32[8,16]{1,0:T(8,128)S(1)} %bitcast.11, bf16[512,512]{1,0:T(8,128)(2,1)S(1)} %copy-done.5, bf16[512,512]{1,0:T(8,128)(2,1)S(1)} %get-tuple-element.65.refs_2_, bf16[512,512]{1,0:T(8,128)(2,1)S(1)} %get-tuple-element.66.refs_3_, ...), custom_call_target="tpu_custom_call" | custom-call | flops 2000000000 | bytes 6000000 | tf_op jit(solution)/shard_map/weights/pallas_call | solution.py:32
  22.1 2.7 %collective-permute-start.9 = (f32[32,128]{1,0:T(8,128)S(1)}, f32[32,128]{1,0:T(8,128)S(1)}, u32[]{:S(2)}, u32[]{:S(2)}) collective-permute-start(f32[32,128]{1,0:T(8,128)S(1)} %slice_add_fusion), channel_id=1, source_target_pairs={{0,8},{1,9},{2,10},{3,11},{4,12},{5,13},{6,14},{7,15},{8,0},{9,1},... | collective-permute-start | bytes 49160 | tf_op jit(solution)/shard_map/ppermute | solution.py:24
  25.0 1.3 %weights.3 = (bf16[1024,512]{1,0:T(8,128)(2,1)S(1)}, f32[1,1024]{1,0:T(1,128)S(1)}) custom-call(s32[8,16]{1,0:T(8,128)S(1)} %bitcast.12, bf16[512,512]{1,0:T(8,128)(2,1)S(1)} %copy-done.5, bf16[512,512]{1,0:T(8,128)(2,1)S(1)} %get-tuple-element.65.refs_2_, bf16[512,512]{1,0:T(8,128)(2,1)S(1)} %get-tuple-element.66.refs_3_, ...), custom_call_target="tpu_custom_call" | custom-call | flops 1500000000 | bytes 4500000 | tf_op jit(solution)/shard_map/weights/pallas_call | solution.py:32
  28.3 1.4 %collective-permute-start.10 = (bf16[64,640]{1,0:T(8,128)(2,1)S(1)}, bf16[64,640]{1,0:T(8,128)(2,1)S(1)}, u32[]{:S(2)}, u32[]{:S(2)}) collective-permute-start(bf16[64,640]{1,0:T(8,128)(2,1)S(1)} %get-tuple-element.75), channel_id=1, source_target_pairs={{0,6},{1,7},{2,4},{3,5},{4,2},{5,3},{6,0},{7,1},{8,14},{9,15},{10,... | collective-permute-start | bytes 245768 | tf_op jit(solution)/shard_map/ppermute | solution.py:24
  30.1 1.7 %collective-permute-start.12 = (bf16[64,640]{1,0:T(8,128)(2,1)S(1)}, bf16[64,640]{1,0:T(8,128)(2,1)S(1)}, u32[]{:S(2)}, u32[]{:S(2)}) collective-permute-start(bf16[64,640]{1,0:T(8,128)(2,1)S(1)} %get-tuple-element.77), channel_id=1, source_target_pairs={{0,4},{1,5},{2,6},{3,7},{4,0},{5,1},{6,2},{7,3},{8,12},{9,13},{10,... | collective-permute-start | bytes 245768 | tf_op jit(solution)/shard_map/ppermute | solution.py:24
  31.8 2.3 %collective-permute-done.10.r1 = bf16[64,640]{1,0:T(8,128)(2,1)S(1)} collective-permute-done((bf16[64,640]{1,0:T(8,128)(2,1)S(1)}, bf16[64,640]{1,0:T(8,128)(2,1)S(1)}, u32[]{:S(2)}, u32[]{:S(2)}) %collective-permute-start.10) | collective-permute-done | bytes 81952 | tf_op jit(solution)/shard_map/ppermute | solution.py:24
  34.1 1.4 %collective-permute-done.11.r2 = bf16[64,640]{1,0:T(8,128)(2,1)S(1)} collective-permute-done((bf16[64,640]{1,0:T(8,128)(2,1)S(1)}, bf16[64,640]{1,0:T(8,128)(2,1)S(1)}, u32[]{:S(2)}, u32[]{:S(2)}) %collective-permute-start.11) | collective-permute-done | bytes 81952 | tf_op jit(solution)/shard_map/ppermute | solution.py:24
  35.8 1.3 %backward.1 = (f32[32,512]{1,0:T(8,128)S(1)}, f32[32,512]{1,0:T(8,128)S(1)}) custom-call(f32[128,512]{1,0:T(8,128)S(1)} %get-tuple-element.58.emit, bf16[64,640]{1,0:T(8,128)(2,1)S(1)} %collective-permute-done.10.r1, bf16[64,640]{1,0:T(8,128)(2,1)S(1)} %collective-permute-done.11.r2, bf16[64,640]{1,0:T(8,128)(2,1)S(1)} %collective-permute-done.12.r3, ...), custom_call_target="tpu_custom_call" | custom-call | flops 1000000000 | bytes 3000000 | tf_op jit(solution)/shard_map/backward/pallas_call | solution.py:32
  38.5 1.7 %collective-permute-start.14 = (bf16[64,512]{1,0:T(8,128)(2,1)S(1)}, bf16[64,512]{1,0:T(8,128)(2,1)S(1)}, u32[]{:S(2)}, u32[]{:S(2)}) collective-permute-start(bf16[64,512]{1,0:T(8,128)(2,1)S(1)} %get-tuple-element.89), channel_id=1, source_target_pairs={{0,6},{1,7},{2,4},{3,5},{4,2},{5,3},{6,0},{7,1},{8,14},{9,15},{10,... | collective-permute-start | bytes 196616 | tf_op jit(solution)/shard_map/ppermute | solution.py:24
  40.7 1.3 %collective-permute-start.16 = (bf16[64,512]{1,0:T(8,128)(2,1)S(1)}, bf16[64,512]{1,0:T(8,128)(2,1)S(1)}, u32[]{:S(2)}, u32[]{:S(2)}) collective-permute-start(bf16[64,512]{1,0:T(8,128)(2,1)S(1)} %get-tuple-element.91), channel_id=1, source_target_pairs={{0,4},{1,5},{2,6},{3,7},{4,0},{5,1},{6,2},{7,3},{8,12},{9,13},{10,... | collective-permute-start | bytes 196616 | tf_op jit(solution)/shard_map/ppermute | solution.py:24
  42.0 1.7 %collective-permute-done.14.r1 = bf16[64,512]{1,0:T(8,128)(2,1)S(1)} collective-permute-done((bf16[64,512]{1,0:T(8,128)(2,1)S(1)}, bf16[64,512]{1,0:T(8,128)(2,1)S(1)}, u32[]{:S(2)}, u32[]{:S(2)}) %collective-permute-start.14) | collective-permute-done | bytes 65568 | tf_op jit(solution)/shard_map/ppermute | solution.py:24
  45.3 1.2 %collective-permute-done.18.u_b.msg_sib = bf16[32,640]{1,0:T(8,128)(2,1)S(1)} collective-permute-done((bf16[32,640]{1,0:T(8,128)(2,1)S(1)}, bf16[32,640]{1,0:T(8,128)(2,1)S(1)}, u32[]{:S(2)}, u32[]{:S(2)}) %collective-permute-start.18) | collective-permute-done | bytes 40992 | tf_op jit(solution)/shard_map/ppermute | solution.py:24
  46.6 2.6 %collective-permute-start.19 = (f32[32,128]{1,0:T(8,128)S(1)}, f32[32,128]{1,0:T(8,128)S(1)}, u32[]{:S(2)}, u32[]{:S(2)}) collective-permute-start(f32[32,128]{1,0:T(8,128)S(1)} %totals.1.here), channel_id=1, source_target_pairs={{0,8},{1,9},{2,10},{3,11},{4,12},{5,13},{6,14},{7,15},{8,0},{9,1},... | collective-permute-start | bytes 49160 | tf_op jit(solution)/shard_map/ppermute | solution.py:24
  49.9 1.4 %collective-permute-done.19.other = f32[32,128]{1,0:T(8,128)S(1)} collective-permute-done((f32[32,128]{1,0:T(8,128)S(1)}, f32[32,128]{1,0:T(8,128)S(1)}, u32[]{:S(2)}, u32[]{:S(2)}) %collective-permute-start.19) | collective-permute-done | bytes 16416 | tf_op jit(solution)/shard_map/ppermute | solution.py:24
  51.4 1.6 %collective-permute-start.20 = (bf16[32,640]{1,0:T(8,128)(2,1)S(1)}, bf16[32,640]{1,0:T(8,128)(2,1)S(1)}, u32[]{:S(2)}, u32[]{:S(2)}) collective-permute-start(bf16[32,640]{1,0:T(8,128)(2,1)S(1)} %get-tuple-element.102), channel_id=1, source_target_pairs={{0,6},{1,7},{2,4},{3,5},{4,2},{5,3},{6,0},{7,1},{8,14},{9,15},{10,... | collective-permute-start | bytes 122888 | tf_op jit(solution)/shard_map/ppermute | solution.py:24
  54.9 1.5 %collective-permute-done.20.r1 = bf16[32,640]{1,0:T(8,128)(2,1)S(1)} collective-permute-done((bf16[32,640]{1,0:T(8,128)(2,1)S(1)}, bf16[32,640]{1,0:T(8,128)(2,1)S(1)}, u32[]{:S(2)}, u32[]{:S(2)}) %collective-permute-start.20) | collective-permute-done | bytes 40992 | tf_op jit(solution)/shard_map/ppermute | solution.py:24
  (52 shorter events, 13.9 us)
Async XLA Ops:
  0.7 15.1 %collective-permute-start.2 = (bf16[512,512]{1,0:T(8,128)(2,1)}, bf16[512,512]{1,0:T(8,128)(2,1)S(1)}, u32[]{:S(2)}, u32[]{:S(2)}) collective-permute-start(bf16[512,512]{1,0:T(8,128)(2,1)} %emb_hbm.1), channel_id=1, source_target_pairs={{0,1},{1,0},{2,3},{3,2},{4,5},{5,4},{6,7},{7,6},{8,9},{9,8},{10,11... | collective-permute-start | bytes 1572872 | tf_op jit(solution)/shard_map/ppermute | solution.py:24
  2.5 13.3 %copy-start.4 = (bf16[512,512]{1,0:T(8,128)(2,1)S(1)}, bf16[512,512]{1,0:T(8,128)(2,1)}, u32[]{:S(2)}) copy-start(bf16[512,512]{1,0:T(8,128)(2,1)} %refs_5_.3) | copy-start | bytes 1572868
  2.5 9.7 %collective-permute-start.4 = (bf16[256,512]{1,0:T(8,128)(2,1)S(1)}, bf16[256,512]{1,0:T(8,128)(2,1)S(1)}, u32[]{:S(2)}, u32[]{:S(2)}) collective-permute-start(bf16[256,512]{1,0:T(8,128)(2,1)S(1)} %get-tuple-element.56.refs_0_.refs_2_), channel_id=1, source_target_pairs={{0,4},{1,5},{2,6},{3,7},{4,0},{5,1},{6,2},{7,3},{8,12},{9,13},{10,... | collective-permute-start | bytes 786440 | tf_op jit(solution)/shard_map/ppermute | solution.py:24
  5.1 9.1 %collective-permute-start.6 = (bf16[256,512]{1,0:T(8,128)(2,1)S(1)}, bf16[256,512]{1,0:T(8,128)(2,1)S(1)}, u32[]{:S(2)}, u32[]{:S(2)}) collective-permute-start(bf16[256,512]{1,0:T(8,128)(2,1)S(1)} %get-tuple-element.57.refs_1_.refs_3_), channel_id=1, source_target_pairs={{0,2},{1,3},{2,0},{3,1},{4,6},{5,7},{6,4},{7,5},{8,10},{9,11},{10,... | collective-permute-start | bytes 786440 | tf_op jit(solution)/shard_map/ppermute | solution.py:24
  6.6 13.2 %collective-permute-start = (bf16[256,512]{1,0:T(8,128)(2,1)S(1)}, bf16[256,512]{1,0:T(8,128)(2,1)S(1)}, u32[]{:S(2)}, u32[]{:S(2)}) collective-permute-start(bf16[256,512]{1,0:T(8,128)(2,1)S(1)} %get-tuple-element.56.refs_0_.refs_2_), channel_id=1, source_target_pairs={{0,2},{1,3},{2,0},{3,1},{4,6},{5,7},{6,4},{7,5},{8,10},{9,11},{10,... | collective-permute-start | bytes 786440 | tf_op jit(solution)/shard_map/ppermute | solution.py:24
  7.1 12.7 %collective-permute-start.1 = (bf16[256,512]{1,0:T(8,128)(2,1)S(1)}, bf16[256,512]{1,0:T(8,128)(2,1)S(1)}, u32[]{:S(2)}, u32[]{:S(2)}) collective-permute-start(bf16[256,512]{1,0:T(8,128)(2,1)S(1)} %get-tuple-element.57.refs_1_.refs_3_), channel_id=1, source_target_pairs={{0,4},{1,5},{2,6},{3,7},{4,0},{5,1},{6,2},{7,3},{8,12},{9,13},{10,... | collective-permute-start | bytes 786440 | tf_op jit(solution)/shard_map/ppermute | solution.py:24
  12.2 12.8 %collective-permute-start.5 = (bf16[256,512]{1,0:T(8,128)(2,1)S(1)}, bf16[256,512]{1,0:T(8,128)(2,1)S(1)}, u32[]{:S(2)}, u32[]{:S(2)}) collective-permute-start(bf16[256,512]{1,0:T(8,128)(2,1)S(1)} %collective-permute-done.4.refs_6_), channel_id=1, source_target_pairs={{0,2},{1,3},{2,0},{3,1},{4,6},{5,7},{6,4},{7,5},{8,10},{9,11},{10,... | collective-permute-start | bytes 786440 | tf_op jit(solution)/shard_map/ppermute | solution.py:24
  14.2 10.8 %collective-permute-start.7 = (bf16[256,512]{1,0:T(8,128)(2,1)S(1)}, bf16[256,512]{1,0:T(8,128)(2,1)S(1)}, u32[]{:S(2)}, u32[]{:S(2)}) collective-permute-start(bf16[256,512]{1,0:T(8,128)(2,1)S(1)} %collective-permute-done.6.refs_5_), channel_id=1, source_target_pairs={{0,4},{1,5},{2,6},{3,7},{4,0},{5,1},{6,2},{7,3},{8,12},{9,13},{10,... | collective-permute-start | bytes 786440 | tf_op jit(solution)/shard_map/ppermute | solution.py:24
  19.8 2.3 %collective-permute-start.3 = (f32[64,640]{1,0:T(8,128)S(1)}, f32[64,640]{1,0:T(8,128)S(1)}, u32[]{:S(2)}, u32[]{:S(2)}) collective-permute-start(f32[64,640]{1,0:T(8,128)S(1)} %get-tuple-element.64.msg_a), channel_id=1, source_target_pairs={{0,1},{1,0},{2,3},{3,2},{4,5},{5,4},{6,7},{7,6},{8,9},{9,8},{10,11... | collective-permute-start | bytes 491528 | tf_op jit(solution)/shard_map/ppermute | solution.py:24
  22.1 4.7 %collective-permute-start.9 = (f32[32,128]{1,0:T(8,128)S(1)}, f32[32,128]{1,0:T(8,128)S(1)}, u32[]{:S(2)}, u32[]{:S(2)}) collective-permute-start(f32[32,128]{1,0:T(8,128)S(1)} %slice_add_fusion), channel_id=1, source_target_pairs={{0,8},{1,9},{2,10},{3,11},{4,12},{5,13},{6,14},{7,15},{8,0},{9,1},... | collective-permute-start | bytes 49160 | tf_op jit(solution)/shard_map/ppermute | solution.py:24
  26.2 1.2 %collective-permute-start.8 = (f32[1,1024]{1,0:T(1,128)S(1)}, f32[1,1024]{1,0:T(1,128)S(1)}, u32[]{:S(2)}, u32[]{:S(2)}) collective-permute-start(f32[1,1024]{1,0:T(1,128)S(1)} %get-tuple-element.69.sums_own), channel_id=1, source_target_pairs={{0,1},{1,0},{2,3},{3,2},{4,5},{5,4},{6,7},{7,6},{8,9},{9,8},{10,11... | collective-permute-start | bytes 12296 | tf_op jit(solution)/shard_map/ppermute | solution.py:24
  28.3 5.8 %collective-permute-start.10 = (bf16[64,640]{1,0:T(8,128)(2,1)S(1)}, bf16[64,640]{1,0:T(8,128)(2,1)S(1)}, u32[]{:S(2)}, u32[]{:S(2)}) collective-permute-start(bf16[64,640]{1,0:T(8,128)(2,1)S(1)} %get-tuple-element.75), channel_id=1, source_target_pairs={{0,6},{1,7},{2,4},{3,5},{4,2},{5,3},{6,0},{7,1},{8,14},{9,15},{10,... | collective-permute-start | bytes 245768 | tf_op jit(solution)/shard_map/ppermute | solution.py:24
  29.7 5.8 %collective-permute-start.11 = (bf16[64,640]{1,0:T(8,128)(2,1)S(1)}, bf16[64,640]{1,0:T(8,128)(2,1)S(1)}, u32[]{:S(2)}, u32[]{:S(2)}) collective-permute-start(bf16[64,640]{1,0:T(8,128)(2,1)S(1)} %get-tuple-element.76), channel_id=1, source_target_pairs={{0,2},{1,3},{2,0},{3,1},{4,6},{5,7},{6,4},{7,5},{8,10},{9,11},{10,... | collective-permute-start | bytes 245768 | tf_op jit(solution)/shard_map/ppermute | solution.py:24
  30.1 5.4 %collective-permute-start.12 = (bf16[64,640]{1,0:T(8,128)(2,1)S(1)}, bf16[64,640]{1,0:T(8,128)(2,1)S(1)}, u32[]{:S(2)}, u32[]{:S(2)}) collective-permute-start(bf16[64,640]{1,0:T(8,128)(2,1)S(1)} %get-tuple-element.77), channel_id=1, source_target_pairs={{0,4},{1,5},{2,6},{3,7},{4,0},{5,1},{6,2},{7,3},{8,12},{9,13},{10,... | collective-permute-start | bytes 245768 | tf_op jit(solution)/shard_map/ppermute | solution.py:24
  35.8 1.4 %collective-permute-start.13 = (bf16[32,512]{1,0:T(8,128)(2,1)S(1)}, bf16[32,512]{1,0:T(8,128)(2,1)S(1)}, u32[]{:S(2)}, u32[]{:S(2)}) collective-permute-start(bf16[32,512]{1,0:T(8,128)(2,1)S(1)} %get-tuple-element.81.u_a), channel_id=1, source_target_pairs={{0,1},{1,0},{2,3},{3,2},{4,5},{5,4},{6,7},{7,6},{8,9},{9,8},{10,11... | collective-permute-start | bytes 98312 | tf_op jit(solution)/shard_map/ppermute | solution.py:24
  38.0 4.1 %collective-permute-start.17 = (f32[32,512]{1,0:T(8,128)S(1)}, f32[32,512]{1,0:T(8,128)S(1)}, u32[]{:S(2)}, u32[]{:S(2)}) collective-permute-start(f32[32,512]{1,0:T(8,128)S(1)} %get-tuple-element.95), channel_id=1, source_target_pairs={{0,1},{1,0},{2,3},{3,2},{4,5},{5,4},{6,7},{7,6},{8,9},{9,8},{10,11... | collective-permute-start | bytes 196616 | tf_op jit(solution)/shard_map/ppermute | solution.py:24
  38.5 5.2 %collective-permute-start.14 = (bf16[64,512]{1,0:T(8,128)(2,1)S(1)}, bf16[64,512]{1,0:T(8,128)(2,1)S(1)}, u32[]{:S(2)}, u32[]{:S(2)}) collective-permute-start(bf16[64,512]{1,0:T(8,128)(2,1)S(1)} %get-tuple-element.89), channel_id=1, source_target_pairs={{0,6},{1,7},{2,4},{3,5},{4,2},{5,3},{6,0},{7,1},{8,14},{9,15},{10,... | collective-permute-start | bytes 196616 | tf_op jit(solution)/shard_map/ppermute | solution.py:24
  40.2 4.7 %collective-permute-start.15 = (bf16[64,512]{1,0:T(8,128)(2,1)S(1)}, bf16[64,512]{1,0:T(8,128)(2,1)S(1)}, u32[]{:S(2)}, u32[]{:S(2)}) collective-permute-start(bf16[64,512]{1,0:T(8,128)(2,1)S(1)} %get-tuple-element.90), channel_id=1, source_target_pairs={{0,2},{1,3},{2,0},{3,1},{4,6},{5,7},{6,4},{7,5},{8,10},{9,11},{10,... | collective-permute-start | bytes 196616 | tf_op jit(solution)/shard_map/ppermute | solution.py:24
  40.7 4.3 %collective-permute-start.16 = (bf16[64,512]{1,0:T(8,128)(2,1)S(1)}, bf16[64,512]{1,0:T(8,128)(2,1)S(1)}, u32[]{:S(2)}, u32[]{:S(2)}) collective-permute-start(bf16[64,512]{1,0:T(8,128)(2,1)S(1)} %get-tuple-element.91), channel_id=1, source_target_pairs={{0,4},{1,5},{2,6},{3,7},{4,0},{5,1},{6,2},{7,3},{8,12},{9,13},{10,... | collective-permute-start | bytes 196616 | tf_op jit(solution)/shard_map/ppermute | solution.py:24
  45.2 1.2 %collective-permute-start.18 = (bf16[32,640]{1,0:T(8,128)(2,1)S(1)}, bf16[32,640]{1,0:T(8,128)(2,1)S(1)}, u32[]{:S(2)}, u32[]{:S(2)}) collective-permute-start(bf16[32,640]{1,0:T(8,128)(2,1)S(1)} %get-tuple-element.96.u_a), channel_id=1, source_target_pairs={{0,1},{1,0},{2,3},{3,2},{4,5},{5,4},{6,7},{7,6},{8,9},{9,8},{10,11... | collective-permute-start | bytes 122888 | tf_op jit(solution)/shard_map/ppermute | solution.py:24
  46.6 4.8 %collective-permute-start.19 = (f32[32,128]{1,0:T(8,128)S(1)}, f32[32,128]{1,0:T(8,128)S(1)}, u32[]{:S(2)}, u32[]{:S(2)}) collective-permute-start(f32[32,128]{1,0:T(8,128)S(1)} %totals.1.here), channel_id=1, source_target_pairs={{0,8},{1,9},{2,10},{3,11},{4,12},{5,13},{6,14},{7,15},{8,0},{9,1},... | collective-permute-start | bytes 49160 | tf_op jit(solution)/shard_map/ppermute | solution.py:24
  51.4 5.0 %collective-permute-start.20 = (bf16[32,640]{1,0:T(8,128)(2,1)S(1)}, bf16[32,640]{1,0:T(8,128)(2,1)S(1)}, u32[]{:S(2)}, u32[]{:S(2)}) collective-permute-start(bf16[32,640]{1,0:T(8,128)(2,1)S(1)} %get-tuple-element.102), channel_id=1, source_target_pairs={{0,6},{1,7},{2,4},{3,5},{4,2},{5,3},{6,0},{7,1},{8,14},{9,15},{10,... | collective-permute-start | bytes 122888 | tf_op jit(solution)/shard_map/ppermute | solution.py:24
  53.0 4.0 %collective-permute-start.21 = (bf16[32,640]{1,0:T(8,128)(2,1)S(1)}, bf16[32,640]{1,0:T(8,128)(2,1)S(1)}, u32[]{:S(2)}, u32[]{:S(2)}) collective-permute-start(bf16[32,640]{1,0:T(8,128)(2,1)S(1)} %get-tuple-element.103), channel_id=1, source_target_pairs={{0,2},{1,3},{2,0},{3,1},{4,6},{5,7},{6,4},{7,5},{8,10},{9,11},{10,... | collective-permute-start | bytes 122888 | tf_op jit(solution)/shard_map/ppermute | solution.py:24
  54.1 4.0 %collective-permute-start.22 = (bf16[32,640]{1,0:T(8,128)(2,1)S(1)}, bf16[32,640]{1,0:T(8,128)(2,1)S(1)}, u32[]{:S(2)}, u32[]{:S(2)}) collective-permute-start(bf16[32,640]{1,0:T(8,128)(2,1)S(1)} %get-tuple-element.104), channel_id=1, source_target_pairs={{0,4},{1,5},{2,6},{3,7},{4,0},{5,1},{6,2},{7,3},{8,12},{9,13},{10,... | collective-permute-start | bytes 122888 | tf_op jit(solution)/shard_map/ppermute | solution.py:24
  (6 other events, 55.4 us)

commit v6 on v5

--- a/solution.py
+++ b/solution.py
@@ -484,15 +484,16 @@
     back, back_sib = call(backward_kernel, (plane, plane), "backward", micros=1)(
         emit, *held, *wts
     )
+    back, u_chain = lax.optimization_barrier((back, u_chain))
     own, *sends = call(
         second_kernel,
         (shape((2 * batch, states), F32),) + (shape((2 * batch, states), BF16),) * 3,
         "second",
         micros=1,
     )(u1, u1_sib, u_chain, *wts)
-    back_sib, own = lax.optimization_barrier((back_sib, own))
+    received = [across(s, shift) for shift, s in zip(SHIFTS, sends)]
+    back, back_sib, own, received[0] = lax.optimization_barrier((back, back_sib, own, received[0]))
     back_sib = across(back_sib, 1)
-    received = [across(s, shift) for shift, s in zip(SHIFTS, sends)]
     g2, chain, msg2, pack = call(combine_kernel, (plane, plane, message, lanes), "combine")(
         own,
         *received,

time: 59 us -> 58.5 us (level)
  transfers between devices with their start and end apart: 23 -> 23, of which waited for: 16 -> 15; matrix products, arithmetic and copies ran while one was open for 0% -> 0% of each run, Pallas kernels for 22% -> 22%
where the time goes in v6:
time: 58.5 us; the launch traced here: 58.4 us
  starting transfers between devices  24.8 us (42%)
  waiting for transfers between devices  16.9 us (29%)
  Pallas kernels  15.9 us (27%)
  between operations  0.79 us (1%)
    ppermute x23, starting transfers between devices, across(): lax.ppermute(shard, axis, [(i, i ^ apart) for i in range(lax.axis_size(ax...  24.8 us
    ppermute x23, waiting for transfers between devices, across(): lax.ppermute(shard, axis, [(i, i ^ apart) for i in range(lax.axis_size(ax...  16.9 us
    pallas_call x14, Pallas kernels, run(): pl.pallas_call(body, out_shape=out_shape, in_specs=[pl.BlockSpec(memory_s...  15.9 us
  transfers between devices with their start and end apart: 23, of which 15 were waited for; matrix products, arithmetic and copies ran while one was open for 0% of the time, Pallas kernels for 22%

profile of v6, /device:TPU:0, one launch (start us, length us, event | category | flops | bytes accessed | tf_op | source)
XLA Modules:
  0.0 58.4 jit_solution(8080248136443806587)
XLA Ops:
  1.2 1.3 %halves.1 = (bf16[256,512]{1,0:T(8,128)(2,1)S(1)}, bf16[256,512]{1,0:T(8,128)(2,1)S(1)}) custom-call(bf16[512,512]{1,0:T(8,128)(2,1)} %emb_hbm.1), custom_call_target="tpu_custom_call" | custom-call | flops 6000000000 | bytes 18000000 | tf_op jit(solution)/shard_map/halves/pallas_call | solution.py:32
  2.5 2.5 %collective-permute-start.4 = (bf16[256,512]{1,0:T(8,128)(2,1)S(1)}, bf16[256,512]{1,0:T(8,128)(2,1)S(1)}, u32[]{:S(2)}, u32[]{:S(2)}) collective-permute-start(bf16[256,512]{1,0:T(8,128)(2,1)S(1)} %get-tuple-element.60.refs_0_.refs_2_), channel_id=1, source_target_pairs={{0,4},{1,5},{2,6},{3,7},{4,0},{5,1},{6,2},{7,3},{8,12},{9,13},{10,... | collective-permute-start | bytes 786440 | tf_op jit(solution)/shard_map/ppermute | solution.py:24
  5.1 1.5 %collective-permute-start.6 = (bf16[256,512]{1,0:T(8,128)(2,1)S(1)}, bf16[256,512]{1,0:T(8,128)(2,1)S(1)}, u32[]{:S(2)}, u32[]{:S(2)}) collective-permute-start(bf16[256,512]{1,0:T(8,128)(2,1)S(1)} %get-tuple-element.61.refs_1_.refs_3_), channel_id=1, source_target_pairs={{0,2},{1,3},{2,0},{3,1},{4,6},{5,7},{6,4},{7,5},{8,10},{9,11},{10,... | collective-permute-start | bytes 786440 | tf_op jit(solution)/shard_map/ppermute | solution.py:24
  7.2 4.1 %emission.1 = (f32[1,512]{1,0:T(1,128)S(1)}, f32[128,512]{1,0:T(8,128)S(1)}, f32[64,640]{1,0:T(8,128)S(1)}, f32[32,128]{1,0:T(8,128)S(1)}) custom-call(bf16[256,512]{1,0:T(8,128)(2,1)S(1)} %get-tuple-element.60.refs_0_.refs_2_, bf16[256,512]{1,0:T(8,128)(2,1)S(1)} %get-tuple-element.61.refs_1_.refs_3_, bf16[512,512]{1,0:T(8,128)(2,1)S(1)} %copy-done.1, ...), custom_call_target="tpu_custom_call" | custom-call | flops 500000000 | bytes 1500000 | tf_op jit(solution)/shard_map/emission/pallas_call | solution.py:32
  12.2 2.0 %collective-permute-start.5 = (bf16[256,512]{1,0:T(8,128)(2,1)S(1)}, bf16[256,512]{1,0:T(8,128)(2,1)S(1)}, u32[]{:S(2)}, u32[]{:S(2)}) collective-permute-start(bf16[256,512]{1,0:T(8,128)(2,1)S(1)} %collective-permute-done.4.refs_6_), channel_id=1, source_target_pairs={{0,2},{1,3},{2,0},{3,1},{4,6},{5,7},{6,4},{7,5},{8,10},{9,11},{10,... | collective-permute-start | bytes 786440 | tf_op jit(solution)/shard_map/ppermute | solution.py:24
  14.2 1.6 %collective-permute-start.7 = (bf16[256,512]{1,0:T(8,128)(2,1)S(1)}, bf16[256,512]{1,0:T(8,128)(2,1)S(1)}, u32[]{:S(2)}, u32[]{:S(2)}) collective-permute-start(bf16[256,512]{1,0:T(8,128)(2,1)S(1)} %collective-permute-done.6.refs_5_), channel_id=1, source_target_pairs={{0,4},{1,5},{2,6},{3,7},{4,0},{5,1},{6,2},{7,3},{8,12},{9,13},{10,... | collective-permute-start | bytes 786440 | tf_op jit(solution)/shard_map/ppermute | solution.py:24
  15.8 1.7 %sources.1 = (bf16[512,512]{1,0:T(8,128)(2,1)S(1)}, bf16[512,512]{1,0:T(8,128)(2,1)S(1)}, bf16[1024,512]{1,0:T(8,128)(2,1)S(1)}, f32[1024,128]{1,0:T(8,128)S(1)}) custom-call(s32[8,16]{1,0:T(8,128)S(1)} %bitcast.10, bf16[512,512]{1,0:T(8,128)(2,1)S(1)} %copy-done.5, bf16[256,512]{1,0:T(8,128)(2,1)S(1)} %get-tuple-element.60.refs_0_.refs_2_, ...), custom_call_target="tpu_custom_call" | custom-call | flops 1500000000 | bytes 4500000 | tf_op jit(solution)/shard_map/sources/pallas_call | solution.py:32
  17.5 2.3 %collective-permute-done.refs_4_ = bf16[256,512]{1,0:T(8,128)(2,1)S(1)} collective-permute-done((bf16[256,512]{1,0:T(8,128)(2,1)S(1)}, bf16[256,512]{1,0:T(8,128)(2,1)S(1)}, u32[]{:S(2)}, u32[]{:S(2)}) %collective-permute-start) | collective-permute-done | bytes 262176 | tf_op jit(solution)/shard_map/ppermute | solution.py:24
  19.8 2.3 %weights.2 = (bf16[1024,512]{1,0:T(8,128)(2,1)S(1)}, bf16[1024,512]{1,0:T(8,128)(2,1)S(1)}, f32[1024,128]{1,0:T(8,128)S(1)}) custom-call(s32[8,16]{1,0:T(8,128)S(1)} %bitcast.11, bf16[512,512]{1,0:T(8,128)(2,1)S(1)} %copy-done.5, bf16[512,512]{1,0:T(8,128)(2,1)S(1)} %get-tuple-element.69.refs_2_, bf16[512,512]{1,0:T(8,128)(2,1)S(1)} %get-tuple-element.70.refs_3_, ...), custom_call_target="tpu_custom_call" | custom-call | flops 2000000000 | bytes 6000000 | tf_op jit(solution)/shard_map/weights/pallas_call | solution.py:32
  22.1 2.7 %collective-permute-start.9 = (f32[32,128]{1,0:T(8,128)S(1)}, f32[32,128]{1,0:T(8,128)S(1)}, u32[]{:S(2)}, u32[]{:S(2)}) collective-permute-start(f32[32,128]{1,0:T(8,128)S(1)} %slice_add_fusion), channel_id=1, source_target_pairs={{0,8},{1,9},{2,10},{3,11},{4,12},{5,13},{6,14},{7,15},{8,0},{9,1},... | collective-permute-start | bytes 49160 | tf_op jit(solution)/shard_map/ppermute | solution.py:24
  25.0 1.3 %weights.3 = (bf16[1024,512]{1,0:T(8,128)(2,1)S(1)}, f32[1,1024]{1,0:T(1,128)S(1)}) custom-call(s32[8,16]{1,0:T(8,128)S(1)} %bitcast.12, bf16[512,512]{1,0:T(8,128)(2,1)S(1)} %copy-done.5, bf16[512,512]{1,0:T(8,128)(2,1)S(1)} %get-tuple-element.69.refs_2_, bf16[512,512]{1,0:T(8,128)(2,1)S(1)} %get-tuple-element.70.refs_3_, ...), custom_call_target="tpu_custom_call" | custom-call | flops 1500000000 | bytes 4500000 | tf_op jit(solution)/shard_map/weights/pallas_call | solution.py:32
  28.3 1.4 %collective-permute-start.10 = (bf16[64,640]{1,0:T(8,128)(2,1)S(1)}, bf16[64,640]{1,0:T(8,128)(2,1)S(1)}, u32[]{:S(2)}, u32[]{:S(2)}) collective-permute-start(bf16[64,640]{1,0:T(8,128)(2,1)S(1)} %get-tuple-element.79), channel_id=1, source_target_pairs={{0,6},{1,7},{2,4},{3,5},{4,2},{5,3},{6,0},{7,1},{8,14},{9,15},{10,... | collective-permute-start | bytes 245768 | tf_op jit(solution)/shard_map/ppermute | solution.py:24
  30.1 1.7 %collective-permute-start.12 = (bf16[64,640]{1,0:T(8,128)(2,1)S(1)}, bf16[64,640]{1,0:T(8,128)(2,1)S(1)}, u32[]{:S(2)}, u32[]{:S(2)}) collective-permute-start(bf16[64,640]{1,0:T(8,128)(2,1)S(1)} %get-tuple-element.81), channel_id=1, source_target_pairs={{0,4},{1,5},{2,6},{3,7},{4,0},{5,1},{6,2},{7,3},{8,12},{9,13},{10,... | collective-permute-start | bytes 245768 | tf_op jit(solution)/shard_map/ppermute | solution.py:24
  31.8 2.3 %collective-permute-done.10.r1 = bf16[64,640]{1,0:T(8,128)(2,1)S(1)} collective-permute-done((bf16[64,640]{1,0:T(8,128)(2,1)S(1)}, bf16[64,640]{1,0:T(8,128)(2,1)S(1)}, u32[]{:S(2)}, u32[]{:S(2)}) %collective-permute-start.10) | collective-permute-done | bytes 81952 | tf_op jit(solution)/shard_map/ppermute | solution.py:24
  34.1 1.4 %collective-permute-done.11.r2 = bf16[64,640]{1,0:T(8,128)(2,1)S(1)} collective-permute-done((bf16[64,640]{1,0:T(8,128)(2,1)S(1)}, bf16[64,640]{1,0:T(8,128)(2,1)S(1)}, u32[]{:S(2)}, u32[]{:S(2)}) %collective-permute-start.11) | collective-permute-done | bytes 81952 | tf_op jit(solution)/shard_map/ppermute | solution.py:24
  35.8 1.3 %backward.1 = (f32[32,512]{1,0:T(8,128)S(1)}, f32[32,512]{1,0:T(8,128)S(1)}) custom-call(f32[128,512]{1,0:T(8,128)S(1)} %get-tuple-element.62.emit, bf16[64,640]{1,0:T(8,128)(2,1)S(1)} %collective-permute-done.10.r1, bf16[64,640]{1,0:T(8,128)(2,1)S(1)} %collective-permute-done.11.r2, bf16[64,640]{1,0:T(8,128)(2,1)S(1)} %collective-permute-done.12.r3, ...), custom_call_target="tpu_custom_call" | custom-call | flops 1000000000 | bytes 3000000 | tf_op jit(solution)/shard_map/backward/pallas_call | solution.py:32
  38.0 1.7 %collective-permute-start.14 = (bf16[64,512]{1,0:T(8,128)(2,1)S(1)}, bf16[64,512]{1,0:T(8,128)(2,1)S(1)}, u32[]{:S(2)}, u32[]{:S(2)}) collective-permute-start(bf16[64,512]{1,0:T(8,128)(2,1)S(1)} %get-tuple-element.95), channel_id=1, source_target_pairs={{0,6},{1,7},{2,4},{3,5},{4,2},{5,3},{6,0},{7,1},{8,14},{9,15},{10,... | collective-permute-start | bytes 196616 | tf_op jit(solution)/shard_map/ppermute | solution.py:24
  40.2 1.3 %collective-permute-start.16 = (bf16[64,512]{1,0:T(8,128)(2,1)S(1)}, bf16[64,512]{1,0:T(8,128)(2,1)S(1)}, u32[]{:S(2)}, u32[]{:S(2)}) collective-permute-start(bf16[64,512]{1,0:T(8,128)(2,1)S(1)} %get-tuple-element.99), channel_id=1, source_target_pairs={{0,4},{1,5},{2,6},{3,7},{4,0},{5,1},{6,2},{7,3},{8,12},{9,13},{10,... | collective-permute-start | bytes 196616 | tf_op jit(solution)/shard_map/ppermute | solution.py:24
  41.5 2.0 %collective-permute-done.14.r1 = bf16[64,512]{1,0:T(8,128)(2,1)S(1)} collective-permute-done((bf16[64,512]{1,0:T(8,128)(2,1)S(1)}, bf16[64,512]{1,0:T(8,128)(2,1)S(1)}, u32[]{:S(2)}, u32[]{:S(2)}) %collective-permute-start.14) | collective-permute-done | bytes 65568 | tf_op jit(solution)/shard_map/ppermute | solution.py:24
  43.5 1.3 %collective-permute-done.15.r2 = bf16[64,512]{1,0:T(8,128)(2,1)S(1)} collective-permute-done((bf16[64,512]{1,0:T(8,128)(2,1)S(1)}, bf16[64,512]{1,0:T(8,128)(2,1)S(1)}, u32[]{:S(2)}, u32[]{:S(2)}) %collective-permute-start.15) | collective-permute-done | bytes 65568 | tf_op jit(solution)/shard_map/ppermute | solution.py:24
  46.4 2.6 %collective-permute-start.19 = (f32[32,128]{1,0:T(8,128)S(1)}, f32[32,128]{1,0:T(8,128)S(1)}, u32[]{:S(2)}, u32[]{:S(2)}) collective-permute-start(f32[32,128]{1,0:T(8,128)S(1)} %totals.1.here), channel_id=1, source_target_pairs={{0,8},{1,9},{2,10},{3,11},{4,12},{5,13},{6,14},{7,15},{8,0},{9,1},... | collective-permute-start | bytes 49160 | tf_op jit(solution)/shard_map/ppermute | solution.py:24
  49.9 1.2 %collective-permute-done.19.other = f32[32,128]{1,0:T(8,128)S(1)} collective-permute-done((f32[32,128]{1,0:T(8,128)S(1)}, f32[32,128]{1,0:T(8,128)S(1)}, u32[]{:S(2)}, u32[]{:S(2)}) %collective-permute-start.19) | collective-permute-done | bytes 16416 | tf_op jit(solution)/shard_map/ppermute | solution.py:24
  51.1 1.7 %collective-permute-start.20 = (bf16[32,640]{1,0:T(8,128)(2,1)S(1)}, bf16[32,640]{1,0:T(8,128)(2,1)S(1)}, u32[]{:S(2)}, u32[]{:S(2)}) collective-permute-start(bf16[32,640]{1,0:T(8,128)(2,1)S(1)} %get-tuple-element.110), channel_id=1, source_target_pairs={{0,6},{1,7},{2,4},{3,5},{4,2},{5,3},{6,0},{7,1},{8,14},{9,15},{10,... | collective-permute-start | bytes 122888 | tf_op jit(solution)/shard_map/ppermute | solution.py:24
  54.6 1.6 %collective-permute-done.20.r1 = bf16[32,640]{1,0:T(8,128)(2,1)S(1)} collective-permute-done((bf16[32,640]{1,0:T(8,128)(2,1)S(1)}, bf16[32,640]{1,0:T(8,128)(2,1)S(1)}, u32[]{:S(2)}, u32[]{:S(2)}) %collective-permute-start.20) | collective-permute-done | bytes 40992 | tf_op jit(solution)/shard_map/ppermute | solution.py:24
  (52 shorter events, 13.0 us)
Async XLA Ops:
  0.7 15.1 %collective-permute-start.2 = (bf16[512,512]{1,0:T(8,128)(2,1)}, bf16[512,512]{1,0:T(8,128)(2,1)S(1)}, u32[]{:S(2)}, u32[]{:S(2)}) collective-permute-start(bf16[512,512]{1,0:T(8,128)(2,1)} %emb_hbm.1), channel_id=1, source_target_pairs={{0,1},{1,0},{2,3},{3,2},{4,5},{5,4},{6,7},{7,6},{8,9},{9,8},{10,11... | collective-permute-start | bytes 1572872 | tf_op jit(solution)/shard_map/ppermute | solution.py:24
  2.5 13.3 %copy-start.4 = (bf16[512,512]{1,0:T(8,128)(2,1)S(1)}, bf16[512,512]{1,0:T(8,128)(2,1)}, u32[]{:S(2)}) copy-start(bf16[512,512]{1,0:T(8,128)(2,1)} %refs_5_.3) | copy-start | bytes 1572868
  2.5 9.7 %collective-permute-start.4 = (bf16[256,512]{1,0:T(8,128)(2,1)S(1)}, bf16[256,512]{1,0:T(8,128)(2,1)S(1)}, u32[]{:S(2)}, u32[]{:S(2)}) collective-permute-start(bf16[256,512]{1,0:T(8,128)(2,1)S(1)} %get-tuple-element.60.refs_0_.refs_2_), channel_id=1, source_target_pairs={{0,4},{1,5},{2,6},{3,7},{4,0},{5,1},{6,2},{7,3},{8,12},{9,13},{10,... | collective-permute-start | bytes 786440 | tf_op jit(solution)/shard_map/ppermute | solution.py:24
  5.1 9.1 %collective-permute-start.6 = (bf16[256,512]{1,0:T(8,128)(2,1)S(1)}, bf16[256,512]{1,0:T(8,128)(2,1)S(1)}, u32[]{:S(2)}, u32[]{:S(2)}) collective-permute-start(bf16[256,512]{1,0:T(8,128)(2,1)S(1)} %get-tuple-element.61.refs_1_.refs_3_), channel_id=1, source_target_pairs={{0,2},{1,3},{2,0},{3,1},{4,6},{5,7},{6,4},{7,5},{8,10},{9,11},{10,... | collective-permute-start | bytes 786440 | tf_op jit(solution)/shard_map/ppermute | solution.py:24
  6.6 13.2 %collective-permute-start = (bf16[256,512]{1,0:T(8,128)(2,1)S(1)}, bf16[256,512]{1,0:T(8,128)(2,1)S(1)}, u32[]{:S(2)}, u32[]{:S(2)}) collective-permute-start(bf16[256,512]{1,0:T(8,128)(2,1)S(1)} %get-tuple-element.60.refs_0_.refs_2_), channel_id=1, source_target_pairs={{0,2},{1,3},{2,0},{3,1},{4,6},{5,7},{6,4},{7,5},{8,10},{9,11},{10,... | collective-permute-start | bytes 786440 | tf_op jit(solution)/shard_map/ppermute | solution.py:24
  7.1 12.7 %collective-permute-start.1 = (bf16[256,512]{1,0:T(8,128)(2,1)S(1)}, bf16[256,512]{1,0:T(8,128)(2,1)S(1)}, u32[]{:S(2)}, u32[]{:S(2)}) collective-permute-start(bf16[256,512]{1,0:T(8,128)(2,1)S(1)} %get-tuple-element.61.refs_1_.refs_3_), channel_id=1, source_target_pairs={{0,4},{1,5},{2,6},{3,7},{4,0},{5,1},{6,2},{7,3},{8,12},{9,13},{10,... | collective-permute-start | bytes 786440 | tf_op jit(solution)/shard_map/ppermute | solution.py:24
  12.2 12.8 %collective-permute-start.5 = (bf16[256,512]{1,0:T(8,128)(2,1)S(1)}, bf16[256,512]{1,0:T(8,128)(2,1)S(1)}, u32[]{:S(2)}, u32[]{:S(2)}) collective-permute-start(bf16[256,512]{1,0:T(8,128)(2,1)S(1)} %collective-permute-done.4.refs_6_), channel_id=1, source_target_pairs={{0,2},{1,3},{2,0},{3,1},{4,6},{5,7},{6,4},{7,5},{8,10},{9,11},{10,... | collective-permute-start | bytes 786440 | tf_op jit(solution)/shard_map/ppermute | solution.py:24
  14.2 10.8 %collective-permute-start.7 = (bf16[256,512]{1,0:T(8,128)(2,1)S(1)}, bf16[256,512]{1,0:T(8,128)(2,1)S(1)}, u32[]{:S(2)}, u32[]{:S(2)}) collective-permute-start(bf16[256,512]{1,0:T(8,128)(2,1)S(1)} %collective-permute-done.6.refs_5_), channel_id=1, source_target_pairs={{0,4},{1,5},{2,6},{3,7},{4,0},{5,1},{6,2},{7,3},{8,12},{9,13},{10,... | collective-permute-start | bytes 786440 | tf_op jit(solution)/shard_map/ppermute | solution.py:24
  19.8 2.3 %collective-permute-start.3 = (f32[64,640]{1,0:T(8,128)S(1)}, f32[64,640]{1,0:T(8,128)S(1)}, u32[]{:S(2)}, u32[]{:S(2)}) collective-permute-start(f32[64,640]{1,0:T(8,128)S(1)} %get-tuple-element.68.msg_a), channel_id=1, source_target_pairs={{0,1},{1,0},{2,3},{3,2},{4,5},{5,4},{6,7},{7,6},{8,9},{9,8},{10,11... | collective-permute-start | bytes 491528 | tf_op jit(solution)/shard_map/ppermute | solution.py:24
  22.1 4.7 %collective-permute-start.9 = (f32[32,128]{1,0:T(8,128)S(1)}, f32[32,128]{1,0:T(8,128)S(1)}, u32[]{:S(2)}, u32[]{:S(2)}) collective-permute-start(f32[32,128]{1,0:T(8,128)S(1)} %slice_add_fusion), channel_id=1, source_target_pairs={{0,8},{1,9},{2,10},{3,11},{4,12},{5,13},{6,14},{7,15},{8,0},{9,1},... | collective-permute-start | bytes 49160 | tf_op jit(solution)/shard_map/ppermute | solution.py:24
  26.2 1.2 %collective-permute-start.8 = (f32[1,1024]{1,0:T(1,128)S(1)}, f32[1,1024]{1,0:T(1,128)S(1)}, u32[]{:S(2)}, u32[]{:S(2)}) collective-permute-start(f32[1,1024]{1,0:T(1,128)S(1)} %get-tuple-element.73.sums_own), channel_id=1, source_target_pairs={{0,1},{1,0},{2,3},{3,2},{4,5},{5,4},{6,7},{7,6},{8,9},{9,8},{10,11... | collective-permute-start | bytes 12296 | tf_op jit(solution)/shard_map/ppermute | solution.py:24
  28.3 5.8 %collective-permute-start.10 = (bf16[64,640]{1,0:T(8,128)(2,1)S(1)}, bf16[64,640]{1,0:T(8,128)(2,1)S(1)}, u32[]{:S(2)}, u32[]{:S(2)}) collective-permute-start(bf16[64,640]{1,0:T(8,128)(2,1)S(1)} %get-tuple-element.79), channel_id=1, source_target_pairs={{0,6},{1,7},{2,4},{3,5},{4,2},{5,3},{6,0},{7,1},{8,14},{9,15},{10,... | collective-permute-start | bytes 245768 | tf_op jit(solution)/shard_map/ppermute | solution.py:24
  29.7 5.8 %collective-permute-start.11 = (bf16[64,640]{1,0:T(8,128)(2,1)S(1)}, bf16[64,640]{1,0:T(8,128)(2,1)S(1)}, u32[]{:S(2)}, u32[]{:S(2)}) collective-permute-start(bf16[64,640]{1,0:T(8,128)(2,1)S(1)} %get-tuple-element.80), channel_id=1, source_target_pairs={{0,2},{1,3},{2,0},{3,1},{4,6},{5,7},{6,4},{7,5},{8,10},{9,11},{10,... | collective-permute-start | bytes 245768 | tf_op jit(solution)/shard_map/ppermute | solution.py:24
  30.1 5.4 %collective-permute-start.12 = (bf16[64,640]{1,0:T(8,128)(2,1)S(1)}, bf16[64,640]{1,0:T(8,128)(2,1)S(1)}, u32[]{:S(2)}, u32[]{:S(2)}) collective-permute-start(bf16[64,640]{1,0:T(8,128)(2,1)S(1)} %get-tuple-element.81), channel_id=1, source_target_pairs={{0,4},{1,5},{2,6},{3,7},{4,0},{5,1},{6,2},{7,3},{8,12},{9,13},{10,... | collective-permute-start | bytes 245768 | tf_op jit(solution)/shard_map/ppermute | solution.py:24
  35.8 1.4 %collective-permute-start.13 = (bf16[32,512]{1,0:T(8,128)(2,1)S(1)}, bf16[32,512]{1,0:T(8,128)(2,1)S(1)}, u32[]{:S(2)}, u32[]{:S(2)}) collective-permute-start(bf16[32,512]{1,0:T(8,128)(2,1)S(1)} %get-tuple-element.85.u_a), channel_id=1, source_target_pairs={{0,1},{1,0},{2,3},{3,2},{4,5},{5,4},{6,7},{7,6},{8,9},{9,8},{10,11... | collective-permute-start | bytes 98312 | tf_op jit(solution)/shard_map/ppermute | solution.py:24
  38.0 5.6 %collective-permute-start.14 = (bf16[64,512]{1,0:T(8,128)(2,1)S(1)}, bf16[64,512]{1,0:T(8,128)(2,1)S(1)}, u32[]{:S(2)}, u32[]{:S(2)}) collective-permute-start(bf16[64,512]{1,0:T(8,128)(2,1)S(1)} %get-tuple-element.95), channel_id=1, source_target_pairs={{0,6},{1,7},{2,4},{3,5},{4,2},{5,3},{6,0},{7,1},{8,14},{9,15},{10,... | collective-permute-start | bytes 196616 | tf_op jit(solution)/shard_map/ppermute | solution.py:24
  39.7 5.1 %collective-permute-start.15 = (bf16[64,512]{1,0:T(8,128)(2,1)S(1)}, bf16[64,512]{1,0:T(8,128)(2,1)S(1)}, u32[]{:S(2)}, u32[]{:S(2)}) collective-permute-start(bf16[64,512]{1,0:T(8,128)(2,1)S(1)} %get-tuple-element.98), channel_id=1, source_target_pairs={{0,2},{1,3},{2,0},{3,1},{4,6},{5,7},{6,4},{7,5},{8,10},{9,11},{10,... | collective-permute-start | bytes 196616 | tf_op jit(solution)/shard_map/ppermute | solution.py:24
  40.2 4.6 %collective-permute-start.16 = (bf16[64,512]{1,0:T(8,128)(2,1)S(1)}, bf16[64,512]{1,0:T(8,128)(2,1)S(1)}, u32[]{:S(2)}, u32[]{:S(2)}) collective-permute-start(bf16[64,512]{1,0:T(8,128)(2,1)S(1)} %get-tuple-element.99), channel_id=1, source_target_pairs={{0,4},{1,5},{2,6},{3,7},{4,0},{5,1},{6,2},{7,3},{8,12},{9,13},{10,... | collective-permute-start | bytes 196616 | tf_op jit(solution)/shard_map/ppermute | solution.py:24
  43.5 1.3 %collective-permute-start.17 = (f32[32,512]{1,0:T(8,128)S(1)}, f32[32,512]{1,0:T(8,128)S(1)}, u32[]{:S(2)}, u32[]{:S(2)}) collective-permute-start(f32[32,512]{1,0:T(8,128)S(1)} %get-tuple-element.103), channel_id=1, source_target_pairs={{0,1},{1,0},{2,3},{3,2},{4,5},{5,4},{6,7},{7,6},{8,9},{9,8},{10,11... | collective-permute-start | bytes 196616 | tf_op jit(solution)/shard_map/ppermute | solution.py:24
  45.1 1.2 %collective-permute-start.18 = (bf16[32,640]{1,0:T(8,128)(2,1)S(1)}, bf16[32,640]{1,0:T(8,128)(2,1)S(1)}, u32[]{:S(2)}, u32[]{:S(2)}) collective-permute-start(bf16[32,640]{1,0:T(8,128)(2,1)S(1)} %get-tuple-element.104.u_a), channel_id=1, source_target_pairs={{0,1},{1,0},{2,3},{3,2},{4,5},{5,4},{6,7},{7,6},{8,9},{9,8},{10,11... | collective-permute-start | bytes 122888 | tf_op jit(solution)/shard_map/ppermute | solution.py:24
  46.4 4.6 %collective-permute-start.19 = (f32[32,128]{1,0:T(8,128)S(1)}, f32[32,128]{1,0:T(8,128)S(1)}, u32[]{:S(2)}, u32[]{:S(2)}) collective-permute-start(f32[32,128]{1,0:T(8,128)S(1)} %totals.1.here), channel_id=1, source_target_pairs={{0,8},{1,9},{2,10},{3,11},{4,12},{5,13},{6,14},{7,15},{8,0},{9,1},... | collective-permute-start | bytes 49160 | tf_op jit(solution)/shard_map/ppermute | solution.py:24
  51.1 5.1 %collective-permute-start.20 = (bf16[32,640]{1,0:T(8,128)(2,1)S(1)}, bf16[32,640]{1,0:T(8,128)(2,1)S(1)}, u32[]{:S(2)}, u32[]{:S(2)}) collective-permute-start(bf16[32,640]{1,0:T(8,128)(2,1)S(1)} %get-tuple-element.110), channel_id=1, source_target_pairs={{0,6},{1,7},{2,4},{3,5},{4,2},{5,3},{6,0},{7,1},{8,14},{9,15},{10,... | collective-permute-start | bytes 122888 | tf_op jit(solution)/shard_map/ppermute | solution.py:24
  52.8 4.0 %collective-permute-start.21 = (bf16[32,640]{1,0:T(8,128)(2,1)S(1)}, bf16[32,640]{1,0:T(8,128)(2,1)S(1)}, u32[]{:S(2)}, u32[]{:S(2)}) collective-permute-start(bf16[32,640]{1,0:T(8,128)(2,1)S(1)} %get-tuple-element.111), channel_id=1, source_target_pairs={{0,2},{1,3},{2,0},{3,1},{4,6},{5,7},{6,4},{7,5},{8,10},{9,11},{10,... | collective-permute-start | bytes 122888 | tf_op jit(solution)/shard_map/ppermute | solution.py:24
  53.6 4.0 %collective-permute-start.22 = (bf16[32,640]{1,0:T(8,128)(2,1)S(1)}, bf16[32,640]{1,0:T(8,128)(2,1)S(1)}, u32[]{:S(2)}, u32[]{:S(2)}) collective-permute-start(bf16[32,640]{1,0:T(8,128)(2,1)S(1)} %get-tuple-element.112), channel_id=1, source_target_pairs={{0,4},{1,5},{2,6},{3,7},{4,0},{5,1},{6,2},{7,3},{8,12},{9,13},{10,... | collective-permute-start | bytes 122888 | tf_op jit(solution)/shard_map/ppermute | solution.py:24
  (6 other events, 55.2 us)

commit v7 on v6

--- a/solution.py
+++ b/solution.py
@@ -174,6 +174,10 @@
     weights_kernel(scale, (0,), mask, to_w, from_a, from_b, top, bottom, out, sum_out)
 
 
+def target_kernel(block, to_w, out):
+    out[...] = dot(block[...], to_w[...], NN).astype(BF16)
+
+
 def weights_kernel(scale, shifts, mask, to_w, from_a, from_b, *refs):
     states = from_a.shape[0]
     count = len(shifts)
@@ -183,7 +187,10 @@
     at_place = lax.broadcasted_iota(jnp.int32, mask.shape, 0)
     at_col = lax.broadcasted_iota(jnp.int32, mask.shape, 1)
     tile = states // 2
-    targets = [dot(block[...], to_w[...], NN).astype(BF16) for block in blocks]
+    if shifts == (6,):
+        targets = [block[...] for block in blocks]
+    else:
+        targets = [dot(block[...], to_w[...], NN).astype(BF16) for block in blocks]
     for side, source in ((0, from_a), (1, from_b)):
         rows = slice(side * states, (side + 1) * states)
         sums = before[0][rows, :] if before else jnp.zeros((states, 128), F32)
@@ -441,8 +448,8 @@
         "sources",
         micros=1.5,
     )(block_mask.T, to_weight, top, bottom, sib, from_weight)
-    d_top = across(z_top, 2)
-    d_bottom = across(y_bottom, 4)
+    d_top = across(call(target_kernel, half_block, "target")(z_top, to_weight), 2)
+    d_bottom = across(call(target_kernel, half_block, "target")(y_bottom, to_weight), 4)
     y_top, z_bottom, sums0 = lax.optimization_barrier((y_top, z_bottom, sums0))
     msg, mass_own, *_ = lax.optimization_barrier((msg, mass_own, y_top, z_bottom))
     msg_sib = across(msg, 1)

time: 58.5 us -> 58.4 us (level)
  waiting for transfers between devices: 16.9 us -> 16.1 us
    ppermute x23, waiting for transfers between devices: 16.9 us -> 16.1 us  [across(): lax.ppermute(shard, axis, [(i, i ^ apart) for i in range(lax.axis_size(ax...]
    pallas_call x14 -> x16, Pallas kernels: 15.9 us -> 16.3 us  [run(): pl.pallas_call(body, out_shape=out_shape, in_specs=[pl.BlockSpec(memory_s...]
  transfers between devices with their start and end apart: 23 -> 23, of which waited for: 15 -> 15; matrix products, arithmetic and copies ran while one was open for 0% -> 0% of each run, Pallas kernels for 22% -> 23%
where the time goes in v7:
time: 58.4 us; the launch traced here: 58.2 us
  starting transfers between devices  24.9 us (43%)
  Pallas kernels  16.3 us (28%)
  waiting for transfers between devices  16.1 us (28%)
  between operations  0.8 us (1%)
    ppermute x23, starting transfers between devices, across(): lax.ppermute(shard, axis, [(i, i ^ apart) for i in range(lax.axis_size(ax...  24.9 us
    pallas_call x16, Pallas kernels, run(): pl.pallas_call(body, out_shape=out_shape, in_specs=[pl.BlockSpec(memory_s...  16.3 us
    ppermute x23, waiting for transfers between devices, across(): lax.ppermute(shard, axis, [(i, i ^ apart) for i in range(lax.axis_size(ax...  16.1 us
  transfers between devices with their start and end apart: 23, of which 15 were waited for; matrix products, arithmetic and copies ran while one was open for 0% of the time, Pallas kernels for 23%

profile of v7, /device:TPU:0, one launch (start us, length us, event | category | flops | bytes accessed | tf_op | source)
XLA Modules:
  0.0 58.2 jit_solution(8283818884646443446)
XLA Ops:
  1.2 1.3 %halves.1 = (bf16[256,512]{1,0:T(8,128)(2,1)S(1)}, bf16[256,512]{1,0:T(8,128)(2,1)S(1)}) custom-call(bf16[512,512]{1,0:T(8,128)(2,1)} %emb_hbm.1), custom_call_target="tpu_custom_call" | custom-call | flops 6000000000 | bytes 18000000 | tf_op jit(solution)/shard_map/halves/pallas_call | solution.py:32
  2.5 2.5 %collective-permute-start.4 = (bf16[256,512]{1,0:T(8,128)(2,1)S(1)}, bf16[256,512]{1,0:T(8,128)(2,1)S(1)}, u32[]{:S(2)}, u32[]{:S(2)}) collective-permute-start(bf16[256,512]{1,0:T(8,128)(2,1)S(1)} %get-tuple-element.60.refs_0_.refs_2_), channel_id=1, source_target_pairs={{0,4},{1,5},{2,6},{3,7},{4,0},{5,1},{6,2},{7,3},{8,12},{9,13},{10,... | collective-permute-start | bytes 786440 | tf_op jit(solution)/shard_map/ppermute | solution.py:24
  5.1 1.5 %collective-permute-start.6 = (bf16[256,512]{1,0:T(8,128)(2,1)S(1)}, bf16[256,512]{1,0:T(8,128)(2,1)S(1)}, u32[]{:S(2)}, u32[]{:S(2)}) collective-permute-start(bf16[256,512]{1,0:T(8,128)(2,1)S(1)} %get-tuple-element.61.refs_1_.refs_3_), channel_id=1, source_target_pairs={{0,2},{1,3},{2,0},{3,1},{4,6},{5,7},{6,4},{7,5},{8,10},{9,11},{10,... | collective-permute-start | bytes 786440 | tf_op jit(solution)/shard_map/ppermute | solution.py:24
  7.2 4.1 %emission.1 = (f32[1,512]{1,0:T(1,128)S(1)}, f32[128,512]{1,0:T(8,128)S(1)}, f32[64,640]{1,0:T(8,128)S(1)}, f32[32,128]{1,0:T(8,128)S(1)}) custom-call(bf16[256,512]{1,0:T(8,128)(2,1)S(1)} %get-tuple-element.60.refs_0_.refs_2_, bf16[256,512]{1,0:T(8,128)(2,1)S(1)} %get-tuple-element.61.refs_1_.refs_3_, bf16[512,512]{1,0:T(8,128)(2,1)S(1)} %copy-done.2, ...), custom_call_target="tpu_custom_call" | custom-call | flops 500000000 | bytes 1500000 | tf_op jit(solution)/shard_map/emission/pallas_call | solution.py:32
  12.5 2.1 %collective-permute-start.5 = (bf16[256,512]{1,0:T(8,128)(2,1)S(1)}, bf16[256,512]{1,0:T(8,128)(2,1)S(1)}, u32[]{:S(2)}, u32[]{:S(2)}) collective-permute-start(bf16[256,512]{1,0:T(8,128)(2,1)S(1)} %target.2), channel_id=1, source_target_pairs={{0,2},{1,3},{2,0},{3,1},{4,6},{5,7},{6,4},{7,5},{8,10},{9,11},{10,... | collective-permute-start | bytes 786440 | tf_op jit(solution)/shard_map/ppermute | solution.py:24
  14.9 1.6 %collective-permute-start.7 = (bf16[256,512]{1,0:T(8,128)(2,1)S(1)}, bf16[256,512]{1,0:T(8,128)(2,1)S(1)}, u32[]{:S(2)}, u32[]{:S(2)}) collective-permute-start(bf16[256,512]{1,0:T(8,128)(2,1)S(1)} %target.3), channel_id=1, source_target_pairs={{0,4},{1,5},{2,6},{3,7},{4,0},{5,1},{6,2},{7,3},{8,12},{9,13},{10,... | collective-permute-start | bytes 786440 | tf_op jit(solution)/shard_map/ppermute | solution.py:24
  16.5 1.7 %sources.1 = (bf16[512,512]{1,0:T(8,128)(2,1)S(1)}, bf16[512,512]{1,0:T(8,128)(2,1)S(1)}, bf16[1024,512]{1,0:T(8,128)(2,1)S(1)}, f32[1024,128]{1,0:T(8,128)S(1)}) custom-call(s32[8,16]{1,0:T(8,128)S(1)} %bitcast.10, bf16[512,512]{1,0:T(8,128)(2,1)S(1)} %copy-done.1, bf16[256,512]{1,0:T(8,128)(2,1)S(1)} %get-tuple-element.60.refs_0_.refs_2_, ...), custom_call_target="tpu_custom_call" | custom-call | flops 1500000000 | bytes 4500000 | tf_op jit(solution)/shard_map/sources/pallas_call | solution.py:32
  18.3 1.5 %collective-permute-done.refs_4_ = bf16[256,512]{1,0:T(8,128)(2,1)S(1)} collective-permute-done((bf16[256,512]{1,0:T(8,128)(2,1)S(1)}, bf16[256,512]{1,0:T(8,128)(2,1)S(1)}, u32[]{:S(2)}, u32[]{:S(2)}) %collective-permute-start) | collective-permute-done | bytes 262176 | tf_op jit(solution)/shard_map/ppermute | solution.py:24
  19.8 2.3 %weights.2 = (bf16[1024,512]{1,0:T(8,128)(2,1)S(1)}, bf16[1024,512]{1,0:T(8,128)(2,1)S(1)}, f32[1024,128]{1,0:T(8,128)S(1)}) custom-call(s32[8,16]{1,0:T(8,128)S(1)} %bitcast.11, bf16[512,512]{1,0:T(8,128)(2,1)S(1)} %copy-done.1, bf16[512,512]{1,0:T(8,128)(2,1)S(1)} %get-tuple-element.69.refs_2_, bf16[512,512]{1,0:T(8,128)(2,1)S(1)} %get-tuple-element.70.refs_3_, ...), custom_call_target="tpu_custom_call" | custom-call | flops 2000000000 | bytes 6000000 | tf_op jit(solution)/shard_map/weights/pallas_call | solution.py:32
  22.1 2.7 %collective-permute-start.9 = (f32[32,128]{1,0:T(8,128)S(1)}, f32[32,128]{1,0:T(8,128)S(1)}, u32[]{:S(2)}, u32[]{:S(2)}) collective-permute-start(f32[32,128]{1,0:T(8,128)S(1)} %slice_add_fusion), channel_id=1, source_target_pairs={{0,8},{1,9},{2,10},{3,11},{4,12},{5,13},{6,14},{7,15},{8,0},{9,1},... | collective-permute-start | bytes 49160 | tf_op jit(solution)/shard_map/ppermute | solution.py:24
  28.1 1.4 %collective-permute-start.10 = (bf16[64,640]{1,0:T(8,128)(2,1)S(1)}, bf16[64,640]{1,0:T(8,128)(2,1)S(1)}, u32[]{:S(2)}, u32[]{:S(2)}) collective-permute-start(bf16[64,640]{1,0:T(8,128)(2,1)S(1)} %get-tuple-element.79), channel_id=1, source_target_pairs={{0,6},{1,7},{2,4},{3,5},{4,2},{5,3},{6,0},{7,1},{8,14},{9,15},{10,... | collective-permute-start | bytes 245768 | tf_op jit(solution)/shard_map/ppermute | solution.py:24
  29.9 1.7 %collective-permute-start.12 = (bf16[64,640]{1,0:T(8,128)(2,1)S(1)}, bf16[64,640]{1,0:T(8,128)(2,1)S(1)}, u32[]{:S(2)}, u32[]{:S(2)}) collective-permute-start(bf16[64,640]{1,0:T(8,128)(2,1)S(1)} %get-tuple-element.81), channel_id=1, source_target_pairs={{0,4},{1,5},{2,6},{3,7},{4,0},{5,1},{6,2},{7,3},{8,12},{9,13},{10,... | collective-permute-start | bytes 245768 | tf_op jit(solution)/shard_map/ppermute | solution.py:24
  31.6 2.3 %collective-permute-done.10.r1 = bf16[64,640]{1,0:T(8,128)(2,1)S(1)} collective-permute-done((bf16[64,640]{1,0:T(8,128)(2,1)S(1)}, bf16[64,640]{1,0:T(8,128)(2,1)S(1)}, u32[]{:S(2)}, u32[]{:S(2)}) %collective-permute-start.10) | collective-permute-done | bytes 81952 | tf_op jit(solution)/shard_map/ppermute | solution.py:24
  33.9 1.3 %collective-permute-done.11.r2 = bf16[64,640]{1,0:T(8,128)(2,1)S(1)} collective-permute-done((bf16[64,640]{1,0:T(8,128)(2,1)S(1)}, bf16[64,640]{1,0:T(8,128)(2,1)S(1)}, u32[]{:S(2)}, u32[]{:S(2)}) %collective-permute-start.11) | collective-permute-done | bytes 81952 | tf_op jit(solution)/shard_map/ppermute | solution.py:24
  35.6 1.3 %backward.1 = (f32[32,512]{1,0:T(8,128)S(1)}, f32[32,512]{1,0:T(8,128)S(1)}) custom-call(f32[128,512]{1,0:T(8,128)S(1)} %get-tuple-element.62.emit, bf16[64,640]{1,0:T(8,128)(2,1)S(1)} %collective-permute-done.10.r1, bf16[64,640]{1,0:T(8,128)(2,1)S(1)} %collective-permute-done.11.r2, bf16[64,640]{1,0:T(8,128)(2,1)S(1)} %collective-permute-done.12.r3, ...), custom_call_target="tpu_custom_call" | custom-call | flops 1000000000 | bytes 3000000 | tf_op jit(solution)/shard_map/backward/pallas_call | solution.py:32
  37.8 1.7 %collective-permute-start.14 = (bf16[64,512]{1,0:T(8,128)(2,1)S(1)}, bf16[64,512]{1,0:T(8,128)(2,1)S(1)}, u32[]{:S(2)}, u32[]{:S(2)}) collective-permute-start(bf16[64,512]{1,0:T(8,128)(2,1)S(1)} %get-tuple-element.95), channel_id=1, source_target_pairs={{0,6},{1,7},{2,4},{3,5},{4,2},{5,3},{6,0},{7,1},{8,14},{9,15},{10,... | collective-permute-start | bytes 196616 | tf_op jit(solution)/shard_map/ppermute | solution.py:24
  40.0 1.3 %collective-permute-start.16 = (bf16[64,512]{1,0:T(8,128)(2,1)S(1)}, bf16[64,512]{1,0:T(8,128)(2,1)S(1)}, u32[]{:S(2)}, u32[]{:S(2)}) collective-permute-start(bf16[64,512]{1,0:T(8,128)(2,1)S(1)} %get-tuple-element.99), channel_id=1, source_target_pairs={{0,4},{1,5},{2,6},{3,7},{4,0},{5,1},{6,2},{7,3},{8,12},{9,13},{10,... | collective-permute-start | bytes 196616 | tf_op jit(solution)/shard_map/ppermute | solution.py:24
  41.4 2.0 %collective-permute-done.14.r1 = bf16[64,512]{1,0:T(8,128)(2,1)S(1)} collective-permute-done((bf16[64,512]{1,0:T(8,128)(2,1)S(1)}, bf16[64,512]{1,0:T(8,128)(2,1)S(1)}, u32[]{:S(2)}, u32[]{:S(2)}) %collective-permute-start.14) | collective-permute-done | bytes 65568 | tf_op jit(solution)/shard_map/ppermute | solution.py:24
  43.4 1.3 %collective-permute-done.15.r2 = bf16[64,512]{1,0:T(8,128)(2,1)S(1)} collective-permute-done((bf16[64,512]{1,0:T(8,128)(2,1)S(1)}, bf16[64,512]{1,0:T(8,128)(2,1)S(1)}, u32[]{:S(2)}, u32[]{:S(2)}) %collective-permute-start.15) | collective-permute-done | bytes 65568 | tf_op jit(solution)/shard_map/ppermute | solution.py:24
  45.0 1.1 %collective-permute-done.18.u_b.msg_sib = bf16[32,640]{1,0:T(8,128)(2,1)S(1)} collective-permute-done((bf16[32,640]{1,0:T(8,128)(2,1)S(1)}, bf16[32,640]{1,0:T(8,128)(2,1)S(1)}, u32[]{:S(2)}, u32[]{:S(2)}) %collective-permute-start.18) | collective-permute-done | bytes 40992 | tf_op jit(solution)/shard_map/ppermute | solution.py:24
  46.2 2.6 %collective-permute-start.19 = (f32[32,128]{1,0:T(8,128)S(1)}, f32[32,128]{1,0:T(8,128)S(1)}, u32[]{:S(2)}, u32[]{:S(2)}) collective-permute-start(f32[32,128]{1,0:T(8,128)S(1)} %totals.1.here), channel_id=1, source_target_pairs={{0,8},{1,9},{2,10},{3,11},{4,12},{5,13},{6,14},{7,15},{8,0},{9,1},... | collective-permute-start | bytes 49160 | tf_op jit(solution)/shard_map/ppermute | solution.py:24
  49.7 1.2 %collective-permute-done.19.other = f32[32,128]{1,0:T(8,128)S(1)} collective-permute-done((f32[32,128]{1,0:T(8,128)S(1)}, f32[32,128]{1,0:T(8,128)S(1)}, u32[]{:S(2)}, u32[]{:S(2)}) %collective-permute-start.19) | collective-permute-done | bytes 16416 | tf_op jit(solution)/shard_map/ppermute | solution.py:24
  51.0 1.7 %collective-permute-start.20 = (bf16[32,640]{1,0:T(8,128)(2,1)S(1)}, bf16[32,640]{1,0:T(8,128)(2,1)S(1)}, u32[]{:S(2)}, u32[]{:S(2)}) collective-permute-start(bf16[32,640]{1,0:T(8,128)(2,1)S(1)} %get-tuple-element.110), channel_id=1, source_target_pairs={{0,6},{1,7},{2,4},{3,5},{4,2},{5,3},{6,0},{7,1},{8,14},{9,15},{10,... | collective-permute-start | bytes 122888 | tf_op jit(solution)/shard_map/ppermute | solution.py:24
  54.5 1.6 %collective-permute-done.20.r1 = bf16[32,640]{1,0:T(8,128)(2,1)S(1)} collective-permute-done((bf16[32,640]{1,0:T(8,128)(2,1)S(1)}, bf16[32,640]{1,0:T(8,128)(2,1)S(1)}, u32[]{:S(2)}, u32[]{:S(2)}) %collective-permute-start.20) | collective-permute-done | bytes 40992 | tf_op jit(solution)/shard_map/ppermute | solution.py:24
  (54 shorter events, 13.5 us)
Async XLA Ops:
  0.7 15.9 %collective-permute-start.2 = (bf16[512,512]{1,0:T(8,128)(2,1)}, bf16[512,512]{1,0:T(8,128)(2,1)S(1)}, u32[]{:S(2)}, u32[]{:S(2)}) collective-permute-start(bf16[512,512]{1,0:T(8,128)(2,1)} %emb_hbm.1), channel_id=1, source_target_pairs={{0,1},{1,0},{2,3},{3,2},{4,5},{5,4},{6,7},{7,6},{8,9},{9,8},{10,11... | collective-permute-start | bytes 1572872 | tf_op jit(solution)/shard_map/ppermute | solution.py:24
  2.5 14.0 %copy-start.5 = (bf16[512,512]{1,0:T(8,128)(2,1)S(1)}, bf16[512,512]{1,0:T(8,128)(2,1)}, u32[]{:S(2)}) copy-start(bf16[512,512]{1,0:T(8,128)(2,1)} %refs_5_.3) | copy-start | bytes 1572868
  2.5 9.7 %collective-permute-start.4 = (bf16[256,512]{1,0:T(8,128)(2,1)S(1)}, bf16[256,512]{1,0:T(8,128)(2,1)S(1)}, u32[]{:S(2)}, u32[]{:S(2)}) collective-permute-start(bf16[256,512]{1,0:T(8,128)(2,1)S(1)} %get-tuple-element.60.refs_0_.refs_2_), channel_id=1, source_target_pairs={{0,4},{1,5},{2,6},{3,7},{4,0},{5,1},{6,2},{7,3},{8,12},{9,13},{10,... | collective-permute-start | bytes 786440 | tf_op jit(solution)/shard_map/ppermute | solution.py:24
  5.1 9.5 %collective-permute-start.6 = (bf16[256,512]{1,0:T(8,128)(2,1)S(1)}, bf16[256,512]{1,0:T(8,128)(2,1)S(1)}, u32[]{:S(2)}, u32[]{:S(2)}) collective-permute-start(bf16[256,512]{1,0:T(8,128)(2,1)S(1)} %get-tuple-element.61.refs_1_.refs_3_), channel_id=1, source_target_pairs={{0,2},{1,3},{2,0},{3,1},{4,6},{5,7},{6,4},{7,5},{8,10},{9,11},{10,... | collective-permute-start | bytes 786440 | tf_op jit(solution)/shard_map/ppermute | solution.py:24
  6.6 13.2 %collective-permute-start = (bf16[256,512]{1,0:T(8,128)(2,1)S(1)}, bf16[256,512]{1,0:T(8,128)(2,1)S(1)}, u32[]{:S(2)}, u32[]{:S(2)}) collective-permute-start(bf16[256,512]{1,0:T(8,128)(2,1)S(1)} %get-tuple-element.60.refs_0_.refs_2_), channel_id=1, source_target_pairs={{0,2},{1,3},{2,0},{3,1},{4,6},{5,7},{6,4},{7,5},{8,10},{9,11},{10,... | collective-permute-start | bytes 786440 | tf_op jit(solution)/shard_map/ppermute | solution.py:24
  7.1 12.7 %collective-permute-start.1 = (bf16[256,512]{1,0:T(8,128)(2,1)S(1)}, bf16[256,512]{1,0:T(8,128)(2,1)S(1)}, u32[]{:S(2)}, u32[]{:S(2)}) collective-permute-start(bf16[256,512]{1,0:T(8,128)(2,1)S(1)} %get-tuple-element.61.refs_1_.refs_3_), channel_id=1, source_target_pairs={{0,4},{1,5},{2,6},{3,7},{4,0},{5,1},{6,2},{7,3},{8,12},{9,13},{10,... | collective-permute-start | bytes 786440 | tf_op jit(solution)/shard_map/ppermute | solution.py:24
  12.5 12.5 %collective-permute-start.5 = (bf16[256,512]{1,0:T(8,128)(2,1)S(1)}, bf16[256,512]{1,0:T(8,128)(2,1)S(1)}, u32[]{:S(2)}, u32[]{:S(2)}) collective-permute-start(bf16[256,512]{1,0:T(8,128)(2,1)S(1)} %target.2), channel_id=1, source_target_pairs={{0,2},{1,3},{2,0},{3,1},{4,6},{5,7},{6,4},{7,5},{8,10},{9,11},{10,... | collective-permute-start | bytes 786440 | tf_op jit(solution)/shard_map/ppermute | solution.py:24
  14.9 10.1 %collective-permute-start.7 = (bf16[256,512]{1,0:T(8,128)(2,1)S(1)}, bf16[256,512]{1,0:T(8,128)(2,1)S(1)}, u32[]{:S(2)}, u32[]{:S(2)}) collective-permute-start(bf16[256,512]{1,0:T(8,128)(2,1)S(1)} %target.3), channel_id=1, source_target_pairs={{0,4},{1,5},{2,6},{3,7},{4,0},{5,1},{6,2},{7,3},{8,12},{9,13},{10,... | collective-permute-start | bytes 786440 | tf_op jit(solution)/shard_map/ppermute | solution.py:24
  19.8 2.3 %collective-permute-start.3 = (f32[64,640]{1,0:T(8,128)S(1)}, f32[64,640]{1,0:T(8,128)S(1)}, u32[]{:S(2)}, u32[]{:S(2)}) collective-permute-start(f32[64,640]{1,0:T(8,128)S(1)} %get-tuple-element.68.msg_a), channel_id=1, source_target_pairs={{0,1},{1,0},{2,3},{3,2},{4,5},{5,4},{6,7},{7,6},{8,9},{9,8},{10,11... | collective-permute-start | bytes 491528 | tf_op jit(solution)/shard_map/ppermute | solution.py:24
  22.1 4.7 %collective-permute-start.9 = (f32[32,128]{1,0:T(8,128)S(1)}, f32[32,128]{1,0:T(8,128)S(1)}, u32[]{:S(2)}, u32[]{:S(2)}) collective-permute-start(f32[32,128]{1,0:T(8,128)S(1)} %slice_add_fusion), channel_id=1, source_target_pairs={{0,8},{1,9},{2,10},{3,11},{4,12},{5,13},{6,14},{7,15},{8,0},{9,1},... | collective-permute-start | bytes 49160 | tf_op jit(solution)/shard_map/ppermute | solution.py:24
  26.0 1.2 %collective-permute-start.8 = (f32[1,1024]{1,0:T(1,128)S(1)}, f32[1,1024]{1,0:T(1,128)S(1)}, u32[]{:S(2)}, u32[]{:S(2)}) collective-permute-start(f32[1,1024]{1,0:T(1,128)S(1)} %get-tuple-element.73.sums_own), channel_id=1, source_target_pairs={{0,1},{1,0},{2,3},{3,2},{4,5},{5,4},{6,7},{7,6},{8,9},{9,8},{10,11... | collective-permute-start | bytes 12296 | tf_op jit(solution)/shard_map/ppermute | solution.py:24
  28.1 5.8 %collective-permute-start.10 = (bf16[64,640]{1,0:T(8,128)(2,1)S(1)}, bf16[64,640]{1,0:T(8,128)(2,1)S(1)}, u32[]{:S(2)}, u32[]{:S(2)}) collective-permute-start(bf16[64,640]{1,0:T(8,128)(2,1)S(1)} %get-tuple-element.79), channel_id=1, source_target_pairs={{0,6},{1,7},{2,4},{3,5},{4,2},{5,3},{6,0},{7,1},{8,14},{9,15},{10,... | collective-permute-start | bytes 245768 | tf_op jit(solution)/shard_map/ppermute | solution.py:24
  29.5 5.8 %collective-permute-start.11 = (bf16[64,640]{1,0:T(8,128)(2,1)S(1)}, bf16[64,640]{1,0:T(8,128)(2,1)S(1)}, u32[]{:S(2)}, u32[]{:S(2)}) collective-permute-start(bf16[64,640]{1,0:T(8,128)(2,1)S(1)} %get-tuple-element.80), channel_id=1, source_target_pairs={{0,2},{1,3},{2,0},{3,1},{4,6},{5,7},{6,4},{7,5},{8,10},{9,11},{10,... | collective-permute-start | bytes 245768 | tf_op jit(solution)/shard_map/ppermute | solution.py:24
  29.9 5.4 %collective-permute-start.12 = (bf16[64,640]{1,0:T(8,128)(2,1)S(1)}, bf16[64,640]{1,0:T(8,128)(2,1)S(1)}, u32[]{:S(2)}, u32[]{:S(2)}) collective-permute-start(bf16[64,640]{1,0:T(8,128)(2,1)S(1)} %get-tuple-element.81), channel_id=1, source_target_pairs={{0,4},{1,5},{2,6},{3,7},{4,0},{5,1},{6,2},{7,3},{8,12},{9,13},{10,... | collective-permute-start | bytes 245768 | tf_op jit(solution)/shard_map/ppermute | solution.py:24
  35.6 1.4 %collective-permute-start.13 = (bf16[32,512]{1,0:T(8,128)(2,1)S(1)}, bf16[32,512]{1,0:T(8,128)(2,1)S(1)}, u32[]{:S(2)}, u32[]{:S(2)}) collective-permute-start(bf16[32,512]{1,0:T(8,128)(2,1)S(1)} %get-tuple-element.85.u_a), channel_id=1, source_target_pairs={{0,1},{1,0},{2,3},{3,2},{4,5},{5,4},{6,7},{7,6},{8,9},{9,8},{10,11... | collective-permute-start | bytes 98312 | tf_op jit(solution)/shard_map/ppermute | solution.py:24
  37.8 5.6 %collective-permute-start.14 = (bf16[64,512]{1,0:T(8,128)(2,1)S(1)}, bf16[64,512]{1,0:T(8,128)(2,1)S(1)}, u32[]{:S(2)}, u32[]{:S(2)}) collective-permute-start(bf16[64,512]{1,0:T(8,128)(2,1)S(1)} %get-tuple-element.95), channel_id=1, source_target_pairs={{0,6},{1,7},{2,4},{3,5},{4,2},{5,3},{6,0},{7,1},{8,14},{9,15},{10,... | collective-permute-start | bytes 196616 | tf_op jit(solution)/shard_map/ppermute | solution.py:24
  39.5 5.1 %collective-permute-start.15 = (bf16[64,512]{1,0:T(8,128)(2,1)S(1)}, bf16[64,512]{1,0:T(8,128)(2,1)S(1)}, u32[]{:S(2)}, u32[]{:S(2)}) collective-permute-start(bf16[64,512]{1,0:T(8,128)(2,1)S(1)} %get-tuple-element.98), channel_id=1, source_target_pairs={{0,2},{1,3},{2,0},{3,1},{4,6},{5,7},{6,4},{7,5},{8,10},{9,11},{10,... | collective-permute-start | bytes 196616 | tf_op jit(solution)/shard_map/ppermute | solution.py:24
  40.0 4.6 %collective-permute-start.16 = (bf16[64,512]{1,0:T(8,128)(2,1)S(1)}, bf16[64,512]{1,0:T(8,128)(2,1)S(1)}, u32[]{:S(2)}, u32[]{:S(2)}) collective-permute-start(bf16[64,512]{1,0:T(8,128)(2,1)S(1)} %get-tuple-element.99), channel_id=1, source_target_pairs={{0,4},{1,5},{2,6},{3,7},{4,0},{5,1},{6,2},{7,3},{8,12},{9,13},{10,... | collective-permute-start | bytes 196616 | tf_op jit(solution)/shard_map/ppermute | solution.py:24
  43.4 1.3 %collective-permute-start.17 = (f32[32,512]{1,0:T(8,128)S(1)}, f32[32,512]{1,0:T(8,128)S(1)}, u32[]{:S(2)}, u32[]{:S(2)}) collective-permute-start(f32[32,512]{1,0:T(8,128)S(1)} %get-tuple-element.103), channel_id=1, source_target_pairs={{0,1},{1,0},{2,3},{3,2},{4,5},{5,4},{6,7},{7,6},{8,9},{9,8},{10,11... | collective-permute-start | bytes 196616 | tf_op jit(solution)/shard_map/ppermute | solution.py:24
  44.9 1.2 %collective-permute-start.18 = (bf16[32,640]{1,0:T(8,128)(2,1)S(1)}, bf16[32,640]{1,0:T(8,128)(2,1)S(1)}, u32[]{:S(2)}, u32[]{:S(2)}) collective-permute-start(bf16[32,640]{1,0:T(8,128)(2,1)S(1)} %get-tuple-element.104.u_a), channel_id=1, source_target_pairs={{0,1},{1,0},{2,3},{3,2},{4,5},{5,4},{6,7},{7,6},{8,9},{9,8},{10,11... | collective-permute-start | bytes 122888 | tf_op jit(solution)/shard_map/ppermute | solution.py:24
  46.2 4.6 %collective-permute-start.19 = (f32[32,128]{1,0:T(8,128)S(1)}, f32[32,128]{1,0:T(8,128)S(1)}, u32[]{:S(2)}, u32[]{:S(2)}) collective-permute-start(f32[32,128]{1,0:T(8,128)S(1)} %totals.1.here), channel_id=1, source_target_pairs={{0,8},{1,9},{2,10},{3,11},{4,12},{5,13},{6,14},{7,15},{8,0},{9,1},... | collective-permute-start | bytes 49160 | tf_op jit(solution)/shard_map/ppermute | solution.py:24
  51.0 5.1 %collective-permute-start.20 = (bf16[32,640]{1,0:T(8,128)(2,1)S(1)}, bf16[32,640]{1,0:T(8,128)(2,1)S(1)}, u32[]{:S(2)}, u32[]{:S(2)}) collective-permute-start(bf16[32,640]{1,0:T(8,128)(2,1)S(1)} %get-tuple-element.110), channel_id=1, source_target_pairs={{0,6},{1,7},{2,4},{3,5},{4,2},{5,3},{6,0},{7,1},{8,14},{9,15},{10,... | collective-permute-start | bytes 122888 | tf_op jit(solution)/shard_map/ppermute | solution.py:24
  52.6 4.0 %collective-permute-start.21 = (bf16[32,640]{1,0:T(8,128)(2,1)S(1)}, bf16[32,640]{1,0:T(8,128)(2,1)S(1)}, u32[]{:S(2)}, u32[]{:S(2)}) collective-permute-start(bf16[32,640]{1,0:T(8,128)(2,1)S(1)} %get-tuple-element.111), channel_id=1, source_target_pairs={{0,2},{1,3},{2,0},{3,1},{4,6},{5,7},{6,4},{7,5},{8,10},{9,11},{10,... | collective-permute-start | bytes 122888 | tf_op jit(solution)/shard_map/ppermute | solution.py:24
  53.4 4.0 %collective-permute-start.22 = (bf16[32,640]{1,0:T(8,128)(2,1)S(1)}, bf16[32,640]{1,0:T(8,128)(2,1)S(1)}, u32[]{:S(2)}, u32[]{:S(2)}) collective-permute-start(bf16[32,640]{1,0:T(8,128)(2,1)S(1)} %get-tuple-element.112), channel_id=1, source_target_pairs={{0,4},{1,5},{2,6},{3,7},{4,0},{5,1},{6,2},{7,3},{8,12},{9,13},{10,... | collective-permute-start | bytes 122888 | tf_op jit(solution)/shard_map/ppermute | solution.py:24
  (6 other events, 52.4 us)
